TPU v7x, 32 devices: a whole 2x2x4 slice. The times are simulated.
32 devices in a mesh: expert: 4 (over y, x), tensor: 2 (over core), dp: 4 (over z).
Axes of the slice: x: 2, y: 2, z: 4, core: 2. Of those that a mesh axis runs over, the one named last changes fastest.
Arguments:
- tokens: bfloat16 [2048, 3072], P(('expert', 'dp'), 'tensor'), may hold values from -6 to 6
- experts_chosen: int32 [2048, 2], P(('expert', 'dp')), may hold values from 0 to 3, all different within a row; in each aligned block of 128 rows (0 to 127, 128 to 255, ...) at most 73 rows name the same one
- route_weights: float32 [2048, 2], P(('expert', 'dp')), may hold values from 0.1 to 1
- cotangent: bfloat16 [2048, 3072], P(('expert', 'dp'), 'tensor'), may hold values from -6 to 6
- gate_weight: bfloat16 [4, 3072, 8192], P('expert', 'dp', 'tensor'), may hold values from -0.15625 to 0.15625
- up_weight: bfloat16 [4, 3072, 8192], P('expert', 'dp', 'tensor'), may hold values from -0.15625 to 0.15625
- down_weight: bfloat16 [4, 8192, 3072], P('expert', 'tensor', 'dp'), may hold values from -0.09375 to 0.09375
Outputs:
- layer_output: bfloat16 [2048, 3072], P(('expert', 'dp'), 'tensor')
- token_grad: bfloat16 [2048, 3072], P(('expert', 'dp'), 'tensor')
- route_grad: float32 [2048, 2], P(('expert', 'dp'))
Inputs may be any that keep to these rules, and one draw needn't show every extreme that they name: `experts_chosen`: each row names 2 different experts. Among the 128 rows of one index of expert+dp no expert is named more than 73 times, and in some such block one expert is named exactly 73 times.
All inputs are finite; a program needn't handle non-finite values.
Results may differ from a plain program's by a relative error of at most 0.0072.
Values may be sent and summed in bfloat16 or wider, within the bound.
No kernel may reach another device: no remote copies, remote signals or barrier semaphores. Data moves between devices by JAX's collectives and lax.ppermute only.
A program may use at most 256 MiB of HBM per device.

v0:
```python
import jax
import jax.numpy as jnp
from jax import lax
from jax.sharding import PartitionSpec as P


def slot_table(experts_chosen, num_experts, cap_rows):
    flat_ids = experts_chosen.reshape(-1)
    expert_hot = (flat_ids[:, None] == jnp.arange(num_experts, dtype=jnp.int32)[None, :]).astype(
        jnp.int32
    )
    earlier = jnp.cumsum(expert_hot, axis=0) - expert_hot
    rank_slot = jnp.sum(earlier * expert_hot, axis=1)
    target = flat_ids * cap_rows + rank_slot
    all_slots = jnp.arange(num_experts * cap_rows, dtype=jnp.int32)
    return (target[:, None] == all_slots[None, :]).astype(jnp.bfloat16)


def to_slots(slot_onehot, pair_rows, num_experts, cap_rows):
    packed = jnp.einsum("ps,pd->sd", slot_onehot, pair_rows, preferred_element_type=jnp.float32)
    return packed.astype(jnp.bfloat16).reshape(num_experts, cap_rows, pair_rows.shape[1])


def from_slots(slot_onehot, returned):
    flat_back = returned.reshape(-1, returned.shape[2])
    return jnp.dot(slot_onehot, flat_back, preferred_element_type=jnp.float32)


def as_blocks(summed, num_experts, cap_rows):
    return summed.astype(jnp.bfloat16).reshape(num_experts, cap_rows, summed.shape[1])


def local(tokens, experts_chosen, route_weights, cotangent, gate_weight, up_weight, down_weight):
    tok_rows, feat_cols = tokens.shape
    top_count = experts_chosen.shape[1]
    num_experts = lax.axis_size("expert")
    cap_rows = min(tok_rows, 9 * tok_rows * top_count // (8 * num_experts) + 1)
    slot_onehot = slot_table(experts_chosen, num_experts, cap_rows)
    pair_weights = route_weights.reshape(-1, 1)
    token_pairs = jnp.repeat(tokens, top_count, axis=0)
    grad_pairs = (
        jnp.repeat(cotangent, top_count, axis=0).astype(jnp.float32) * pair_weights
    ).astype(jnp.bfloat16)
    token_send = to_slots(slot_onehot, token_pairs, num_experts, cap_rows)
    grad_send = to_slots(slot_onehot, grad_pairs, num_experts, cap_rows)
    token_recv = lax.all_to_all(token_send, "expert", split_axis=0, concat_axis=0, tiled=True)
    token_full = lax.all_gather(token_recv, "tensor", axis=2, tiled=True)
    model_cols = token_full.shape[2]
    token_rows = token_full.reshape(-1, model_cols)
    gate_all, up_all = (
        lax.all_gather(gate_weight, "dp", axis=1, tiled=True),
        lax.all_gather(up_weight, "dp", axis=1, tiled=True),
    )
    gate_pre = jnp.dot(token_rows, gate_all[0], preferred_element_type=jnp.float32)
    up_pre = jnp.dot(token_rows, up_all[0], preferred_element_type=jnp.float32)
    hidden = (jax.nn.silu(gate_pre) * up_pre).astype(jnp.bfloat16)
    down_all = lax.all_gather(down_weight, "dp", axis=2, tiled=True)
    out_part = jnp.dot(hidden, down_all[0], preferred_element_type=jnp.float32)
    out_sum = lax.psum_scatter(
        out_part.astype(jnp.bfloat16), "tensor", scatter_dimension=1, tiled=True
    ).astype(jnp.float32)
    out_back = lax.all_to_all(
        as_blocks(out_sum, num_experts, cap_rows), "expert", split_axis=0, concat_axis=0, tiled=True
    )
    grad_recv = lax.all_to_all(grad_send, "expert", split_axis=0, concat_axis=0, tiled=True)
    grad_full = lax.all_gather(grad_recv, "tensor", axis=2, tiled=True)
    grad_rows_all = grad_full.reshape(-1, model_cols)
    contract = (((1,), (1,)), ((), ()))
    hidden_grad = lax.dot_general(
        grad_rows_all, down_all[0], contract, preferred_element_type=jnp.float32
    )
    sigmoid_gate = jax.nn.sigmoid(gate_pre)
    up_grad = (hidden_grad * jax.nn.silu(gate_pre)).astype(jnp.bfloat16)
    gate_grad = (
        hidden_grad * up_pre * sigmoid_gate * (1.0 + gate_pre * (1.0 - sigmoid_gate))
    ).astype(jnp.bfloat16)
    in_part = lax.dot_general(gate_grad, gate_all[0], contract, preferred_element_type=jnp.float32)
    in_part = in_part + lax.dot_general(
        up_grad, up_all[0], contract, preferred_element_type=jnp.float32
    )
    in_sum = lax.psum_scatter(
        in_part.astype(jnp.bfloat16), "tensor", scatter_dimension=1, tiled=True
    ).astype(jnp.float32)
    in_back = lax.all_to_all(
        as_blocks(in_sum, num_experts, cap_rows), "expert", split_axis=0, concat_axis=0, tiled=True
    )
    out_pairs = from_slots(slot_onehot, out_back).reshape(tok_rows, top_count, feat_cols)
    in_pairs = from_slots(slot_onehot, in_back).reshape(tok_rows, top_count, feat_cols)
    layer_output = jnp.sum(route_weights[:, :, None] * out_pairs, axis=1).astype(jnp.bfloat16)
    token_grad = jnp.sum(in_pairs, axis=1).astype(jnp.bfloat16)
    local_dots = jnp.sum(cotangent.astype(jnp.float32)[:, None, :] * out_pairs, axis=2)
    route_grad = lax.psum(local_dots, "tensor")
    return (layer_output, token_grad, route_grad)


def solution(mesh):
    in_specs = (
        P(("expert", "dp"), "tensor"),
        P(("expert", "dp"), None),
        P(("expert", "dp"), None),
        P(("expert", "dp"), "tensor"),
        P("expert", "dp", "tensor"),
        P("expert", "dp", "tensor"),
        P("expert", "tensor", "dp"),
    )
    out_specs = (
        P(("expert", "dp"), "tensor"),
        P(("expert", "dp"), "tensor"),
        P(("expert", "dp"), None),
    )
    return jax.shard_map(local, mesh=mesh, in_specs=in_specs, out_specs=out_specs, check_vma=False)
```

profile of v0, /device:TPU:0, one launch (start us, length us, event | category | flops | bytes accessed | tf_op | source)
XLA Modules:
  0.0 1455.3 jit_solution(10602917999644850191)
XLA Ops:
  7.2 0.8 copy.21
  8.3 1.4 broadcast_in_dim.4
  10.1 1.2 reduce-window.6
  12.5 18.7 %all_to_all.20 = bf16[4,73,1536]{2,1,0:T(8,128)(2,1)} all-to-all(bf16[4,73,1536]{2,1,0:T(8,128)(2,1)S(1)} %reshape.107), channel_id=1, replica_groups=mesh['expert'=4,'tensor'=2,'dp'=4] {'expert'}, dimensions={0} | all-to-all | bytes 1794048 | tf_op jit(solution)/shard_map/all_to_all | solution.py:46
  31.7 1.1 convert_element_type.57
  33.0 0.5 convolution_convert_fusion
  33.8 15.7 %all_to_all.21 = bf16[4,73,1536]{2,1,0:T(8,128)(2,1)} all-to-all(bf16[4,73,1536]{2,1,0:T(8,128)(2,1)S(1)} %reshape.111), channel_id=1, replica_groups=mesh['expert'=4,'tensor'=2,'dp'=4] {'expert'}, dimensions={0} | all-to-all | bytes 1794048 | tf_op jit(solution)/shard_map/all_to_all | solution.py:65
  49.6 0.7 all-gather.10.cloned.1.call-update
  50.9 0.5 all-gather.12.cloned.1.call-update
  51.7 2.0 reshape.108
  53.7 5.9 all-gather.14.cloned.1.call-done
  59.6 3.3 reshape.112
  62.9 424.7 %all-gather.10.cloned.1.call-done = bf16[1,3072,4096]{2,1,0:T(8,128)(2,1)} async-done(((bf16[1,768,4096]{2,1,0:T(8,128)(2,1)}), bf16[1,3072,4096]{2,1,0:T(8,128)(2,1)}) %all-gather.10.cloned.1.call-update) | async-done | bytes 25165840 | tf_op jit(solution)/shard_map/all_gather | solution.py:52
  487.6 16.4 %fusion.6 = f32[292,4096]{1,0:T(8,128)} fusion(bf16[292,3072]{1,0:T(8,128)(2,1)S(1)} %reshape.108, bf16[1,3072,4096]{2,1,0:T(8,128)(2,1)} %all-gather.10.cloned.1.call-done), kind=kOutput, calls=%fused_computation.6 | convolution fusion | flops 7348420608 | bytes 31744000 | tf_op jit(solution)/shard_map/dot_general | solution.py:55
  504.0 408.4 %all-gather.8.cloned.1.call-done = bf16[1,3072,4096]{2,1,0:T(8,128)(2,1)} async-done(((bf16[1,768,4096]{2,1,0:T(8,128)(2,1)}), bf16[1,3072,4096]{2,1,0:T(8,128)(2,1)}) %all-gather.8.cloned.1.call-update) | async-done | bytes 25165840 | tf_op jit(solution)/shard_map/all_gather | solution.py:51
  912.4 16.3 %fusion.10 = f32[292,4096]{1,0:T(8,128)} fusion(bf16[292,3072]{1,0:T(8,128)(2,1)S(1)} %reshape.108, bf16[1,3072,4096]{2,1,0:T(8,128)(2,1)} %all-gather.8.cloned.1.call-done), kind=kOutput, calls=%fused_computation.10 | convolution fusion | flops 7348420608 | bytes 31744000 | tf_op jit(solution)/shard_map/dot_general | solution.py:54
  928.8 408.5 %all-gather.12.cloned.1.call-done = bf16[1,4096,3072]{2,1,0:T(8,128)(2,1)} async-done(((bf16[1,4096,768]{2,1,0:T(8,128)(2,1)}), bf16[1,4096,3072]{2,1,0:T(8,128)(2,1)}) %all-gather.12.cloned.1.call-update) | async-done | bytes 25165840 | tf_op jit(solution)/shard_map/all_gather | solution.py:57
  1337.3 14.5 fusion
  1351.7 16.7 %fusion.4 = f32[292,3072]{1,0:T(8,128)} fusion(bf16[1,3072,4096]{2,1,0:T(8,128)(2,1)} %all-gather.10.cloned.1.call-done, f32[292,4096]{1,0:T(8,128)} %fusion, f32[292,4096]{1,0:T(8,128)} %fusion.10), kind=kOutput, calls=%fused_computation.4 | convolution fusion | flops 7355596800 | bytes 38322176 | tf_op jit(solution)/shard_map/dot_general | solution.py:78
  1368.5 21.3 %fusion.16 = bf16[292,3072]{1,0:T(8,128)(2,1)} fusion(f32[292,3072]{1,0:T(8,128)} %fusion.4, bf16[1,3072,4096]{2,1,0:T(8,128)(2,1)} %all-gather.8.cloned.1.call-done, f32[292,4096]{1,0:T(8,128)} %fusion.10, f32[292,4096]{1,0:T(8,128)} %fusion, f32[292,4096]{1,0:T(8,128)} %fusion.6), kind=kOutput, calls=%fused_computation.18 | convolution fusion | flops 7362174976 | bytes 44900352 | tf_op jit(solution)/shard_map/dot_general | solution.py:77
  1389.9 17.2 %fusion.19 = bf16[292,3072]{1,0:T(8,128)(2,1)} fusion(bf16[1,4096,3072]{2,1,0:T(8,128)(2,1)} %all-gather.12.cloned.1.call-done, f32[292,4096]{1,0:T(8,128)} %fusion.6, f32[292,4096]{1,0:T(8,128)} %fusion.10), kind=kOutput, calls=%fused_computation.19 | convolution fusion | flops 7356493824 | bytes 36528128 | tf_op jit(solution)/shard_map/dot_general | solution.py:58
  1407.1 2.4 reshape.113
  1409.5 3.6 all-to-all-start.3
  1413.2 1.5 reduce-scatter.3.cloned.1.call-done
  1414.7 2.4 reshape.109
  1417.1 9.3 all-to-all-done.3
  1426.5 3.5 all-to-all-start.1
  1430.0 1.0 convert_element_type.56
  1431.5 1.4 convolution_reduce_fusion
  1432.8 9.6 all-to-all-done.1
  1442.7 2.7 multiply_reduce_fusion
  1445.4 3.0 psum.7
  (43 shorter events, 4.5 us)
Async XLA Ops:
  7.2 24.1 %copy-start = (bf16[128,1536]{1,0:T(8,128)(2,1)S(1)}, bf16[128,1536]{1,0:T(8,128)(2,1)}, u32[]{:S(2)}) copy-start(bf16[128,1536]{1,0:T(8,128)(2,1)} %param.10) | copy-start | bytes 1179652
  7.2 44.5 %all-gather.6.cloned.1.call-start = ((), (), s32[]{:S(2)}) async-start(), calls=%async_computation.6 | async-start | bytes 2949120 | tf_op jit(solution)/shard_map/all_gather | solution.py:47
  12.2 20.5 %copy-start.2 = (f32[128,2]{0,1:T(2,128)S(1)}, f32[128,2]{0,1:T(2,128)}, u32[]{:S(2)}) copy-start(f32[128,2]{0,1:T(2,128)} %param.9) | copy-start | bytes 3076
  31.2 28.4 %all-gather.14.cloned.1.call-start = ((), (), s32[]{:S(2)}) async-start(), calls=%async_computation.11 | async-start | bytes 2949120 | tf_op jit(solution)/shard_map/all_gather | solution.py:66
  49.5 438.1 %all-gather.10.cloned.1.call-start = ((), (), s32[]{:S(2)}) async-start(), calls=%async_computation.8 | async-start | bytes 31457280 | tf_op jit(solution)/shard_map/all_gather | solution.py:52
  50.3 862.2 %all-gather.8.cloned.1.call-start = ((), (), s32[]{:S(2)}) async-start(), calls=%async_computation.7 | async-start | bytes 31457280 | tf_op jit(solution)/shard_map/all_gather | solution.py:51
  50.9 1286.4 %all-gather.12.cloned.1.call-start = ((), (), s32[]{:S(2)}) async-start(), calls=%async_computation.9 | async-start | bytes 31457280 | tf_op jit(solution)/shard_map/all_gather | solution.py:57
  51.5 1355.7 %reduce-scatter.5.cloned.1.call-start = ((), (), s32[]{:S(2)}) async-start(), calls=%async_computation.12 | async-start | bytes 2727936 | tf_op jit(solution)/shard_map/reduce_scatter | solution.py:81
  1389.8 24.9 %reduce-scatter.3.cloned.1.call-start = ((), (), s32[]{:S(2)}) async-start(), calls=%async_computation.10 | async-start | bytes 2727936 | tf_op jit(solution)/shard_map/reduce_scatter | solution.py:59
  1407.1 24.1 %copy-start.1 = (s32[128,2]{0,1:T(2,128)S(1)}, s32[128,2]{0,1:T(2,128)}, u32[]{:S(2)}) copy-start(s32[128,2]{0,1:T(2,128)} %param.8) | copy-start | bytes 3076
  1409.5 16.9 %all-to-all-start.3 = ((bf16[4,73,1536]{2,1,0:T(8,128)(2,1)}), bf16[4,73,1536]{2,1,0:T(8,128)(2,1)S(1)}, u32[]{:S(2)}, u32[]{:S(2)}) async-start(bf16[4,73,1536]{2,1,0:T(8,128)(2,1)} %reshape.113), calls=%async_computation.5 | async-start | bytes 1966080 | tf_op jit(solution)/shard_map/all_to_all | solution.py:84
  1426.5 16.0 %all-to-all-start.1 = ((bf16[4,73,1536]{2,1,0:T(8,128)(2,1)}), bf16[4,73,1536]{2,1,0:T(8,128)(2,1)S(1)}, u32[]{:S(2)}, u32[]{:S(2)}) async-start(bf16[4,73,1536]{2,1,0:T(8,128)(2,1)} %reshape.109), calls=%async_computation.2 | async-start | bytes 1966080 | tf_op jit(solution)/shard_map/all_to_all | solution.py:62
Sparse Core Ops, SparseCore 0:
  31.3 9.9 all-gather.5
  49.7 9.9 all-gather.13
  61.2 426.3 all-gather.9
  489.0 423.3 all-gather.7
  913.9 423.3 all-gather.11
  1389.9 7.5 reduce-scatter.4
  1407.2 7.4 reduce-scatter.2
where the time goes:
time: 1460 us
  waiting for transfers between devices  1270 us (87%)
  matrix products  108 us (7%)
  blocking collectives  37.4 us (3%)
  local copies, waits for them, and re-layouts  16.2 us (1%)
    all_gather x1, waiting for transfers between devices, local(): lax.all_gather(up_weight, 'dp', axis=1, tiled=True)  425 us
    all_gather x1, waiting for transfers between devices, local(): down_all = lax.all_gather(down_weight, 'dp', axis=2, tiled=True)  408 us
    all_gather x1, waiting for transfers between devices, local(): lax.all_gather(gate_weight, 'dp', axis=1, tiled=True)  408 us
  transfers between devices with their start and end apart: 9, of which 7 were waited for; matrix products, arithmetic and copies ran while one was open for 4% of the time, Pallas kernels for 0%

commit v1 on v0

v1 whole, which is shorter than its diff:
```python
import jax
import jax.numpy as jnp
from jax import lax
from jax.sharding import PartitionSpec as P

F32 = jnp.float32
BF16 = jnp.bfloat16


def swap(value, axis, shift):
    size = lax.axis_size(axis)
    return lax.ppermute(value, axis, [(i, i ^ shift) for i in range(size)])


def resplit(shard, split_dim, size, me):
    part = shard.shape[split_dim] // size

    def chunk(index):
        return lax.dynamic_slice_in_dim(shard, index * part, part, split_dim)

    return [chunk(me)] + [swap(chunk(me ^ s), "dp", s) for s in range(1, size)]


def assemble(pieces, join_dim, me):
    own = pieces[0].shape[join_dim]
    shape = list(pieces[0].shape)
    shape[join_dim] = own * len(pieces)
    whole = jnp.zeros(shape, pieces[0].dtype)
    for s, piece in enumerate(pieces):
        whole = lax.dynamic_update_slice_in_dim(whole, piece, (me ^ s) * own, join_dim)
    return whole


def local(tokens, experts_chosen, route_weights, cotangent, gate_weight, up_weight, down_weight):
    E, T, Z = lax.axis_size("expert"), lax.axis_size("tensor"), lax.axis_size("dp")
    me_e, me_t, me_d = lax.axis_index("expert"), lax.axis_index("tensor"), lax.axis_index("dp")
    B, Fh = tokens.shape
    K = experts_chosen.shape[1]
    cap = min(B, 9 * B * K // (8 * E) + 1)
    capr = -(-Z * cap // 8) * 8
    G = Z * B
    R = E * capr

    gate_p = resplit(gate_weight[0], 1, Z, me_d)
    up_p = resplit(up_weight[0], 1, Z, me_d)
    down_in = lax.optimization_barrier((down_weight[0], gate_p[1:]))[0]
    down_p = resplit(down_in, 0, Z, me_d)

    tok_g = lax.all_gather(tokens, "dp", axis=0, tiled=True)
    cot_g = lax.all_gather(cotangent, "dp", axis=0, tiled=True)
    ids = lax.all_gather(experts_chosen, "dp", axis=0, tiled=True)
    wts = lax.all_gather(route_weights, "dp", axis=0, tiled=True)
    rel = me_e ^ jnp.arange(E, dtype=jnp.int32)
    named = ids[:, :, None] == rel[None, None, :]
    hit = jnp.any(named, axis=1)
    wtok = jnp.sum(jnp.where(named, wts[:, :, None], 0.0), axis=1)
    order = jnp.arange(G, dtype=jnp.int32)
    before = (order[None, :] < order[:, None]).astype(BF16)
    pos = jnp.dot(before, hit.astype(BF16), preferred_element_type=F32)
    pos = jnp.where(hit, pos, -1.0)
    place = pos.T[:, None, :] == jnp.arange(capr, dtype=F32)[None, :, None]
    pick = place.astype(BF16).reshape(R, G)
    wslot = jnp.sum(jnp.where(place, wtok.T[:, None, :], 0.0), axis=2).reshape(R, 1)

    x_send = jnp.dot(pick, tok_g, preferred_element_type=F32).astype(BF16).reshape(E, capr, Fh)
    c_send = jnp.dot(pick, cot_g, preferred_element_type=F32)
    g_send = (c_send * wslot).astype(BF16).reshape(E, capr, Fh)
    x_half = jnp.concatenate([x_send[0]] + [swap(x_send[s], "expert", s) for s in range(1, E)], 0)
    g_half = jnp.concatenate([g_send[0]] + [swap(g_send[s], "expert", s) for s in range(1, E)], 0)
    x = lax.all_gather(x_half, "tensor", axis=1, tiled=True)
    g = lax.all_gather(g_half, "tensor", axis=1, tiled=True)

    gate = assemble(gate_p, 0, me_d)
    up = assemble(up_p, 0, me_d)
    gate_pre = jnp.dot(x, gate, preferred_element_type=F32)
    up_pre = jnp.dot(x, up, preferred_element_type=F32)
    sig = jax.nn.sigmoid(gate_pre)
    silu = gate_pre * sig
    hidden = (silu * up_pre).astype(BF16)

    down = assemble(down_p, 1, me_d)
    contract = (((1,), (1,)), ((), ()))

    def send_back(part):
        mine = lax.psum_scatter(part.astype(BF16), "tensor", scatter_dimension=1, tiled=True)
        mine = mine.reshape(E, capr, Fh)
        return jnp.concatenate([mine[0]] + [swap(mine[s], "expert", s) for s in range(1, E)], 0)

    out_back = send_back(jnp.dot(hidden, down, preferred_element_type=F32))
    heavy = jnp.where(place, wtok.T[:, None, :], 0.0).reshape(R, G)
    heavy_hi = heavy.astype(BF16)
    heavy_lo = (heavy - heavy_hi.astype(F32)).astype(BF16)
    over_rows = (((0,), (0,)), ((), ()))

    def combine(weights, rows):
        return lax.dot_general(weights, rows, over_rows, preferred_element_type=F32)

    out_tok = combine(heavy_hi, out_back) + combine(heavy_lo, out_back)
    layer_output = lax.psum_scatter(out_tok.astype(BF16), "dp", scatter_dimension=0, tiled=True)

    hidden_grad = lax.dot_general(g, down, contract, preferred_element_type=F32)
    up_grad = (hidden_grad * silu).astype(BF16)
    gate_grad = (hidden_grad * up_pre * sig * (1.0 + gate_pre * (1.0 - sig))).astype(BF16)
    in_part = lax.dot_general(gate_grad, gate, contract, preferred_element_type=F32)
    in_part = in_part + lax.dot_general(up_grad, up, contract, preferred_element_type=F32)
    in_back = send_back(in_part)
    token_grad = lax.psum_scatter(
        combine(pick, in_back).astype(BF16), "dp", scatter_dimension=0, tiled=True
    )

    dots = jnp.sum(hidden.astype(F32) * hidden_grad, axis=1).reshape(E, capr)
    dots = jnp.stack([dots[0]] + [swap(dots[s], "expert", s) for s in range(1, E)], 0)
    by_tok = jnp.sum(jnp.where(place, dots[:, :, None], 0.0), axis=1).T
    by_tok = by_tok / jnp.where(hit, wtok, 1.0)
    pair = jnp.sum(jnp.where(named, by_tok[:, None, :], 0.0), axis=2)
    pair = lax.psum(pair, ("tensor", "dp"))
    route_grad = lax.dynamic_slice_in_dim(pair, me_d * B, B, 0)
    return layer_output, token_grad, route_grad


def solution(mesh):
    rows = P(("expert", "dp"), "tensor")
    pairs = P(("expert", "dp"), None)
    wide = P("expert", "dp", "tensor")
    in_specs = (rows, pairs, pairs, rows, wide, wide, P("expert", "tensor", "dp"))
    return jax.shard_map(
        local, mesh=mesh, in_specs=in_specs, out_specs=(rows, rows, pairs), check_vma=False
    )
```

time: 1460 us -> 771 us (0.53)
  waiting for transfers between devices: 1270 us -> 374 us
  starting transfers between devices: 7.58 us -> 126 us
  local copies, waits for them, and re-layouts: 16.2 us -> 58.7 us
  blocking collectives: 37.4 us -> 67.5 us
    all_gather x5 -> x4, waiting for transfers between devices: 1250 us -> 27 us  [the longest x1 27 us: local(): tok_g = lax.all_gather(tokens, 'dp', axis=0, tiled=True)]
    ppermute x0 -> x24, waiting for transfers between devices: none -> 334 us  [swap(): return lax.ppermute(value, axis, [(i, i ^ shift) for i in range(size)])]
    ppermute x0 -> x24, starting transfers between devices: none -> 126 us  [swap(): return lax.ppermute(value, axis, [(i, i ^ shift) for i in range(size)])]
    psum x1, blocking collectives: 3 us -> 45.5 us  [local(): pair = lax.psum(pair, ('tensor', 'dp'))]
    all_to_all x2 -> x0, blocking collectives: 34.4 us -> none  [the longest x1 18.7 us: local(): lax.all_to_all(token_send, 'expert', split_axis=0, concat_axis=0, tiled=T...]
    dynamic_update_slice x0 -> x11, local copies, waits for them, and re-layouts: none -> 28.4 us  [assemble(): lax.dynamic_update_slice_in_dim(whole, piece, (me ^ s) * own, join_dim)]
    all_gather x0 -> x2, blocking collectives: none -> 22 us  [the longest x1 12.8 us: local(): ids = lax.all_gather(experts_chosen, 'dp', axis=0, tiled=True)]
    all_to_all x2 -> x0, waiting for transfers between devices: 19 us -> none  [the longest x1 9.63 us: local(): lax.all_to_all(as_blocks(out_sum, num_experts, cap_rows), 'expert', split...]
  transfers between devices with their start and end apart: 9 -> 32, of which waited for: 7 -> 20; matrix products, arithmetic and copies ran while one was open for 4% -> 20% of each run, Pallas kernels for 0% -> 0%
where the time goes in v1:
time: 771 us; the launch traced here: 767 us
  waiting for transfers between devices  374 us (49%)
  starting transfers between devices  126 us (16%)
  matrix products  119 us (15%)
  blocking collectives  67.5 us (9%)
  local copies, waits for them, and re-layouts  58.7 us (8%)
  between operations  14.6 us (2%)
    ppermute x24, waiting for transfers between devices, swap(): return lax.ppermute(value, axis, [(i, i ^ shift) for i in range(size)])  334 us
    ppermute x24, starting transfers between devices, swap(): return lax.ppermute(value, axis, [(i, i ^ shift) for i in range(size)])  126 us
    psum x1, blocking collectives, local(): pair = lax.psum(pair, ('tensor', 'dp'))  45.5 us
    dynamic_update_slice x11, local copies, waits for them, and re-layouts, assemble(): lax.dynamic_update_slice_in_dim(whole, piece, (me ^ s) * own, join_dim)  28.4 us
    all_gather x1, waiting for transfers between devices, local(): tok_g = lax.all_gather(tokens, 'dp', axis=0, tiled=True)  27 us
    dot_general x1, matrix products, local(): lax.dot_general(up_grad, up, contract, preferred_element_type=F32)  25.1 us
    dot_general x1, matrix products, local(): lax.dot_general(gate_grad, gate, contract, preferred_element_type=F32)  23 us
    dot_general x1, matrix products, local(): hidden_grad = lax.dot_general(g, down, contract, preferred_element_type=F32)  16.5 us
  transfers between devices with their start and end apart: 32, of which 20 were waited for; matrix products, arithmetic and copies ran while one was open for 20% of the time, Pallas kernels for 0%

profile of v1, /device:TPU:0, one launch (start us, length us, event | category | flops | bytes accessed | tf_op | source)
XLA Modules:
  0.0 767.4 jit_solution(11509160820756698752)
XLA Ops:
  8.7 12.8 %all_gather.18 = s32[512,2]{0,1:T(2,128)S(1)} all-gather(s32[128,2]{0,1:T(2,128)} %param.8), channel_id=1, replica_groups=mesh['expert'=4,'tensor'=2,'dp'=4] {'dp'}, dimensions={0}, use_global_device_ids=true | all-gather | bytes 5120 | tf_op jit(solution)/shard_map/all_gather | solution.py:51
  22.4 27.0 %all-gather.5.cloned.1.call-done = bf16[512,1536]{1,0:T(8,128)(2,1)} async-done(((bf16[128,1536]{1,0:T(8,128)(2,1)}), bf16[512,1536]{1,0:T(8,128)(2,1)}) %all-gather.5.cloned.1.call-update) | async-done | bytes 1572880 | tf_op jit(solution)/shard_map/all_gather | solution.py:49
  49.4 3.5 convolution_convert_fusion.1
  56.7 20.5 %collective-permute-done.2 = bf16[296,1536]{1,0:T(8,128)(2,1)S(1)} collective-permute-done((bf16[296,1536]{1,0:T(8,128)(2,1)S(1)}, bf16[296,1536]{1,0:T(8,128)(2,1)S(1)}, u32[]{:S(2)}, u32[]{:S(2)}) %collective-permute-start.2) | collective-permute-done | bytes 909344 | tf_op jit(solution)/shard_map/ppermute | solution.py:12
  77.2 18.2 %collective-permute-done.1 = bf16[296,1536]{1,0:T(8,128)(2,1)S(1)} collective-permute-done((bf16[296,1536]{1,0:T(8,128)(2,1)S(1)}, bf16[296,1536]{1,0:T(8,128)(2,1)S(1)}, u32[]{:S(2)}, u32[]{:S(2)}) %collective-permute-start.1) | collective-permute-done | bytes 909344 | tf_op jit(solution)/shard_map/ppermute | solution.py:12
  97.5 9.1 %all_gather.19 = f32[512,2]{0,1:T(2,128)S(1)} all-gather(f32[128,2]{0,1:T(2,128)S(1)} %copy-done.11), channel_id=1, replica_groups=mesh['expert'=4,'tensor'=2,'dp'=4] {'dp'}, dimensions={0}, use_global_device_ids=true | all-gather | bytes 5120 | tf_op jit(solution)/shard_map/all_gather | solution.py:52
  107.2 3.6 fusion
  115.9 4.8 dynamic-slice_bitcast_fusion.3
  121.9 14.9 %collective-permute-done.17 = bf16[296,1536]{1,0:T(8,128)(2,1)} collective-permute-done((bf16[296,1536]{1,0:T(8,128)(2,1)}, bf16[296,1536]{1,0:T(8,128)(2,1)}, u32[]{:S(2)}, u32[]{:S(2)}) %collective-permute-start.17) | collective-permute-done | bytes 909344 | tf_op jit(solution)/shard_map/ppermute | solution.py:12
  139.7 13.3 %collective-permute-done.16 = bf16[296,1536]{1,0:T(8,128)(2,1)} collective-permute-done((bf16[296,1536]{1,0:T(8,128)(2,1)}, bf16[296,1536]{1,0:T(8,128)(2,1)}, u32[]{:S(2)}, u32[]{:S(2)}) %collective-permute-start.16) | collective-permute-done | bytes 909344 | tf_op jit(solution)/shard_map/ppermute | solution.py:12
  153.7 3.5 pad_maximum_fusion.2
  158.1 31.4 %collective-permute-done.3 = bf16[768,1024]{1,0:T(8,128)(2,1)} collective-permute-done((bf16[768,1024]{1,0:T(8,128)(2,1)}, bf16[768,1024]{1,0:T(8,128)(2,1)}, u32[]{:S(2)}, u32[]{:S(2)}) %collective-permute-start.3) | collective-permute-done | bytes 1572896 | tf_op jit(solution)/shard_map/ppermute | solution.py:12
  190.6 36.7 %collective-permute-done.4 = bf16[768,1024]{1,0:T(8,128)(2,1)} collective-permute-done((bf16[768,1024]{1,0:T(8,128)(2,1)}, bf16[768,1024]{1,0:T(8,128)(2,1)}, u32[]{:S(2)}, u32[]{:S(2)}) %collective-permute-start.4) | collective-permute-done | bytes 1572896 | tf_op jit(solution)/shard_map/ppermute | solution.py:12
  227.2 3.5 broadcast_in_dim.79
  230.7 5.6 constant_dynamic-slice_fusion
  236.3 101.7 %collective-permute-start.9 = (bf16[1024,768]{1,0:T(8,128)(2,1)}, bf16[1024,768]{1,0:T(8,128)(2,1)}, u32[]{:S(2)}, u32[]{:S(2)}) collective-permute-start(bf16[1024,768]{1,0:T(8,128)(2,1)} %get-tuple-element.12), channel_id=1, source_target_pairs={{0,1},{1,0},{2,3},{3,2},{4,5},{5,4},{6,7},{7,6},{8,9},{9,8},{10,11... | collective-permute-start | bytes 4718600 | tf_op jit(solution)/shard_map/ppermute | solution.py:12
  360.7 68.7 %collective-permute-done.7 = bf16[768,1024]{1,0:T(8,128)(2,1)S(1)} collective-permute-done((bf16[768,1024]{1,0:T(8,128)(2,1)}, bf16[768,1024]{1,0:T(8,128)(2,1)S(1)}, u32[]{:S(2)}, u32[]{:S(2)}) %collective-permute-start.7) | collective-permute-done | bytes 1572896 | tf_op jit(solution)/shard_map/ppermute | solution.py:12
  438.8 58.1 %collective-permute-done.10 = bf16[1024,768]{1,0:T(8,128)(2,1)} collective-permute-done((bf16[1024,768]{1,0:T(8,128)(2,1)}, bf16[1024,768]{1,0:T(8,128)(2,1)}, u32[]{:S(2)}, u32[]{:S(2)}) %collective-permute-start.10) | collective-permute-done | bytes 1572896 | tf_op jit(solution)/shard_map/ppermute | solution.py:12
  502.4 13.5 %fusion.34 = f32[1184,1024]{1,0:T(8,128)} fusion(bf16[1184,3072]{1,0:T(8,128)(2,1)} %all-gather.7.cloned.1.call-done, bf16[3072,1024]{1,0:T(8,128)(2,1)} %constant_dynamic-update-slice_fusion.2), kind=kOutput, calls=%fused_computation.79 | convolution fusion | flops 7449083904 | bytes 18415616 | tf_op jit(solution)/shard_map/dot_general | solution.py:76
  515.9 11.4 %fusion.33 = f32[1184,1024]{1,0:T(8,128)} fusion(bf16[1184,3072]{1,0:T(8,128)(2,1)S(1)} %copy-done.12, bf16[3072,1024]{1,0:T(8,128)(2,1)} %constant_dynamic-update-slice_fusion.5), kind=kOutput, calls=%fused_computation.78 | convolution fusion | flops 7449083904 | bytes 18415616 | tf_op jit(solution)/shard_map/dot_general | solution.py:75
  527.3 16.5 %multiply_reduce_fusion = (f32[1184]{0:T(1024)S(1)}, bf16[1184,1024]{1,0:T(8,128)(2,1)S(1)}, f32[1184,1024]{1,0:T(8,128)}) fusion(f32[1184,1024]{1,0:T(8,128)} %fusion.34, f32[1184,1024]{1,0:T(8,128)} %fusion.33, bf16[1184,3072]{1,0:T(8,128)(2,1)} %all-gather.11.cloned.1.call-done, bf16[1024,3072]{1,0:T(8,128)(2,1)} %constant_dynamic-update-slice_fusion.8), kind=kOutput, calls=%fused_computation.5 | convolution fusion | flops 7459994624 | bytes 30544512 | tf_op jit(solution)/shard_map/dot_general | solution.py:101
  543.9 12.5 %convolution_convert_fusion = bf16[1184,3072]{1,0:T(8,128)(2,1)} fusion(bf16[1184,1024]{1,0:T(8,128)(2,1)S(1)} %get-tuple-element.6, bf16[1024,3072]{1,0:T(8,128)(2,1)} %constant_dynamic-update-slice_fusion.8), kind=kOutput, calls=%fused_computation.1 | convolution fusion | flops 7452721152 | bytes 15990784 | tf_op jit(solution)/shard_map/dot_general | solution.py:89
  556.4 25.1 %fusion.14 = f32[1184,3072]{1,0:T(8,128)} fusion(bf16[3072,1024]{1,0:T(8,128)(2,1)} %constant_dynamic-update-slice_fusion.2, f32[1184,1024]{1,0:T(8,128)} %get-tuple-element.37, f32[1184,1024]{1,0:T(8,128)} %fusion.33), kind=kOutput, calls=%fused_computation.25 | convolution fusion | flops 7456358400 | bytes 30539776 | tf_op jit(solution)/shard_map/dot_general | solution.py:105
  581.6 23.0 %add_convert_fusion = bf16[1184,3072]{1,0:T(8,128)(2,1)} fusion(f32[1184,3072]{1,0:T(8,128)} %fusion.14, bf16[3072,1024]{1,0:T(8,128)(2,1)} %constant_dynamic-update-slice_fusion.5, f32[1184,1024]{1,0:T(8,128)} %fusion.33, f32[1184,1024]{1,0:T(8,128)} %get-tuple-element.37, f32[1184,1024]{1,0:T(8,128)} %fusion.34), kind=kOutput, calls=%fused_computation | convolution fusion | flops 7468482560 | bytes 42663936 | tf_op jit(solution)/shard_map/dot_general | solution.py:104
  611.1 19.9 %collective-permute-done.14 = bf16[296,1536]{1,0:T(8,128)(2,1)S(1)} collective-permute-done((bf16[296,1536]{1,0:T(8,128)(2,1)S(1)}, bf16[296,1536]{1,0:T(8,128)(2,1)S(1)}, u32[]{:S(2)}, u32[]{:S(2)}) %collective-permute-start.14) | collective-permute-done | bytes 909344 | tf_op jit(solution)/shard_map/ppermute | solution.py:12
  631.0 10.5 %collective-permute-done.13 = bf16[296,1536]{1,0:T(8,128)(2,1)S(1)} collective-permute-done((bf16[296,1536]{1,0:T(8,128)(2,1)S(1)}, bf16[296,1536]{1,0:T(8,128)(2,1)S(1)}, u32[]{:S(2)}, u32[]{:S(2)}) %collective-permute-start.13) | collective-permute-done | bytes 909344 | tf_op jit(solution)/shard_map/ppermute | solution.py:12
  644.3 3.6 fusion.10
  653.8 20.5 %collective-permute-done.20 = bf16[296,1536]{1,0:T(8,128)(2,1)S(1)} collective-permute-done((bf16[296,1536]{1,0:T(8,128)(2,1)S(1)}, bf16[296,1536]{1,0:T(8,128)(2,1)S(1)}, u32[]{:S(2)}, u32[]{:S(2)}) %collective-permute-start.20) | collective-permute-done | bytes 909344 | tf_op jit(solution)/shard_map/ppermute | solution.py:12
  674.4 18.1 %collective-permute-done.19 = bf16[296,1536]{1,0:T(8,128)(2,1)S(1)} collective-permute-done((bf16[296,1536]{1,0:T(8,128)(2,1)S(1)}, bf16[296,1536]{1,0:T(8,128)(2,1)S(1)}, u32[]{:S(2)}, u32[]{:S(2)}) %collective-permute-start.19) | collective-permute-done | bytes 909344 | tf_op jit(solution)/shard_map/ppermute | solution.py:12
  692.8 3.6 fusion.11
  703.6 45.5 %psum.7 = f32[512,2]{0,1:T(2,128)S(1)} all-reduce(f32[512,2]{0,1:T(2,128)S(1)} %fusion.22), channel_id=1, replica_groups=mesh['expert'=4,'tensor'=2,'dp'=4] {'tensor','dp'}, use_global_device_ids=true, to_apply=%region_10.11 | all-reduce | flops 1024 | bytes 8192 | tf_op jit(solution)/shard_map/psum | solution.py:116
  749.7 10.7 %reduce-scatter.11.cloned.1.call-done = bf16[128,1536]{1,0:T(8,128)(2,1)} async-done(((bf16[512,1536]{1,0:T(8,128)(2,1)}), bf16[128,1536]{1,0:T(8,128)(2,1)}) %reduce-scatter.11.cloned.1.call-update) | async-done | bytes 393232 | tf_op jit(solution)/shard_map/reduce_scatter | solution.py:107
  (129 shorter events, 81.4 us)
Async XLA Ops:
  7.2 42.2 %all-gather.5.cloned.1.call-start = ((), (), s32[]{:S(2)}) async-start(), calls=%async_computation.4 | async-start | bytes 1966080 | tf_op jit(solution)/shard_map/all_gather | solution.py:49
  7.9 99.3 %all-gather.9.cloned.1.call-start = ((), (), s32[]{:S(2)}) async-start(), calls=%async_computation.8 | async-start | bytes 1966080 | tf_op jit(solution)/shard_map/all_gather | solution.py:50
  8.6 493.8 %all-gather.7.cloned.1.call-start = ((), (), s32[]{:S(2)}) async-start(), calls=%async_computation.5 | async-start | bytes 10911744 | tf_op jit(solution)/shard_map/all_gather | solution.py:70
  53.1 24.1 %collective-permute-start.2 = (bf16[296,1536]{1,0:T(8,128)(2,1)S(1)}, bf16[296,1536]{1,0:T(8,128)(2,1)S(1)}, u32[]{:S(2)}, u32[]{:S(2)}) collective-permute-start(bf16[296,1536]{1,0:T(8,128)(2,1)S(1)} %get-tuple-element.26), channel_id=1, source_target_pairs={{0,24},{8,16},{16,8},{24,0},{1,25},{9,17},{17,9},{25,1},{2,26},{10... | collective-permute-start | bytes 2727944 | tf_op jit(solution)/shard_map/ppermute | solution.py:12
  55.6 39.8 %collective-permute-start.1 = (bf16[296,1536]{1,0:T(8,128)(2,1)S(1)}, bf16[296,1536]{1,0:T(8,128)(2,1)S(1)}, u32[]{:S(2)}, u32[]{:S(2)}) collective-permute-start(bf16[296,1536]{1,0:T(8,128)(2,1)S(1)} %get-tuple-element.27), channel_id=1, source_target_pairs={{0,16},{8,24},{16,0},{24,8},{1,17},{9,25},{17,1},{25,9},{2,18},{10... | collective-permute-start | bytes 2727944 | tf_op jit(solution)/shard_map/ppermute | solution.py:12
  56.1 39.3 %collective-permute-start = (bf16[296,1536]{1,0:T(8,128)(2,1)S(1)}, bf16[296,1536]{1,0:T(8,128)(2,1)S(1)}, u32[]{:S(2)}, u32[]{:S(2)}) collective-permute-start(bf16[296,1536]{1,0:T(8,128)(2,1)S(1)} %get-tuple-element.28), channel_id=1, source_target_pairs={{0,8},{8,0},{16,24},{24,16},{1,9},{9,1},{17,25},{25,17},{2,10},{10... | collective-permute-start | bytes 2727944 | tf_op jit(solution)/shard_map/ppermute | solution.py:12
  97.5 429.9 %all-gather.11.cloned.1.call-start = ((), (), s32[]{:S(2)}) async-start(), calls=%async_computation.9 | async-start | bytes 10911744 | tf_op jit(solution)/shard_map/all_gather | solution.py:71
  112.4 24.3 %collective-permute-start.17 = (bf16[296,1536]{1,0:T(8,128)(2,1)}, bf16[296,1536]{1,0:T(8,128)(2,1)}, u32[]{:S(2)}, u32[]{:S(2)}) collective-permute-start(bf16[296,1536]{1,0:T(8,128)(2,1)} %get-tuple-element.30), channel_id=1, source_target_pairs={{0,24},{8,16},{16,8},{24,0},{1,25},{9,17},{17,9},{25,1},{2,26},{10... | collective-permute-start | bytes 2727944 | tf_op jit(solution)/shard_map/ppermute | solution.py:12
  113.9 39.1 %collective-permute-start.16 = (bf16[296,1536]{1,0:T(8,128)(2,1)}, bf16[296,1536]{1,0:T(8,128)(2,1)}, u32[]{:S(2)}, u32[]{:S(2)}) collective-permute-start(bf16[296,1536]{1,0:T(8,128)(2,1)} %get-tuple-element.31), channel_id=1, source_target_pairs={{0,16},{8,24},{16,0},{24,8},{1,17},{9,25},{17,1},{25,9},{2,18},{10... | collective-permute-start | bytes 2727944 | tf_op jit(solution)/shard_map/ppermute | solution.py:12
  115.4 38.3 %collective-permute-start.15 = (bf16[296,1536]{1,0:T(8,128)(2,1)}, bf16[296,1536]{1,0:T(8,128)(2,1)}, u32[]{:S(2)}, u32[]{:S(2)}) collective-permute-start(bf16[296,1536]{1,0:T(8,128)(2,1)} %get-tuple-element.32), channel_id=1, source_target_pairs={{0,8},{8,0},{16,24},{24,16},{1,9},{9,1},{17,25},{25,17},{2,10},{10... | collective-permute-start | bytes 2727944 | tf_op jit(solution)/shard_map/ppermute | solution.py:12
  120.7 68.8 %collective-permute-start.3 = (bf16[768,1024]{1,0:T(8,128)(2,1)}, bf16[768,1024]{1,0:T(8,128)(2,1)}, u32[]{:S(2)}, u32[]{:S(2)}) collective-permute-start(bf16[768,1024]{1,0:T(8,128)(2,1)} %get-tuple-element.15), channel_id=1, source_target_pairs={{0,1},{1,0},{2,3},{3,2},{4,5},{5,4},{6,7},{7,6},{8,9},{9,8},{10,11... | collective-permute-start | bytes 4718600 | tf_op jit(solution)/shard_map/ppermute | solution.py:12
  121.2 106.0 %collective-permute-start.4 = (bf16[768,1024]{1,0:T(8,128)(2,1)}, bf16[768,1024]{1,0:T(8,128)(2,1)}, u32[]{:S(2)}, u32[]{:S(2)}) collective-permute-start(bf16[768,1024]{1,0:T(8,128)(2,1)} %get-tuple-element.16), channel_id=1, source_target_pairs={{0,2},{1,3},{2,0},{3,1},{4,6},{5,7},{6,4},{7,5},{8,10},{9,11},{10,... | collective-permute-start | bytes 4718600 | tf_op jit(solution)/shard_map/ppermute | solution.py:12
  136.7 90.5 %collective-permute-start.5 = (bf16[768,1024]{1,0:T(8,128)(2,1)}, bf16[768,1024]{1,0:T(8,128)(2,1)}, u32[]{:S(2)}, u32[]{:S(2)}) collective-permute-start(bf16[768,1024]{1,0:T(8,128)(2,1)} %get-tuple-element.14), channel_id=1, source_target_pairs={{0,3},{1,2},{2,1},{3,0},{4,7},{5,6},{6,5},{7,4},{8,11},{9,10},{10,... | collective-permute-start | bytes 4718600 | tf_op jit(solution)/shard_map/ppermute | solution.py:12
  153.0 185.0 %collective-permute-start.6 = (bf16[768,1024]{1,0:T(8,128)(2,1)}, bf16[768,1024]{1,0:T(8,128)(2,1)}, u32[]{:S(2)}, u32[]{:S(2)}) collective-permute-start(bf16[768,1024]{1,0:T(8,128)(2,1)} %get-tuple-element.8), channel_id=1, source_target_pairs={{0,1},{1,0},{2,3},{3,2},{4,5},{5,4},{6,7},{7,6},{8,9},{9,8},{10,11... | collective-permute-start | bytes 4718600 | tf_op jit(solution)/shard_map/ppermute | solution.py:12
  157.2 447.5 %reduce-scatter.5.cloned.1.call-start = ((), (), s32[]{:S(2)}) async-start(), calls=%async_computation.6 | async-start | bytes 10911744 | tf_op jit(solution)/shard_map/reduce_scatter | solution.py:85
  157.3 272.1 %collective-permute-start.7 = (bf16[768,1024]{1,0:T(8,128)(2,1)}, bf16[768,1024]{1,0:T(8,128)(2,1)S(1)}, u32[]{:S(2)}, u32[]{:S(2)}) collective-permute-start(bf16[768,1024]{1,0:T(8,128)(2,1)} %get-tuple-element.9), channel_id=1, source_target_pairs={{0,2},{1,3},{2,0},{3,1},{4,6},{5,7},{6,4},{7,5},{8,10},{9,11},{10,... | collective-permute-start | bytes 4718600 | tf_op jit(solution)/shard_map/ppermute | solution.py:12
  189.5 243.8 %collective-permute-start.8 = (bf16[768,1024]{1,0:T(8,128)(2,1)S(1)}, bf16[768,1024]{1,0:T(8,128)(2,1)}, u32[]{:S(2)}, u32[]{:S(2)}) collective-permute-start(bf16[768,1024]{1,0:T(8,128)(2,1)S(1)} %copy-done), channel_id=1, source_target_pairs={{0,3},{1,2},{2,1},{3,0},{4,7},{5,6},{6,5},{7,4},{8,11},{9,10},{10,... | collective-permute-start | bytes 4718600 | tf_op jit(solution)/shard_map/ppermute | solution.py:12
  236.3 199.7 %collective-permute-start.9 = (bf16[1024,768]{1,0:T(8,128)(2,1)}, bf16[1024,768]{1,0:T(8,128)(2,1)}, u32[]{:S(2)}, u32[]{:S(2)}) collective-permute-start(bf16[1024,768]{1,0:T(8,128)(2,1)} %get-tuple-element.12), channel_id=1, source_target_pairs={{0,1},{1,0},{2,3},{3,2},{4,5},{5,4},{6,7},{7,6},{8,9},{9,8},{10,11... | collective-permute-start | bytes 4718600 | tf_op jit(solution)/shard_map/ppermute | solution.py:12
  338.1 158.8 %collective-permute-start.10 = (bf16[1024,768]{1,0:T(8,128)(2,1)}, bf16[1024,768]{1,0:T(8,128)(2,1)}, u32[]{:S(2)}, u32[]{:S(2)}) collective-permute-start(bf16[1024,768]{1,0:T(8,128)(2,1)} %get-tuple-element.11), channel_id=1, source_target_pairs={{0,2},{1,3},{2,0},{3,1},{4,6},{5,7},{6,4},{7,5},{8,10},{9,11},{10,... | collective-permute-start | bytes 4718600 | tf_op jit(solution)/shard_map/ppermute | solution.py:12
  338.1 161.6 %collective-permute-start.11 = (bf16[1024,768]{1,0:T(8,128)(2,1)}, bf16[1024,768]{1,0:T(8,128)(2,1)}, u32[]{:S(2)}, u32[]{:S(2)}) collective-permute-start(bf16[1024,768]{1,0:T(8,128)(2,1)} %get-tuple-element.10), channel_id=1, source_target_pairs={{0,3},{1,2},{2,1},{3,0},{4,7},{5,6},{6,5},{7,4},{8,11},{9,10},{10,... | collective-permute-start | bytes 4718600 | tf_op jit(solution)/shard_map/ppermute | solution.py:12
  556.4 91.6 %reduce-scatter.9.cloned.1.call-start = ((), (), s32[]{:S(2)}) async-start(), calls=%async_computation.10 | async-start | bytes 10911744 | tf_op jit(solution)/shard_map/reduce_scatter | solution.py:85
  604.6 145.0 %reduce-scatter.7.cloned.1.call-start = ((), (), s32[]{:S(2)}) async-start(), calls=%async_computation.7 | async-start | bytes 1966080 | tf_op jit(solution)/shard_map/reduce_scatter | solution.py:99
  606.9 24.1 %collective-permute-start.14 = (bf16[296,1536]{1,0:T(8,128)(2,1)S(1)}, bf16[296,1536]{1,0:T(8,128)(2,1)S(1)}, u32[]{:S(2)}, u32[]{:S(2)}) collective-permute-start(bf16[296,1536]{1,0:T(8,128)(2,1)S(1)} %get-tuple-element.22), channel_id=1, source_target_pairs={{0,24},{8,16},{16,8},{24,0},{1,25},{9,17},{17,9},{25,1},{2,26},{10... | collective-permute-start | bytes 2727944 | tf_op jit(solution)/shard_map/ppermute | solution.py:12
  608.2 33.3 %collective-permute-start.13 = (bf16[296,1536]{1,0:T(8,128)(2,1)S(1)}, bf16[296,1536]{1,0:T(8,128)(2,1)S(1)}, u32[]{:S(2)}, u32[]{:S(2)}) collective-permute-start(bf16[296,1536]{1,0:T(8,128)(2,1)S(1)} %get-tuple-element.23), channel_id=1, source_target_pairs={{0,16},{8,24},{16,0},{24,8},{1,17},{9,25},{17,1},{25,9},{2,18},{10... | collective-permute-start | bytes 2727944 | tf_op jit(solution)/shard_map/ppermute | solution.py:12
  609.8 32.0 %collective-permute-start.12 = (bf16[296,1536]{1,0:T(8,128)(2,1)S(1)}, bf16[296,1536]{1,0:T(8,128)(2,1)S(1)}, u32[]{:S(2)}, u32[]{:S(2)}) collective-permute-start(bf16[296,1536]{1,0:T(8,128)(2,1)S(1)} %get-tuple-element.24), channel_id=1, source_target_pairs={{0,8},{8,0},{16,24},{24,16},{1,9},{9,1},{17,25},{25,17},{2,10},{10... | collective-permute-start | bytes 2727944 | tf_op jit(solution)/shard_map/ppermute | solution.py:12
  647.9 112.4 %reduce-scatter.11.cloned.1.call-start = ((), (), s32[]{:S(2)}) async-start(), calls=%async_computation.11 | async-start | bytes 1966080 | tf_op jit(solution)/shard_map/reduce_scatter | solution.py:107
  650.3 24.1 %collective-permute-start.20 = (bf16[296,1536]{1,0:T(8,128)(2,1)S(1)}, bf16[296,1536]{1,0:T(8,128)(2,1)S(1)}, u32[]{:S(2)}, u32[]{:S(2)}) collective-permute-start(bf16[296,1536]{1,0:T(8,128)(2,1)S(1)} %get-tuple-element.18), channel_id=1, source_target_pairs={{0,24},{8,16},{16,8},{24,0},{1,25},{9,17},{17,9},{25,1},{2,26},{10... | collective-permute-start | bytes 2727944 | tf_op jit(solution)/shard_map/ppermute | solution.py:12
  651.9 40.7 %collective-permute-start.19 = (bf16[296,1536]{1,0:T(8,128)(2,1)S(1)}, bf16[296,1536]{1,0:T(8,128)(2,1)S(1)}, u32[]{:S(2)}, u32[]{:S(2)}) collective-permute-start(bf16[296,1536]{1,0:T(8,128)(2,1)S(1)} %get-tuple-element.19), channel_id=1, source_target_pairs={{0,16},{8,24},{16,0},{24,8},{1,17},{9,25},{17,1},{25,9},{2,18},{10... | collective-permute-start | bytes 2727944 | tf_op jit(solution)/shard_map/ppermute | solution.py:12
  653.3 39.6 %collective-permute-start.18 = (bf16[296,1536]{1,0:T(8,128)(2,1)S(1)}, bf16[296,1536]{1,0:T(8,128)(2,1)S(1)}, u32[]{:S(2)}, u32[]{:S(2)}) collective-permute-start(bf16[296,1536]{1,0:T(8,128)(2,1)S(1)} %get-tuple-element.20), channel_id=1, source_target_pairs={{0,8},{8,0},{16,24},{24,16},{1,9},{9,1},{17,25},{25,17},{2,10},{10... | collective-permute-start | bytes 2727944 | tf_op jit(solution)/shard_map/ppermute | solution.py:12
  696.6 4.5 collective-permute-start.23
  698.0 3.6 collective-permute-start.22
  699.5 3.6 collective-permute-start.21
  (15 other events, 499.4 us)
Sparse Core Ops, SparseCore 0:
  9.6 39.7 all-gather.4
  51.0 35.9 all-gather.8
  97.6 16.4 all-gather.6
  157.4 16.4 all-gather.10
  556.5 39.8 reduce-scatter.4
  604.7 39.0 reduce-scatter.8
  648.0 63.2 reduce-scatter.6
  714.2 46.1 reduce-scatter.10

commit v2 on v1

v2 whole, which is shorter than its diff:
```python
import jax
import jax.numpy as jnp
from jax import lax
from jax.experimental import pallas as pl
from jax.experimental.pallas import tpu as pltpu
from jax.sharding import PartitionSpec as P

F32 = jnp.float32
BF16 = jnp.bfloat16
ROWS = (((1,), (1,)), ((), ()))
OVER = (((0,), (0,)), ((), ()))
LIGHT = pl.CostEstimate(flops=0, bytes_accessed=0, transcendentals=0)


def swap(value, axis, shift):
    size = lax.axis_size(axis)
    return lax.ppermute(value, axis, [(i, i ^ shift) for i in range(size)])


def tie(*values):
    return lax.optimization_barrier(values)


def mm(a, b):
    return jnp.dot(a, b, preferred_element_type=F32)


def mmt(a, b):
    return lax.dot_general(a, b, ROWS, preferred_element_type=F32)


def join_body(at_ref, *refs):
    parts = len(refs) - at_ref.shape[0]
    pieces, wholes = refs[:-parts], refs[-parts:]
    for n, piece in enumerate(pieces):

        @pl.when(pl.program_id(0) == n)
        def _(piece=piece):
            rows = piece.shape[0] // len(wholes)
            for k, whole in enumerate(wholes):
                whole[...] = piece[k * rows : (k + 1) * rows]


def join(pieces, dim, places, parts):
    rows, cols = pieces[0].shape
    rows //= parts
    shape = (rows * len(pieces), cols) if dim == 0 else (rows, cols * len(pieces))
    spec = pl.BlockSpec((rows, cols), lambda n, at: (at[n], 0) if dim == 0 else (0, at[n]))
    return pl.pallas_call(
        join_body,
        grid_spec=pltpu.PrefetchScalarGridSpec(
            num_scalar_prefetch=1,
            grid=(len(pieces),),
            in_specs=[pl.BlockSpec((rows * parts, cols), lambda n, at: (0, 0))] * len(pieces),
            out_specs=[spec] * parts,
        ),
        out_shape=[jax.ShapeDtypeStruct(shape, BF16)] * parts,
        cost_estimate=LIGHT,
        compiler_params=pltpu.CompilerParams(vmem_limit_bytes=56 << 20),
        name="join",
    )(places, *pieces)


def chunk_body(at_ref, gate_ref, up_ref, out_ref):
    @pl.when(pl.program_id(0) == 0)
    def _():
        out_ref[...] = gate_ref[...]

    @pl.when(pl.program_id(0) == 1)
    def _():
        out_ref[...] = up_ref[...]


def gate_up_chunk(gate, up, index, width):
    rows = gate.shape[0]
    tile = rows // 3 if rows % 48 == 0 else rows
    steps = rows // tile
    return pl.pallas_call(
        chunk_body,
        grid_spec=pltpu.PrefetchScalarGridSpec(
            num_scalar_prefetch=1,
            grid=(2, steps),
            in_specs=[
                pl.BlockSpec((tile, width), lambda p, n, at: (jnp.where(p == 0, n, steps - 1), at[0])),
                pl.BlockSpec((tile, width), lambda p, n, at: (jnp.where(p == 0, 0, n), at[0])),
            ],
            out_specs=pl.BlockSpec((tile, width), lambda p, n, at: (p * steps + n, 0)),
        ),
        out_shape=jax.ShapeDtypeStruct((2 * rows, width), BF16),
        cost_estimate=LIGHT,
        name="gate_up_chunk",
    )(jnp.reshape(index, (1,)).astype(jnp.int32), gate, up)


def product_body(a_ref, w_ref, *rest):
    total = mm(a_ref[...], w_ref[...])
    if len(rest) == 2 and rest[0].shape[1] == 1:
        total = total * rest[0][...]
    elif len(rest) == 2:
        total = total + rest[0][...].astype(F32)
    rest[-1][...] = total.astype(BF16)


def product(a, w, first, width, extra=None, scale=None):
    height, depth = a.shape
    tile = 256
    steps = width // tile
    out_spec = pl.BlockSpec((height, tile), lambda n: (0, n))
    return pl.pallas_call(
        product_body,
        grid=(steps,),
        in_specs=[
            pl.BlockSpec((height, depth), lambda n: (0, 0)),
            pl.BlockSpec((depth, tile), lambda n: (0, first * steps + n)),
        ]
        + ([] if extra is None else [out_spec])
        + ([] if scale is None else [pl.BlockSpec((height, 1), lambda n: (0, 0))]),
        out_specs=out_spec,
        out_shape=jax.ShapeDtypeStruct((height, width), BF16),
        cost_estimate=LIGHT,
        compiler_params=pltpu.CompilerParams(vmem_limit_bytes=56 << 20),
        name="product",
    )(*([a, w] + [part for part in (extra, scale) if part is not None]))


def pair_body(a_ref, b_ref, wa_ref, wb_ref, *rest):
    total = mmt(a_ref[...], wa_ref[...]) + mmt(b_ref[...], wb_ref[...])
    if len(rest) == 2:
        total = total + rest[0][...].astype(F32)
    rest[-1][...] = total.astype(BF16)


def pair_product(a, b, wa, wb, first, width, extra=None):
    height, depth = a.shape
    tile = 256
    steps = width // tile
    row_spec = pl.BlockSpec((height, depth), lambda n: (0, 0))
    col_spec = pl.BlockSpec((tile, depth), lambda n: (first * steps + n, 0))
    out_spec = pl.BlockSpec((height, tile), lambda n: (0, n))
    ins = [a, b, wa, wb] + ([] if extra is None else [extra])
    return pl.pallas_call(
        pair_body,
        grid=(steps,),
        in_specs=[row_spec, row_spec, col_spec, col_spec] + ([] if extra is None else [out_spec]),
        out_specs=out_spec,
        out_shape=jax.ShapeDtypeStruct((height, width), BF16),
        cost_estimate=LIGHT,
        compiler_params=pltpu.CompilerParams(vmem_limit_bytes=56 << 20),
        name="pair_product",
    )(*ins)


def hidden_body(xa_ref, xb_ref, gate_ref, up_ref, hid_ref, silu_ref, fac_ref):
    half = xa_ref.shape[1]

    def pre(w_ref):
        return mm(xa_ref[...], w_ref[:half]) + mm(xb_ref[...], w_ref[half:])

    gate, up = pre(gate_ref), pre(up_ref)
    sig = jax.nn.sigmoid(gate)
    silu = gate * sig
    silu_ref[...] = silu
    hid_ref[...] = (silu * up).astype(BF16)
    fac_ref[...] = up * sig * (1.0 + gate * (1.0 - sig))


def hidden_layer(xa, xb, gate, up, height):
    R, half = xa.shape
    D, Fc = gate.shape
    tile = min(256, Fc)
    row = pl.BlockSpec((height, half), lambda r, f: (r, 0))
    col = pl.BlockSpec((D, tile), lambda r, f: (0, f))
    block = pl.BlockSpec((height, tile), lambda r, f: (r, f))
    return pl.pallas_call(
        hidden_body,
        grid=(R // height, Fc // tile),
        in_specs=[row, row, col, col],
        out_specs=[block] * 3,
        out_shape=[
            jax.ShapeDtypeStruct((R, Fc), BF16),
            jax.ShapeDtypeStruct((R, Fc), F32),
            jax.ShapeDtypeStruct((R, Fc), F32),
        ],
        cost_estimate=LIGHT,
        compiler_params=pltpu.CompilerParams(vmem_limit_bytes=48 << 20),
        name="hidden_layer",
    )(xa, xb, gate, up)


def grads_body(ga_ref, gb_ref, down_ref, silu_ref, fac_ref, hid_ref, up_ref, gate_ref, dots_ref):
    half = ga_ref.shape[1]
    hg = mmt(ga_ref[...], down_ref[:, :half]) + mmt(gb_ref[...], down_ref[:, half:])
    up_ref[...] = (hg * silu_ref[...]).astype(BF16)
    gate_ref[...] = (hg * fac_ref[...]).astype(BF16)
    prod = hg * hid_ref[...].astype(F32)
    lanes = dots_ref.shape[1]
    total = prod[:, :lanes]
    for n in range(1, prod.shape[1] // lanes):
        total = total + prod[:, n * lanes : (n + 1) * lanes]

    @pl.when(pl.program_id(1) == 0)
    def _():
        dots_ref[...] = total

    @pl.when(pl.program_id(1) > 0)
    def _():
        dots_ref[...] += total


def grads(g_a, g_b, down, silu, fac, hidden, height):
    R, Fc = hidden.shape
    half = g_a.shape[1]
    tile = min(256, Fc)
    block = pl.BlockSpec((height, tile), lambda r, f: (r, f))
    return pl.pallas_call(
        grads_body,
        grid=(R // height, Fc // tile),
        in_specs=[
            pl.BlockSpec((height, half), lambda r, f: (r, 0)),
            pl.BlockSpec((height, half), lambda r, f: (r, 0)),
            pl.BlockSpec((tile, 2 * half), lambda r, f: (f, 0)),
            block,
            block,
            block,
        ],
        out_specs=[block, block, pl.BlockSpec((height, 128), lambda r, f: (r, 0))],
        out_shape=[
            jax.ShapeDtypeStruct((R, Fc), BF16),
            jax.ShapeDtypeStruct((R, Fc), BF16),
            jax.ShapeDtypeStruct((R, 128), F32),
        ],
        cost_estimate=LIGHT,
        compiler_params=pltpu.CompilerParams(vmem_limit_bytes=56 << 20),
        name="grads",
    )(g_a, g_b, down, silu, fac, hidden)


def local(tokens, experts_chosen, route_weights, cotangent, gate_weight, up_weight, down_weight):
    E, T, Z = lax.axis_size("expert"), lax.axis_size("tensor"), lax.axis_size("dp")
    me_t, me_d = lax.axis_index("tensor"), lax.axis_index("dp")
    B, Fh = tokens.shape
    K = experts_chosen.shape[1]
    cap = min(B, 9 * B * K // (8 * E) + 1)
    capr = -(-Z * cap // 8) * 8
    G = Z * B
    R = E * capr
    Dq, Ft = gate_weight.shape[1:]
    Fc = Ft // Z
    D = Dq * Z
    two = T == 2 and Z % 2 == 0 and Fh % 256 == 0
    H = R // 2

    def place_of(q):
        if not two:
            return q
        return ((q // (Z // 2)) ^ me_t) * (Z // 2) + q % (Z // 2)

    wide = [experts_chosen.astype(F32)]
    left = route_weights
    for _ in range(3):
        wide.append(left.astype(BF16).astype(F32))
        left = left - wide[-1]
    wide = jnp.concatenate(wide, axis=1).astype(BF16)
    wide = jnp.pad(wide, ((0, 0), (0, 128 - wide.shape[1])))
    tok_g = lax.all_gather(jnp.concatenate([tokens, wide], axis=1), "dp", axis=0, tiled=True)
    cot_g = lax.all_gather(cotangent, "dp", axis=0, tiled=True)

    gate_up_p = [gate_up_chunk(gate_weight[0], up_weight[0], me_d ^ s, Fc) for s in range(Z)]
    down_p = [lax.dynamic_slice_in_dim(down_weight[0], (me_d ^ s) * Fc, Fc, 0) for s in range(Z)]
    tok_g, gate_up_p, down_p = tie(tok_g, gate_up_p, down_p)
    shifts = list(range(2, Z)) + [1]
    for s in shifts:
        gate_up_p[s] = swap(gate_up_p[s], "dp", s)
    for s in shifts:
        down_p[s], gate_up_p[s] = tie(down_p[s], gate_up_p[s])
        down_p[s] = swap(down_p[s], "dp", s)

    routing = tok_g[:, Fh:].astype(F32)
    tok_g = tok_g[:, :Fh]
    ids = routing[:, :K].astype(jnp.int32)
    wts = routing[:, K : 2 * K] + routing[:, 2 * K : 3 * K] + routing[:, 3 * K : 4 * K]
    rel = jnp.arange(E, dtype=jnp.int32)
    named = ids[:, :, None] == rel[None, None, :]
    hit = jnp.any(named, axis=1)
    wtok = jnp.sum(jnp.where(named, wts[:, :, None], 0.0), axis=1)
    order = jnp.arange(G, dtype=jnp.int32)
    before = (order[None, :] < order[:, None]).astype(BF16)
    pos = jnp.where(hit, mm(before, hit.astype(BF16)), -1.0)
    place = pos.T[:, None, :] == jnp.arange(capr, dtype=F32)[None, :, None]
    pick = place.astype(BF16).reshape(R, G)
    heavy = jnp.where(place, wtok.T[:, None, :], 0.0).reshape(R, G)
    heavy_hi = heavy.astype(BF16)
    heavy_lo = (heavy - heavy_hi.astype(F32)).astype(BF16)
    wslot = jnp.sum(heavy, axis=1, keepdims=True)

    def over_expert(rows):
        rows = rows.reshape(E, capr, -1)
        return lax.all_to_all(rows, "expert", 0, 0, tiled=True).reshape(R, -1)

    def widen(half):
        if two:
            return half, swap(half, "tensor", 1)
        full = lax.all_gather(half, "tensor", axis=1, tiled=True)
        return full[:, : D // 2], full[:, D // 2 :]

    if two:
        x_send, g_send = product(pick, tok_g, 0, Fh), product(pick, cot_g, 0, Fh, scale=wslot)
    else:
        x_send, g_send = mm(pick, tok_g).astype(BF16), (mm(pick, cot_g) * wslot).astype(BF16)
    me_e = lax.axis_index("expert")
    x_back = x_send
    for s in range(1, E):
        at = (me_e ^ s) * capr
        part = swap(lax.dynamic_slice_in_dim(x_send, at, capr, 0), "expert", s)
        x_back = lax.dynamic_update_slice_in_dim(x_back, part, at, 0)
    g_send, gate_up_p = tie(g_send, gate_up_p)
    x = widen(x_back)
    g = widen(over_expert(g_send))

    places = place_of(me_d ^ jnp.arange(Z, dtype=jnp.int32))
    gate, up = join(gate_up_p, 0, places, 2)
    hidden, silu, fac = hidden_layer(x[0], x[1], gate, up, H)
    down_p, hidden, silu, fac = lax.optimization_barrier((down_p, hidden, silu, fac))
    (down,) = join(down_p, 1, places, 1)

    def combine(weights, back):
        return lax.dot_general(weights, back, OVER, preferred_element_type=F32)

    def to_blocks(value, dtype):
        def block(s):
            return lax.dynamic_slice_in_dim(value, (me_d ^ s) * B, B, 0)

        total = block(0)
        for s in range(1, Z):
            total = total + swap(block(s).astype(dtype), "dp", s).astype(F32)
        return total

    def fold(make, whole, parts):
        if not two:
            mine = lax.psum_scatter(
                whole().astype(BF16), "tensor", scatter_dimension=1, tiled=True
            )
            return [mine]
        others = [swap(make(parts + n, parts), "tensor", 1) for n in range(parts)]
        return [make(n, parts, others[n]) for n in range(parts)]

    def make_out(first, parts, extra=None):
        return product(hidden, down, first, D // 2 // parts, extra)

    (out_mine,) = fold(make_out, lambda: mm(hidden, down), 1)
    (g_mine, g_other), out_mine = tie(g, out_mine)
    out_back = over_expert(out_mine)
    up_grad, gate_grad, dots = grads(g_mine, g_other, down, silu, fac, hidden, H)

    def make_in(first, parts, extra=None):
        return pair_product(gate_grad, up_grad, gate, up, first, D // 2 // parts, extra)

    in_mine = fold(make_in, lambda: mmt(gate_grad, gate) + mmt(up_grad, up), 2)
    dots = jnp.sum(dots, axis=1)
    if two:
        dots = dots + swap(dots, "tensor", 1)
    else:
        dots = lax.psum(dots, "tensor")
    dots = dots.reshape(E, capr)
    spare = two and capr - Z * cap >= 3 and D // 4 >= capr
    if spare:
        rows3 = []
        for _ in range(3):
            rows3.append(dots.astype(BF16))
            dots = dots - rows3[-1].astype(F32)
        rows3 = jnp.pad(jnp.stack(rows3, axis=1), ((0, 0), (0, 0), (0, D // 4 - capr)))
        last = in_mine[1].reshape(E, capr, -1)
        last = lax.dynamic_update_slice(last, rows3, (0, Z * cap, 0))
        in_mine[1] = last.reshape(R, -1)
    in_mine, out_back = tie(in_mine, out_back)
    in_back = []
    for n, part in enumerate(in_mine):
        if n:
            part, in_back[n - 1] = tie(part, in_back[n - 1])
        in_back.append(over_expert(part))
    if spare:
        dots = in_back[1].reshape(E, capr, -1)[:, Z * cap : Z * cap + 3, :capr].astype(F32)
        dots = jnp.sum(dots, axis=1)
    else:
        dots = over_expert(dots.reshape(R, 1)).reshape(E, capr)
    out_tok = (combine(heavy_hi, out_back) + combine(heavy_lo, out_back)).astype(BF16)
    layer_output = lax.psum_scatter(out_tok, "dp", scatter_dimension=0, tiled=True)
    token_grad = [to_blocks(combine(pick, p), BF16).astype(BF16) for p in in_back]
    token_grad = jnp.concatenate(token_grad, axis=1)

    by_tok = jnp.sum(jnp.where(place, dots[:, :, None], 0.0), axis=1).T
    by_tok = by_tok / jnp.where(hit, wtok, 1.0)
    pair = jnp.sum(jnp.where(named, by_tok[:, None, :], 0.0), axis=2)
    route_grad = to_blocks(pair, F32)
    return layer_output, token_grad, route_grad


def solution(mesh):
    rows = P(("expert", "dp"), "tensor")
    pairs = P(("expert", "dp"), None)
    wide = P("expert", "dp", "tensor")
    in_specs = (rows, pairs, pairs, rows, wide, wide, P("expert", "tensor", "dp"))
    return jax.shard_map(
        local, mesh=mesh, in_specs=in_specs, out_specs=(rows, rows, pairs), check_vma=False
    )
```

time: 771 us -> 715 us (0.927)
  Pallas kernels: 0 us -> 144 us
  matrix products: 119 us -> 16.9 us
  waiting for transfers between devices: 374 us -> 445 us
  starting transfers between devices: 126 us -> 56.8 us
  blocking collectives: 67.5 us -> 0 us
  local copies, waits for them, and re-layouts: 58.7 us -> 24.9 us
    pallas_call x0 -> x16, Pallas kernels: none -> 144 us  [the longest x4 33.5 us: pair_product(): pl.pallas_call(pair_body, grid=(steps,), in_specs=[row_spec, row_spec, co...]
    all_gather x1, waiting for transfers between devices: 0.01 us -> 110 us  [local(): cot_g = lax.all_gather(cotangent, 'dp', axis=0, tiled=True)]
    dot_general x12 -> x5, matrix products: 119 us -> 16.9 us  [the longest x4 16.7 us: combine(): return lax.dot_general(weights, back, OVER, preferred_element_type=F32)]
    ppermute x24, starting transfers between devices: 126 us -> 39.2 us  [swap(): return lax.ppermute(value, axis, [(i, i ^ shift) for i in range(size)])]
    psum x1 -> x0, blocking collectives: 45.5 us -> none  [local(): pair = lax.psum(pair, ('tensor', 'dp'))]
    ppermute x24, waiting for transfers between devices: 334 us -> 305 us  [swap(): return lax.ppermute(value, axis, [(i, i ^ shift) for i in range(size)])]
    dynamic_update_slice x11 -> x3, local copies, waits for them, and re-layouts: 28.4 us -> 3.52 us  [the longest x2 2.06 us: local(): x_back = lax.dynamic_update_slice_in_dim(x_back, part, at, 0)]
    all_gather x2 -> x0, blocking collectives: 22 us -> none  [the longest x1 12.8 us: local(): ids = lax.all_gather(experts_chosen, 'dp', axis=0, tiled=True)]
  transfers between devices with their start and end apart: 32 -> 31, of which waited for: 20 -> 14; matrix products, arithmetic and copies ran while one was open for 20% -> 5% of each run, Pallas kernels for 0% -> 19%
where the time goes in v2:
time: 715 us; the launch traced here: 713 us
  waiting for transfers between devices  445 us (62%)
  Pallas kernels  144 us (20%)
  starting transfers between devices  56.8 us (8%)
  local copies, waits for them, and re-layouts  24.9 us (3%)
  matrix products  16.9 us (2%)
  between operations  14 us (2%)
  other arithmetic  11 us (2%)
    ppermute x24, waiting for transfers between devices, swap(): return lax.ppermute(value, axis, [(i, i ^ shift) for i in range(size)])  305 us
    all_gather x1, waiting for transfers between devices, local(): cot_g = lax.all_gather(cotangent, 'dp', axis=0, tiled=True)  110 us
    ppermute x24, starting transfers between devices, swap(): return lax.ppermute(value, axis, [(i, i ^ shift) for i in range(size)])  39.2 us
    pallas_call x4, Pallas kernels, pair_product(): pl.pallas_call(pair_body, grid=(steps,), in_specs=[row_spec, row_spec, co...  33.5 us
    pallas_call x4, Pallas kernels, product(): pl.pallas_call(product_body, grid=(steps,), in_specs=[pl.BlockSpec((heigh...  31.7 us
    pallas_call x1, Pallas kernels, hidden_layer(): pl.pallas_call(hidden_body, grid=(R // height, Fc // tile), in_specs=[row...  22 us
    pallas_call x4, Pallas kernels, gate_up_chunk(): pl.pallas_call(chunk_body, grid_spec=pltpu.PrefetchScalarGridSpec(num_sca...  22 us
    pallas_call x1, Pallas kernels, grads(): pl.pallas_call(grads_body, grid=(R // height, Fc // tile), in_specs=[pl.B...  17.6 us
  transfers between devices with their start and end apart: 31, of which 14 were waited for; matrix products, arithmetic and copies ran while one was open for 5% of the time, Pallas kernels for 19%

profile of v2, /device:TPU:0, one launch (start us, length us, event | category | flops | bytes accessed | tf_op | source)
XLA Modules:
  0.0 712.6 jit_solution(10932047555361528550)
XLA Ops:
  10.7 5.5 gate_up_chunk.5
  16.2 5.5 gate_up_chunk.6
  21.7 5.5 gate_up_chunk.7
  27.2 5.5 gate_up_chunk.4.refs_0_
  32.7 5.6 dynamic-slice_bitcast_fusion
  38.3 14.4 %all-gather.3.cloned.1.call-done = bf16[512,1664]{1,0:T(8,128)(2,1)} async-done(((bf16[128,1664]{1,0:T(8,128)(2,1)}), bf16[512,1664]{1,0:T(8,128)(2,1)}) %all-gather.3.cloned.1.call-update) | async-done | bytes 1703952 | tf_op jit(solution)/shard_map/all_gather | solution.py:265
  58.8 6.9 product.5
  73.8 16.3 %collective-permute-done.7 = bf16[296,1536]{1,0:T(8,128)(2,1)} collective-permute-done((bf16[296,1536]{1,0:T(8,128)(2,1)}, bf16[296,1536]{1,0:T(8,128)(2,1)}, u32[]{:S(2)}, u32[]{:S(2)}) %collective-permute-start.7) | collective-permute-done | bytes 909344 | tf_op jit(solution)/shard_map/ppermute | solution.py:17
  95.9 37.6 %collective-permute-done.8 = bf16[296,1536]{1,0:T(8,128)(2,1)S(1)} collective-permute-done((bf16[296,1536]{1,0:T(8,128)(2,1)S(1)}, bf16[296,1536]{1,0:T(8,128)(2,1)S(1)}, u32[]{:S(2)}, u32[]{:S(2)}) %collective-permute-start.8) | collective-permute-done | bytes 909344 | tf_op jit(solution)/shard_map/ppermute | solution.py:17
  137.1 109.7 %all-gather.5.cloned.1.call-done.w_ref = bf16[512,1536]{1,0:T(8,128)(2,1)} async-done(((bf16[128,1536]{1,0:T(8,128)(2,1)}), bf16[512,1536]{1,0:T(8,128)(2,1)}) %all-gather.5.cloned.1.call-update) | async-done | bytes 1572880 | tf_op jit(solution)/shard_map/all_gather | solution.py:266
  246.8 7.0 product.4
  253.8 112.6 %collective-permute-done.1.refs_2_ = bf16[1536,1024]{1,0:T(8,128)(2,1)} collective-permute-done((bf16[1536,1024]{1,0:T(8,128)(2,1)}, bf16[1536,1024]{1,0:T(8,128)(2,1)}, u32[]{:S(2)}, u32[]{:S(2)}) %collective-permute-start.1) | collective-permute-done | bytes 3145760 | tf_op jit(solution)/shard_map/ppermute | solution.py:17
  376.1 10.6 %join.2 = (bf16[3072,1024]{1,0:T(8,128)(2,1)}, bf16[3072,1024]{1,0:T(8,128)(2,1)}) custom-call(s32[4]{0:T(128)} %fusion.20.at_ref, bf16[1536,1024]{1,0:T(8,128)(2,1)} %gate_up_chunk.4.refs_0_, bf16[1536,1024]{1,0:T(8,128)(2,1)} %collective-permute-done.refs_1_, bf16[1536,1024]{1,0:T(8,128)(2,1)} %collective-permute-done.1.refs_2_, ...), custom_call_target="tpu_custom_call" | custom-call | tf_op jit(solution)/shard_map/join/pallas_call | solution.py:49
  386.7 22.0 %hidden_layer.1 = (bf16[1184,1024]{1,0:T(8,128)(2,1)S(1)}, f32[1184,1024]{1,0:T(8,128)}, f32[1184,1024]{1,0:T(8,128)}) custom-call(bf16[1184,1536]{1,0:T(8,128)(2,1)S(1)} %copy-done, bf16[1184,1536]{1,0:T(8,128)(2,1)} %collective-permute-done.10.xb_ref, bf16[3072,1024]{1,0:T(8,128)(2,1)} %get-tuple-element.66.gate_ref.wa_ref, ...), custom_call_target="tpu_custom_call" | custom-call | tf_op jit(solution)/shard_map/hidden_layer/pallas_call | solution.py:174
  410.6 96.3 %collective-permute-done.5.refs_2_ = bf16[1024,768]{1,0:T(8,128)(2,1)S(1)} collective-permute-done((bf16[1024,768]{1,0:T(8,128)(2,1)}, bf16[1024,768]{1,0:T(8,128)(2,1)S(1)}, u32[]{:S(2)}, u32[]{:S(2)}) %collective-permute-start.5) | collective-permute-done | bytes 1572896 | tf_op jit(solution)/shard_map/ppermute | solution.py:17
  508.1 6.7 join.3.w_ref.down_ref
  514.8 8.6 %product.6 = bf16[1184,1536]{1,0:T(8,128)(2,1)} custom-call(bf16[1184,1024]{1,0:T(8,128)(2,1)} %copy-done.1, bf16[1024,3072]{1,0:T(8,128)(2,1)} %join.3.w_ref.down_ref), custom_call_target="tpu_custom_call" | custom-call | tf_op jit(solution)/shard_map/product/pallas_call | solution.py:109
  523.8 6.2 collective-permute-done.11.rest_0_
  530.0 9.2 %product.7 = bf16[1184,1536]{1,0:T(8,128)(2,1)} custom-call(bf16[1184,1024]{1,0:T(8,128)(2,1)} %copy-done.1, bf16[1024,3072]{1,0:T(8,128)(2,1)} %join.3.w_ref.down_ref, bf16[1184,1536]{1,0:T(8,128)(2,1)} %collective-permute-done.11.rest_0_), custom_call_target="tpu_custom_call" | custom-call | tf_op jit(solution)/shard_map/product/pallas_call | solution.py:109
  539.3 4.9 all-to-all-start.1
  544.2 17.6 %grads.1 = (bf16[1184,1024]{1,0:T(8,128)(2,1)}, bf16[1184,1024]{1,0:T(8,128)(2,1)}, f32[1184,128]{1,0:T(8,128)}) custom-call(bf16[1184,1536]{1,0:T(8,128)(2,1)} %bitcast.15.ga_ref, bf16[1184,1536]{1,0:T(8,128)(2,1)} %collective-permute-done.3.gb_ref, bf16[1024,3072]{1,0:T(8,128)(2,1)} %join.3.w_ref.down_ref, f32[1184,1024]{1,0:T(8,128)} %get-tuple-element.78.silu_ref, ...), custom_call_target="tpu_custom_call" | custom-call | tf_op jit(solution)/shard_map/grads/pallas_call | solution.py:215
  561.8 8.1 %pair_product.6 = bf16[1184,768]{1,0:T(8,128)(2,1)} custom-call(bf16[1184,1024]{1,0:T(8,128)(2,1)} %get-tuple-element.80.a_ref, bf16[1184,1024]{1,0:T(8,128)(2,1)} %get-tuple-element.81.b_ref, bf16[3072,1024]{1,0:T(8,128)(2,1)} %get-tuple-element.66.gate_ref.wa_ref, bf16[3072,1024]{1,0:T(8,128)(2,1)} %get-tuple-element.67.up_ref.wb_ref), custom_call_target="tpu_custom_call" | custom-call | tf_op jit(solution)/shard_map/pair_product/pallas_call | solution.py:141
  570.1 8.1 %pair_product.4 = bf16[1184,768]{1,0:T(8,128)(2,1)} custom-call(bf16[1184,1024]{1,0:T(8,128)(2,1)} %get-tuple-element.80.a_ref, bf16[1184,1024]{1,0:T(8,128)(2,1)} %get-tuple-element.81.b_ref, bf16[3072,1024]{1,0:T(8,128)(2,1)} %get-tuple-element.66.gate_ref.wa_ref, bf16[3072,1024]{1,0:T(8,128)(2,1)} %get-tuple-element.67.up_ref.wb_ref), custom_call_target="tpu_custom_call" | custom-call | tf_op jit(solution)/shard_map/pair_product/pallas_call | solution.py:141
  582.1 8.7 %pair_product.7 = bf16[1184,768]{1,0:T(8,128)(2,1)} custom-call(bf16[1184,1024]{1,0:T(8,128)(2,1)} %get-tuple-element.80.a_ref, bf16[1184,1024]{1,0:T(8,128)(2,1)} %get-tuple-element.81.b_ref, bf16[3072,1024]{1,0:T(8,128)(2,1)} %get-tuple-element.66.gate_ref.wa_ref, bf16[3072,1024]{1,0:T(8,128)(2,1)} %get-tuple-element.67.up_ref.wb_ref, ...), custom_call_target="tpu_custom_call" | custom-call | tf_op jit(solution)/shard_map/pair_product/pallas_call | solution.py:141
  593.6 8.5 %pair_product.5 = bf16[1184,768]{1,0:T(8,128)(2,1)} custom-call(bf16[1184,1024]{1,0:T(8,128)(2,1)} %get-tuple-element.80.a_ref, bf16[1184,1024]{1,0:T(8,128)(2,1)} %get-tuple-element.81.b_ref, bf16[3072,1024]{1,0:T(8,128)(2,1)} %get-tuple-element.66.gate_ref.wa_ref, bf16[3072,1024]{1,0:T(8,128)(2,1)} %get-tuple-element.67.up_ref.wb_ref, ...), custom_call_target="tpu_custom_call" | custom-call | tf_op jit(solution)/shard_map/pair_product/pallas_call | solution.py:141
  606.7 5.9 fusion.24
  612.6 15.9 %all-to-all-done.2 = bf16[4,296,768]{2,1,0:T(8,128)(2,1)S(1)} async-done(((bf16[4,296,768]{2,1,0:T(8,128)(2,1)}), bf16[4,296,768]{2,1,0:T(8,128)(2,1)S(1)}, u32[]{:S(2)}, u32[]{:S(2)}) %all-to-all-start.2) | async-done | bytes 1818656 | tf_op jit(solution)/shard_map/all_to_all | solution.py:298
  633.6 6.4 fusion
  648.7 16.7 %collective-permute-done.15 = bf16[128,768]{1,0:T(8,128)(2,1)S(1)} collective-permute-done((bf16[128,768]{1,0:T(8,128)(2,1)S(1)}, bf16[128,768]{1,0:T(8,128)(2,1)S(1)}, u32[]{:S(2)}, u32[]{:S(2)}) %collective-permute-start.15) | collective-permute-done | bytes 196640 | tf_op jit(solution)/shard_map/ppermute | solution.py:17
  665.4 6.9 collective-permute-done.16
  673.8 13.4 %collective-permute-start.21 = (f32[128,2]{0,1:T(2,128)S(1)}, f32[128,2]{0,1:T(2,128)S(1)}, u32[]{:S(2)}, u32[]{:S(2)}) collective-permute-start(f32[128,2]{0,1:T(2,128)S(1)} %get-tuple-element.109), channel_id=1, source_target_pairs={{0,1},{1,0},{2,3},{3,2},{4,5},{5,4},{6,7},{7,6},{8,9},{9,8},{10,11... | collective-permute-start | bytes 3080 | tf_op jit(solution)/shard_map/ppermute | solution.py:17
  700.2 5.0 collective-permute-done.19
  (114 shorter events, 80.9 us)
Async XLA Ops:
  7.2 45.5 %all-gather.3.cloned.1.call-start = ((), (), s32[]{:S(2)}) async-start(), calls=%async_computation.5 | async-start | bytes 2129920 | tf_op jit(solution)/shard_map/all_gather | solution.py:265
  10.6 236.2 %all-gather.5.cloned.1.call-start = ((), (), s32[]{:S(2)}) async-start(), calls=%async_computation.6 | async-start | bytes 1966080 | tf_op jit(solution)/shard_map/all_gather | solution.py:266
  67.9 22.2 %collective-permute-start.7 = (bf16[296,1536]{1,0:T(8,128)(2,1)}, bf16[296,1536]{1,0:T(8,128)(2,1)}, u32[]{:S(2)}, u32[]{:S(2)}) collective-permute-start(bf16[296,1536]{1,0:T(8,128)(2,1)} %constant_dynamic-slice_fusion.6), channel_id=1, source_target_pairs={{0,8},{8,0},{16,24},{24,16},{1,9},{9,1},{17,25},{25,17},{2,10},{10... | collective-permute-start | bytes 2727944 | tf_op jit(solution)/shard_map/ppermute | solution.py:17
  69.4 184.4 %collective-permute-start.2 = (bf16[1536,1024]{1,0:T(8,128)(2,1)}, bf16[1536,1024]{1,0:T(8,128)(2,1)}, u32[]{:S(2)}, u32[]{:S(2)}) collective-permute-start(bf16[1536,1024]{1,0:T(8,128)(2,1)} %gate_up_chunk.7), channel_id=1, source_target_pairs={{0,3},{1,2},{2,1},{3,0},{4,7},{5,6},{6,5},{7,4},{8,11},{9,10},{10,... | collective-permute-start | bytes 9437192 | tf_op jit(solution)/shard_map/ppermute | solution.py:17
  70.6 295.7 %collective-permute-start.1 = (bf16[1536,1024]{1,0:T(8,128)(2,1)}, bf16[1536,1024]{1,0:T(8,128)(2,1)}, u32[]{:S(2)}, u32[]{:S(2)}) collective-permute-start(bf16[1536,1024]{1,0:T(8,128)(2,1)} %gate_up_chunk.6), channel_id=1, source_target_pairs={{0,2},{1,3},{2,0},{3,1},{4,6},{5,7},{6,4},{7,5},{8,10},{9,11},{10,... | collective-permute-start | bytes 9437192 | tf_op jit(solution)/shard_map/ppermute | solution.py:17
  71.2 295.1 %collective-permute-start = (bf16[1536,1024]{1,0:T(8,128)(2,1)S(1)}, bf16[1536,1024]{1,0:T(8,128)(2,1)}, u32[]{:S(2)}, u32[]{:S(2)}) collective-permute-start(bf16[1536,1024]{1,0:T(8,128)(2,1)S(1)} %copy-done.2), channel_id=1, source_target_pairs={{0,1},{1,0},{2,3},{3,2},{4,5},{5,4},{6,7},{7,6},{8,9},{9,8},{10,11... | collective-permute-start | bytes 9437192 | tf_op jit(solution)/shard_map/ppermute | solution.py:17
  93.0 40.5 %collective-permute-start.8 = (bf16[296,1536]{1,0:T(8,128)(2,1)S(1)}, bf16[296,1536]{1,0:T(8,128)(2,1)S(1)}, u32[]{:S(2)}, u32[]{:S(2)}) collective-permute-start(bf16[296,1536]{1,0:T(8,128)(2,1)S(1)} %get-tuple-element.94), channel_id=1, source_target_pairs={{0,16},{8,24},{16,0},{24,8},{1,17},{9,25},{17,1},{25,9},{2,18},{10... | collective-permute-start | bytes 2727944 | tf_op jit(solution)/shard_map/ppermute | solution.py:17
  94.5 39.9 %collective-permute-start.9 = (bf16[296,1536]{1,0:T(8,128)(2,1)S(1)}, bf16[296,1536]{1,0:T(8,128)(2,1)S(1)}, u32[]{:S(2)}, u32[]{:S(2)}) collective-permute-start(bf16[296,1536]{1,0:T(8,128)(2,1)S(1)} %get-tuple-element.93), channel_id=1, source_target_pairs={{0,24},{8,16},{16,8},{24,0},{1,25},{9,17},{17,9},{25,1},{2,26},{10... | collective-permute-start | bytes 2727944 | tf_op jit(solution)/shard_map/ppermute | solution.py:17
  135.5 251.2 %collective-permute-start.10 = (bf16[1184,1536]{1,0:T(8,128)(2,1)}, bf16[1184,1536]{1,0:T(8,128)(2,1)}, u32[]{:S(2)}, u32[]{:S(2)}) collective-permute-start(bf16[1184,1536]{1,0:T(8,128)(2,1)} %constant_dynamic-update-slice_fusion.xa_ref), channel_id=1, source_target_pairs={{0,4},{4,0},{1,5},{5,1},{2,6},{6,2},{3,7},{7,3},{8,12},{12,8},{9,1... | collective-permute-start | bytes 10911752 | tf_op jit(solution)/shard_map/ppermute | solution.py:17
  366.4 157.0 %all-to-all-start = ((bf16[4,296,1536]{2,1,0:T(8,128)(2,1)}), bf16[4,296,1536]{2,1,0:T(8,128)(2,1)}, u32[]{:S(2)}, u32[]{:S(2)}) async-start(bf16[4,296,1536]{2,1,0:T(8,128)(2,1)} %bitcast.66), calls=%async_computation | async-start | bytes 7274496 | tf_op jit(solution)/shard_map/all_to_all | solution.py:298
  371.1 39.5 %collective-permute-start.6 = (bf16[1024,768]{1,0:T(8,128)(2,1)}, bf16[1024,768]{1,0:T(8,128)(2,1)S(1)}, u32[]{:S(2)}, u32[]{:S(2)}) collective-permute-start(bf16[1024,768]{1,0:T(8,128)(2,1)} %get-tuple-element.61), channel_id=1, source_target_pairs={{0,3},{1,2},{2,1},{3,0},{4,7},{5,6},{6,5},{7,4},{8,11},{9,10},{10,... | collective-permute-start | bytes 4718600 | tf_op jit(solution)/shard_map/ppermute | solution.py:17
  373.8 133.2 %collective-permute-start.5 = (bf16[1024,768]{1,0:T(8,128)(2,1)}, bf16[1024,768]{1,0:T(8,128)(2,1)S(1)}, u32[]{:S(2)}, u32[]{:S(2)}) collective-permute-start(bf16[1024,768]{1,0:T(8,128)(2,1)} %get-tuple-element.60), channel_id=1, source_target_pairs={{0,2},{1,3},{2,0},{3,1},{4,6},{5,7},{6,4},{7,5},{8,10},{9,11},{10,... | collective-permute-start | bytes 4718600 | tf_op jit(solution)/shard_map/ppermute | solution.py:17
  373.8 133.2 %collective-permute-start.4 = (bf16[1024,768]{1,0:T(8,128)(2,1)}, bf16[1024,768]{1,0:T(8,128)(2,1)}, u32[]{:S(2)}, u32[]{:S(2)}) collective-permute-start(bf16[1024,768]{1,0:T(8,128)(2,1)} %get-tuple-element.59), channel_id=1, source_target_pairs={{0,1},{1,0},{2,3},{3,2},{4,5},{5,4},{6,7},{7,6},{8,9},{9,8},{10,11... | collective-permute-start | bytes 4718600 | tf_op jit(solution)/shard_map/ppermute | solution.py:17
  410.6 96.3 %copy-start.5 = (bf16[1024,768]{1,0:T(8,128)(2,1)}, bf16[1024,768]{1,0:T(8,128)(2,1)S(1)}, u32[]{:S(2)}) copy-start(bf16[1024,768]{1,0:T(8,128)(2,1)S(1)} %collective-permute-done.6.refs_3_) | copy-start | bytes 4718596
  523.3 6.7 collective-permute-start.11
  523.3 15.9 %collective-permute-start.3 = (bf16[1184,1536]{1,0:T(8,128)(2,1)}, bf16[1184,1536]{1,0:T(8,128)(2,1)}, u32[]{:S(2)}, u32[]{:S(2)}) collective-permute-start(bf16[1184,1536]{1,0:T(8,128)(2,1)} %bitcast.15.ga_ref), channel_id=1, source_target_pairs={{0,4},{4,0},{1,5},{5,1},{2,6},{6,2},{3,7},{7,3},{8,12},{12,8},{9,1... | collective-permute-start | bytes 10911752 | tf_op jit(solution)/shard_map/ppermute | solution.py:17
  539.3 62.9 %all-to-all-start.1 = ((bf16[4,296,1536]{2,1,0:T(8,128)(2,1)}), bf16[4,296,1536]{2,1,0:T(8,128)(2,1)}, u32[]{:S(2)}, u32[]{:S(2)}) async-start(bf16[4,296,1536]{2,1,0:T(8,128)(2,1)} %bitcast.67), calls=%async_computation.1 | async-start | bytes 7274496 | tf_op jit(solution)/shard_map/all_to_all | solution.py:298
  569.9 12.2 %collective-permute-start.13 = (bf16[1184,768]{1,0:T(8,128)(2,1)}, bf16[1184,768]{1,0:T(8,128)(2,1)}, u32[]{:S(2)}, u32[]{:S(2)}) collective-permute-start(bf16[1184,768]{1,0:T(8,128)(2,1)} %pair_product.6), channel_id=1, source_target_pairs={{0,4},{4,0},{1,5},{5,1},{2,6},{6,2},{3,7},{7,3},{8,12},{12,8},{9,1... | collective-permute-start | bytes 5455880 | tf_op jit(solution)/shard_map/ppermute | solution.py:17
  578.2 14.1 %collective-permute-start.12 = (bf16[1184,768]{1,0:T(8,128)(2,1)}, bf16[1184,768]{1,0:T(8,128)(2,1)S(1)}, u32[]{:S(2)}, u32[]{:S(2)}) collective-permute-start(bf16[1184,768]{1,0:T(8,128)(2,1)} %pair_product.4), channel_id=1, source_target_pairs={{0,4},{4,0},{1,5},{5,1},{2,6},{6,2},{3,7},{7,3},{8,12},{12,8},{9,1... | collective-permute-start | bytes 5455880 | tf_op jit(solution)/shard_map/ppermute | solution.py:17
  578.8 3.2 collective-permute-start.14
  602.2 26.3 %all-to-all-start.2 = ((bf16[4,296,768]{2,1,0:T(8,128)(2,1)}), bf16[4,296,768]{2,1,0:T(8,128)(2,1)S(1)}, u32[]{:S(2)}, u32[]{:S(2)}) async-start(bf16[4,296,768]{2,1,0:T(8,128)(2,1)} %bitcast.68), calls=%async_computation.3 | async-start | bytes 3637248 | tf_op jit(solution)/shard_map/all_to_all | solution.py:298
  629.7 43.7 %all-to-all-start.3 = ((bf16[4,296,768]{2,1,0:T(8,128)(2,1)}), bf16[4,296,768]{2,1,0:T(8,128)(2,1)S(1)}, u32[]{:S(2)}, u32[]{:S(2)}) async-start(bf16[4,296,768]{2,1,0:T(8,128)(2,1)} %bitcast.22), calls=%async_computation.4 | async-start | bytes 3637248 | tf_op jit(solution)/shard_map/all_to_all | solution.py:298
  633.3 72.7 %reduce-scatter.2.cloned.1.call-start = ((), (), s32[]{:S(2)}) async-start(), calls=%async_computation.7 | async-start | bytes 1966080 | tf_op jit(solution)/shard_map/reduce_scatter | solution.py:387
  644.3 21.1 %collective-permute-start.15 = (bf16[128,768]{1,0:T(8,128)(2,1)S(1)}, bf16[128,768]{1,0:T(8,128)(2,1)S(1)}, u32[]{:S(2)}, u32[]{:S(2)}) collective-permute-start(bf16[128,768]{1,0:T(8,128)(2,1)S(1)} %get-tuple-element.96), channel_id=1, source_target_pairs={{0,1},{1,0},{2,3},{3,2},{4,5},{5,4},{6,7},{7,6},{8,9},{9,8},{10,11... | collective-permute-start | bytes 589832 | tf_op jit(solution)/shard_map/ppermute | solution.py:17
  644.4 27.9 %collective-permute-start.16 = (bf16[128,768]{1,0:T(8,128)(2,1)S(1)}, bf16[128,768]{1,0:T(8,128)(2,1)S(1)}, u32[]{:S(2)}, u32[]{:S(2)}) collective-permute-start(bf16[128,768]{1,0:T(8,128)(2,1)S(1)} %get-tuple-element.98), channel_id=1, source_target_pairs={{0,2},{1,3},{2,0},{3,1},{4,6},{5,7},{6,4},{7,5},{8,10},{9,11},{10,... | collective-permute-start | bytes 589832 | tf_op jit(solution)/shard_map/ppermute | solution.py:17
  646.1 26.2 %collective-permute-start.17 = (bf16[128,768]{1,0:T(8,128)(2,1)S(1)}, bf16[128,768]{1,0:T(8,128)(2,1)S(1)}, u32[]{:S(2)}, u32[]{:S(2)}) collective-permute-start(bf16[128,768]{1,0:T(8,128)(2,1)S(1)} %get-tuple-element.97), channel_id=1, source_target_pairs={{0,3},{1,2},{2,1},{3,0},{4,7},{5,6},{6,5},{7,4},{8,11},{9,10},{10,... | collective-permute-start | bytes 589832 | tf_op jit(solution)/shard_map/ppermute | solution.py:17
  673.8 19.4 %collective-permute-start.21 = (f32[128,2]{0,1:T(2,128)S(1)}, f32[128,2]{0,1:T(2,128)S(1)}, u32[]{:S(2)}, u32[]{:S(2)}) collective-permute-start(f32[128,2]{0,1:T(2,128)S(1)} %get-tuple-element.109), channel_id=1, source_target_pairs={{0,1},{1,0},{2,3},{3,2},{4,5},{5,4},{6,7},{7,6},{8,9},{9,8},{10,11... | collective-permute-start | bytes 3080 | tf_op jit(solution)/shard_map/ppermute | solution.py:17
  687.2 8.3 %collective-permute-start.22 = (f32[128,2]{0,1:T(2,128)S(1)}, f32[128,2]{0,1:T(2,128)S(1)}, u32[]{:S(2)}, u32[]{:S(2)}) collective-permute-start(f32[128,2]{0,1:T(2,128)S(1)} %get-tuple-element.111), channel_id=1, source_target_pairs={{0,2},{1,3},{2,0},{3,1},{4,6},{5,7},{6,4},{7,5},{8,10},{9,11},{10,... | collective-permute-start | bytes 3080 | tf_op jit(solution)/shard_map/ppermute | solution.py:17
  687.4 8.2 %collective-permute-start.23 = (f32[128,2]{0,1:T(2,128)S(1)}, f32[128,2]{0,1:T(2,128)S(1)}, u32[]{:S(2)}, u32[]{:S(2)}) collective-permute-start(f32[128,2]{0,1:T(2,128)S(1)} %get-tuple-element.110), channel_id=1, source_target_pairs={{0,3},{1,2},{2,1},{3,0},{4,7},{5,6},{6,5},{7,4},{8,11},{9,10},{10,... | collective-permute-start | bytes 3080 | tf_op jit(solution)/shard_map/ppermute | solution.py:17
  691.1 9.1 %collective-permute-start.18 = (bf16[128,768]{1,0:T(8,128)(2,1)S(1)}, bf16[128,768]{1,0:T(8,128)(2,1)S(1)}, u32[]{:S(2)}, u32[]{:S(2)}) collective-permute-start(bf16[128,768]{1,0:T(8,128)(2,1)S(1)} %get-tuple-element.99), channel_id=1, source_target_pairs={{0,1},{1,0},{2,3},{3,2},{4,5},{5,4},{6,7},{7,6},{8,9},{9,8},{10,11... | collective-permute-start | bytes 589832 | tf_op jit(solution)/shard_map/ppermute | solution.py:17
  692.2 13.0 %collective-permute-start.19 = (bf16[128,768]{1,0:T(8,128)(2,1)S(1)}, bf16[128,768]{1,0:T(8,128)(2,1)S(1)}, u32[]{:S(2)}, u32[]{:S(2)}) collective-permute-start(bf16[128,768]{1,0:T(8,128)(2,1)S(1)} %get-tuple-element.101), channel_id=1, source_target_pairs={{0,2},{1,3},{2,0},{3,1},{4,6},{5,7},{6,4},{7,5},{8,10},{9,11},{10,... | collective-permute-start | bytes 589832 | tf_op jit(solution)/shard_map/ppermute | solution.py:17
  693.3 11.9 %collective-permute-start.20 = (bf16[128,768]{1,0:T(8,128)(2,1)S(1)}, bf16[128,768]{1,0:T(8,128)(2,1)S(1)}, u32[]{:S(2)}, u32[]{:S(2)}) collective-permute-start(bf16[128,768]{1,0:T(8,128)(2,1)S(1)} %get-tuple-element.100), channel_id=1, source_target_pairs={{0,3},{1,2},{2,1},{3,0},{4,7},{5,6},{6,5},{7,4},{8,11},{9,10},{10,... | collective-permute-start | bytes 589832 | tf_op jit(solution)/shard_map/ppermute | solution.py:17
  (8 other events, 37.9 us)
Sparse Core Ops, SparseCore 0:
  10.7 41.9 all-gather.2
  73.9 172.8 all-gather.4
  640.1 48.7 reduce-scatter.1

commit v3 on v2

--- a/solution.py
+++ b/solution.py
@@ -267,12 +267,19 @@
 
     gate_up_p = [gate_up_chunk(gate_weight[0], up_weight[0], me_d ^ s, Fc) for s in range(Z)]
     down_p = [lax.dynamic_slice_in_dim(down_weight[0], (me_d ^ s) * Fc, Fc, 0) for s in range(Z)]
-    tok_g, gate_up_p, down_p = tie(tok_g, gate_up_p, down_p)
-    shifts = list(range(2, Z)) + [1]
-    for s in shifts:
+    tok_g, gate_up_p[3:], down_p = tie(tok_g, gate_up_p[3:], down_p)
+    gate_up_p[1] = swap(gate_up_p[1], "dp", 1)
+    for s in range(2, Z):
+        if s > 2:
+            gate_up_p[s], gate_up_p[s - 1] = tie(gate_up_p[s], gate_up_p[s - 1])
         gate_up_p[s] = swap(gate_up_p[s], "dp", s)
-    for s in shifts:
-        down_p[s], gate_up_p[s] = tie(down_p[s], gate_up_p[s])
+    down_p[1], gate_up_p[1] = tie(down_p[1], gate_up_p[1])
+    down_p[1] = swap(down_p[1], "dp", 1)
+    for s in range(2, Z):
+        if s > 2:
+            down_p[s], down_p[s - 1] = tie(down_p[s], down_p[s - 1])
+        else:
+            down_p[s], gate_up_p = tie(down_p[s], gate_up_p)
         down_p[s] = swap(down_p[s], "dp", s)
 
     routing = tok_g[:, Fh:].astype(F32)
@@ -373,17 +380,17 @@
         last = lax.dynamic_update_slice(last, rows3, (0, Z * cap, 0))
         in_mine[1] = last.reshape(R, -1)
     in_mine, out_back = tie(in_mine, out_back)
+    out_tok = (combine(heavy_hi, out_back) + combine(heavy_lo, out_back)).astype(BF16)
     in_back = []
     for n, part in enumerate(in_mine):
         if n:
-            part, in_back[n - 1] = tie(part, in_back[n - 1])
+            part, in_back[n - 1], out_tok = tie(part, in_back[n - 1], out_tok)
         in_back.append(over_expert(part))
     if spare:
         dots = in_back[1].reshape(E, capr, -1)[:, Z * cap : Z * cap + 3, :capr].astype(F32)
         dots = jnp.sum(dots, axis=1)
     else:
         dots = over_expert(dots.reshape(R, 1)).reshape(E, capr)
-    out_tok = (combine(heavy_hi, out_back) + combine(heavy_lo, out_back)).astype(BF16)
     layer_output = lax.psum_scatter(out_tok, "dp", scatter_dimension=0, tiled=True)
     token_grad = [to_blocks(combine(pick, p), BF16).astype(BF16) for p in in_back]
     token_grad = jnp.concatenate(token_grad, axis=1)

time: 715 us -> 683 us (0.955)
  waiting for transfers between devices: 445 us -> 314 us
  starting transfers between devices: 56.8 us -> 157 us
    all_gather x1, waiting for transfers between devices: 110 us -> 0.01 us  [local(): cot_g = lax.all_gather(cotangent, 'dp', axis=0, tiled=True)]
    ppermute x24, starting transfers between devices: 39.2 us -> 139 us  [swap(): return lax.ppermute(value, axis, [(i, i ^ shift) for i in range(size)])]
    ppermute x24, waiting for transfers between devices: 305 us -> 209 us  [swap(): return lax.ppermute(value, axis, [(i, i ^ shift) for i in range(size)])]
    all_gather x1, waiting for transfers between devices: 14.4 us -> 92.8 us  [local(): lax.all_gather(jnp.concatenate([tokens, wide], axis=1), 'dp', axis=0, til...]
  transfers between devices with their start and end apart: 31 -> 31, of which waited for: 14 -> 14; matrix products, arithmetic and copies ran while one was open for 5% -> 6% of each run, Pallas kernels for 19% -> 21%
where the time goes in v3:
time: 683 us; the launch traced here: 681 us
  waiting for transfers between devices  314 us (46%)
  starting transfers between devices  157 us (23%)
  Pallas kernels  144 us (21%)
  local copies, waits for them, and re-layouts  25.6 us (4%)
  matrix products  14.3 us (2%)
  between operations  14 us (2%)
  other arithmetic  11.6 us (2%)
    ppermute x24, waiting for transfers between devices, swap(): return lax.ppermute(value, axis, [(i, i ^ shift) for i in range(size)])  209 us
    ppermute x24, starting transfers between devices, swap(): return lax.ppermute(value, axis, [(i, i ^ shift) for i in range(size)])  139 us
    all_gather x1, waiting for transfers between devices, local(): lax.all_gather(jnp.concatenate([tokens, wide], axis=1), 'dp', axis=0, til...  92.8 us
    pallas_call x4, Pallas kernels, pair_product(): pl.pallas_call(pair_body, grid=(steps,), in_specs=[row_spec, row_spec, co...  33.5 us
    pallas_call x4, Pallas kernels, product(): pl.pallas_call(product_body, grid=(steps,), in_specs=[pl.BlockSpec((heigh...  31.5 us
    pallas_call x4, Pallas kernels, gate_up_chunk(): pl.pallas_call(chunk_body, grid_spec=pltpu.PrefetchScalarGridSpec(num_sca...  22 us
    pallas_call x1, Pallas kernels, hidden_layer(): pl.pallas_call(hidden_body, grid=(R // height, Fc // tile), in_specs=[row...  21.9 us
    pallas_call x1, Pallas kernels, grads(): pl.pallas_call(grads_body, grid=(R // height, Fc // tile), in_specs=[pl.B...  17.5 us
  transfers between devices with their start and end apart: 31, of which 14 were waited for; matrix products, arithmetic and copies ran while one was open for 6% of the time, Pallas kernels for 21%

profile of v3, /device:TPU:0, one launch (start us, length us, event | category | flops | bytes accessed | tf_op | source)
XLA Modules:
  0.0 680.9 jit_solution(1676958725337300805)
XLA Ops:
  10.7 5.5 gate_up_chunk.7
  20.2 5.5 gate_up_chunk.6
  27.4 5.5 gate_up_chunk.4
  32.9 5.5 dynamic-slice_bitcast_fusion
  38.5 92.8 %all-gather.3.cloned.1.call-done = bf16[512,1664]{1,0:T(8,128)(2,1)} async-done(((bf16[128,1664]{1,0:T(8,128)(2,1)}), bf16[512,1664]{1,0:T(8,128)(2,1)}) %all-gather.3.cloned.1.call-update) | async-done | bytes 1703952 | tf_op jit(solution)/shard_map/all_gather | solution.py:265
  138.9 6.7 product.5
  145.5 37.9 %collective-permute-done.1.refs_2_ = bf16[1536,1024]{1,0:T(8,128)(2,1)S(1)} collective-permute-done((bf16[1536,1024]{1,0:T(8,128)(2,1)}, bf16[1536,1024]{1,0:T(8,128)(2,1)S(1)}, u32[]{:S(2)}, u32[]{:S(2)}) %collective-permute-start.1) | collective-permute-done | bytes 3145760 | tf_op jit(solution)/shard_map/ppermute | solution.py:17
  190.7 20.5 %collective-permute-done.7 = bf16[296,1536]{1,0:T(8,128)(2,1)} collective-permute-done((bf16[296,1536]{1,0:T(8,128)(2,1)}, bf16[296,1536]{1,0:T(8,128)(2,1)}, u32[]{:S(2)}, u32[]{:S(2)}) %collective-permute-start.7) | collective-permute-done | bytes 909344 | tf_op jit(solution)/shard_map/ppermute | solution.py:17
  217.0 37.4 %collective-permute-done.8 = bf16[296,1536]{1,0:T(8,128)(2,1)S(1)} collective-permute-done((bf16[296,1536]{1,0:T(8,128)(2,1)S(1)}, bf16[296,1536]{1,0:T(8,128)(2,1)S(1)}, u32[]{:S(2)}, u32[]{:S(2)}) %collective-permute-start.8) | collective-permute-done | bytes 909344 | tf_op jit(solution)/shard_map/ppermute | solution.py:17
  261.9 7.5 %collective-permute-done.2.refs_3_ = bf16[1536,1024]{1,0:T(8,128)(2,1)} collective-permute-done((bf16[1536,1024]{1,0:T(8,128)(2,1)}, bf16[1536,1024]{1,0:T(8,128)(2,1)}, u32[]{:S(2)}, u32[]{:S(2)}) %collective-permute-start.2) | collective-permute-done | bytes 3145760 | tf_op jit(solution)/shard_map/ppermute | solution.py:17
  269.4 77.6 %collective-permute-start.5 = (bf16[1024,768]{1,0:T(8,128)(2,1)}, bf16[1024,768]{1,0:T(8,128)(2,1)S(1)}, u32[]{:S(2)}, u32[]{:S(2)}) collective-permute-start(bf16[1024,768]{1,0:T(8,128)(2,1)} %get-tuple-element.64), channel_id=1, source_target_pairs={{0,2},{1,3},{2,0},{3,1},{4,6},{5,7},{6,4},{7,5},{8,10},{9,11},{10,... | collective-permute-start | bytes 4718600 | tf_op jit(solution)/shard_map/ppermute | solution.py:17
  348.6 7.0 %product.4 = bf16[1184,1536]{1,0:T(8,128)(2,1)} custom-call(bf16[1184,512]{1,0:T(8,128)(2,1)} %get-tuple-element.111.a_ref, bf16[512,1536]{1,0:T(8,128)(2,1)} %all-gather.5.cloned.1.call-done.w_ref, f32[1184,1]{1,0:T(8,128)} %broadcast_in_dim.79.rest_0_), custom_call_target="tpu_custom_call" | custom-call | tf_op jit(solution)/shard_map/product/pallas_call | solution.py:109
  360.7 54.3 %collective-permute-done.5.refs_2_ = bf16[1024,768]{1,0:T(8,128)(2,1)S(1)} collective-permute-done((bf16[1024,768]{1,0:T(8,128)(2,1)}, bf16[1024,768]{1,0:T(8,128)(2,1)S(1)}, u32[]{:S(2)}, u32[]{:S(2)}) %collective-permute-start.5) | collective-permute-done | bytes 1572896 | tf_op jit(solution)/shard_map/ppermute | solution.py:17
  417.9 10.5 %join.2 = (bf16[3072,1024]{1,0:T(8,128)(2,1)}, bf16[3072,1024]{1,0:T(8,128)(2,1)}) custom-call(s32[4]{0:T(128)} %fusion.20.at_ref, bf16[1536,1024]{1,0:T(8,128)(2,1)} %gate_up_chunk.5.refs_0_, bf16[1536,1024]{1,0:T(8,128)(2,1)} %collective-permute-done.refs_1_, bf16[1536,1024]{1,0:T(8,128)(2,1)} %copy-done.2, bf16[1536,1024]{1,0:T(8,128)(2,1)} %collective-permute-done.2.refs_3_), custom_call_target="tpu_custom_call" | custom-call | tf_op jit(solution)/shard_map/join/pallas_call | solution.py:49
  428.5 21.9 %hidden_layer.1 = (bf16[1184,1024]{1,0:T(8,128)(2,1)S(1)}, f32[1184,1024]{1,0:T(8,128)}, f32[1184,1024]{1,0:T(8,128)}) custom-call(bf16[1184,1536]{1,0:T(8,128)(2,1)S(1)} %copy-done, bf16[1184,1536]{1,0:T(8,128)(2,1)} %collective-permute-done.10.xb_ref, bf16[3072,1024]{1,0:T(8,128)(2,1)} %get-tuple-element.71.gate_ref.wa_ref, ...), custom_call_target="tpu_custom_call" | custom-call | tf_op jit(solution)/shard_map/hidden_layer/pallas_call | solution.py:174
  451.8 9.5 %collective-permute-done.4.refs_1_ = bf16[1024,768]{1,0:T(8,128)(2,1)S(1)} collective-permute-done((bf16[1024,768]{1,0:T(8,128)(2,1)}, bf16[1024,768]{1,0:T(8,128)(2,1)S(1)}, u32[]{:S(2)}, u32[]{:S(2)}) %collective-permute-start.4) | collective-permute-done | bytes 1572896 | tf_op jit(solution)/shard_map/ppermute | solution.py:17
  462.5 6.9 %join.3.w_ref.down_ref = bf16[1024,3072]{1,0:T(8,128)(2,1)} custom-call(s32[4]{0:T(128)} %fusion.20.at_ref, bf16[1024,768]{1,0:T(8,128)(2,1)} %get-tuple-element.77.refs_0_, bf16[1024,768]{1,0:T(8,128)(2,1)} %copy-done.6, bf16[1024,768]{1,0:T(8,128)(2,1)} %copy-done.5, bf16[1024,768]{1,0:T(8,128)(2,1)} %collective-permute-done.6.refs_3_), custom_call_target="tpu_custom_call" | custom-call | tf_op jit(solution)/shard_map/join/pallas_call | solution.py:49
  469.4 8.6 %product.6 = bf16[1184,1536]{1,0:T(8,128)(2,1)} custom-call(bf16[1184,1024]{1,0:T(8,128)(2,1)} %copy-done.1, bf16[1024,3072]{1,0:T(8,128)(2,1)} %join.3.w_ref.down_ref), custom_call_target="tpu_custom_call" | custom-call | tf_op jit(solution)/shard_map/product/pallas_call | solution.py:109
  478.6 6.2 collective-permute-done.11.rest_0_
  484.7 9.3 %product.7 = bf16[1184,1536]{1,0:T(8,128)(2,1)} custom-call(bf16[1184,1024]{1,0:T(8,128)(2,1)} %copy-done.1, bf16[1024,3072]{1,0:T(8,128)(2,1)} %join.3.w_ref.down_ref, bf16[1184,1536]{1,0:T(8,128)(2,1)} %collective-permute-done.11.rest_0_), custom_call_target="tpu_custom_call" | custom-call | tf_op jit(solution)/shard_map/product/pallas_call | solution.py:109
  499.0 17.5 %grads.1 = (bf16[1184,1024]{1,0:T(8,128)(2,1)}, bf16[1184,1024]{1,0:T(8,128)(2,1)}, f32[1184,128]{1,0:T(8,128)}) custom-call(bf16[1184,1536]{1,0:T(8,128)(2,1)} %bitcast.14.ga_ref, bf16[1184,1536]{1,0:T(8,128)(2,1)} %collective-permute-done.3.gb_ref, bf16[1024,3072]{1,0:T(8,128)(2,1)} %join.3.w_ref.down_ref, f32[1184,1024]{1,0:T(8,128)} %get-tuple-element.83.silu_ref, ...), custom_call_target="tpu_custom_call" | custom-call | tf_op jit(solution)/shard_map/grads/pallas_call | solution.py:215
  516.5 8.1 %pair_product.6 = bf16[1184,768]{1,0:T(8,128)(2,1)} custom-call(bf16[1184,1024]{1,0:T(8,128)(2,1)} %get-tuple-element.85.a_ref, bf16[1184,1024]{1,0:T(8,128)(2,1)} %get-tuple-element.86.b_ref, bf16[3072,1024]{1,0:T(8,128)(2,1)} %get-tuple-element.71.gate_ref.wa_ref, bf16[3072,1024]{1,0:T(8,128)(2,1)} %get-tuple-element.72.up_ref.wb_ref), custom_call_target="tpu_custom_call" | custom-call | tf_op jit(solution)/shard_map/pair_product/pallas_call | solution.py:141
  524.8 8.1 %pair_product.4 = bf16[1184,768]{1,0:T(8,128)(2,1)} custom-call(bf16[1184,1024]{1,0:T(8,128)(2,1)} %get-tuple-element.85.a_ref, bf16[1184,1024]{1,0:T(8,128)(2,1)} %get-tuple-element.86.b_ref, bf16[3072,1024]{1,0:T(8,128)(2,1)} %get-tuple-element.71.gate_ref.wa_ref, bf16[3072,1024]{1,0:T(8,128)(2,1)} %get-tuple-element.72.up_ref.wb_ref), custom_call_target="tpu_custom_call" | custom-call | tf_op jit(solution)/shard_map/pair_product/pallas_call | solution.py:141
  536.8 8.8 %pair_product.7 = bf16[1184,768]{1,0:T(8,128)(2,1)} custom-call(bf16[1184,1024]{1,0:T(8,128)(2,1)} %get-tuple-element.85.a_ref, bf16[1184,1024]{1,0:T(8,128)(2,1)} %get-tuple-element.86.b_ref, bf16[3072,1024]{1,0:T(8,128)(2,1)} %get-tuple-element.71.gate_ref.wa_ref, bf16[3072,1024]{1,0:T(8,128)(2,1)} %get-tuple-element.72.up_ref.wb_ref, ...), custom_call_target="tpu_custom_call" | custom-call | tf_op jit(solution)/shard_map/pair_product/pallas_call | solution.py:141
  548.3 8.5 %pair_product.5 = bf16[1184,768]{1,0:T(8,128)(2,1)} custom-call(bf16[1184,1024]{1,0:T(8,128)(2,1)} %get-tuple-element.85.a_ref, bf16[1184,1024]{1,0:T(8,128)(2,1)} %get-tuple-element.86.b_ref, bf16[3072,1024]{1,0:T(8,128)(2,1)} %get-tuple-element.71.gate_ref.wa_ref, bf16[3072,1024]{1,0:T(8,128)(2,1)} %get-tuple-element.72.up_ref.wb_ref, ...), custom_call_target="tpu_custom_call" | custom-call | tf_op jit(solution)/shard_map/pair_product/pallas_call | solution.py:141
  565.7 5.6 fusion
  571.3 11.9 %all-to-all-done.2 = bf16[4,296,768]{2,1,0:T(8,128)(2,1)S(1)} async-done(((bf16[4,296,768]{2,1,0:T(8,128)(2,1)}), bf16[4,296,768]{2,1,0:T(8,128)(2,1)S(1)}, u32[]{:S(2)}, u32[]{:S(2)}) %all-to-all-start.2) | async-done | bytes 1818656 | tf_op jit(solution)/shard_map/all_to_all | solution.py:305
  592.8 21.2 %collective-permute-start.15 = (bf16[128,768]{1,0:T(8,128)(2,1)S(1)}, bf16[128,768]{1,0:T(8,128)(2,1)S(1)}, u32[]{:S(2)}, u32[]{:S(2)}) collective-permute-start(bf16[128,768]{1,0:T(8,128)(2,1)S(1)} %get-tuple-element.102), channel_id=1, source_target_pairs={{0,1},{1,0},{2,3},{3,2},{4,5},{5,4},{6,7},{7,6},{8,9},{9,8},{10,11... | collective-permute-start | bytes 589832 | tf_op jit(solution)/shard_map/ppermute | solution.py:17
  616.4 8.5 %collective-permute-done.15 = bf16[128,768]{1,0:T(8,128)(2,1)S(1)} collective-permute-done((bf16[128,768]{1,0:T(8,128)(2,1)S(1)}, bf16[128,768]{1,0:T(8,128)(2,1)S(1)}, u32[]{:S(2)}, u32[]{:S(2)}) %collective-permute-start.15) | collective-permute-done | bytes 196640 | tf_op jit(solution)/shard_map/ppermute | solution.py:17
  624.9 15.6 %collective-permute-done.16 = bf16[128,768]{1,0:T(8,128)(2,1)S(1)} collective-permute-done((bf16[128,768]{1,0:T(8,128)(2,1)S(1)}, bf16[128,768]{1,0:T(8,128)(2,1)S(1)}, u32[]{:S(2)}, u32[]{:S(2)}) %collective-permute-start.16) | collective-permute-done | bytes 196640 | tf_op jit(solution)/shard_map/ppermute | solution.py:17
  642.0 13.7 %collective-permute-start.21 = (f32[128,2]{0,1:T(2,128)S(1)}, f32[128,2]{0,1:T(2,128)S(1)}, u32[]{:S(2)}, u32[]{:S(2)}) collective-permute-start(f32[128,2]{0,1:T(2,128)S(1)} %get-tuple-element.115), channel_id=1, source_target_pairs={{0,1},{1,0},{2,3},{3,2},{4,5},{5,4},{6,7},{7,6},{8,9},{9,8},{10,11... | collective-permute-start | bytes 3080 | tf_op jit(solution)/shard_map/ppermute | solution.py:17
  666.0 7.4 %collective-permute-done.19 = bf16[128,768]{1,0:T(8,128)(2,1)S(1)} collective-permute-done((bf16[128,768]{1,0:T(8,128)(2,1)S(1)}, bf16[128,768]{1,0:T(8,128)(2,1)S(1)}, u32[]{:S(2)}, u32[]{:S(2)}) %collective-permute-start.19) | collective-permute-done | bytes 196640 | tf_op jit(solution)/shard_map/ppermute | solution.py:17
  (116 shorter events, 95.2 us)
Async XLA Ops:
  7.2 124.1 %all-gather.3.cloned.1.call-start = ((), (), s32[]{:S(2)}) async-start(), calls=%async_computation.5 | async-start | bytes 2129920 | tf_op jit(solution)/shard_map/all_gather | solution.py:265
  10.6 338.0 %all-gather.5.cloned.1.call-start = ((), (), s32[]{:S(2)}) async-start(), calls=%async_computation.6 | async-start | bytes 1966080 | tf_op jit(solution)/shard_map/all_gather | solution.py:266
  16.2 167.2 %collective-permute-start.1 = (bf16[1536,1024]{1,0:T(8,128)(2,1)}, bf16[1536,1024]{1,0:T(8,128)(2,1)S(1)}, u32[]{:S(2)}, u32[]{:S(2)}) collective-permute-start(bf16[1536,1024]{1,0:T(8,128)(2,1)} %gate_up_chunk.7), channel_id=1, source_target_pairs={{0,2},{1,3},{2,0},{3,1},{4,6},{5,7},{6,4},{7,5},{8,10},{9,11},{10,... | collective-permute-start | bytes 9437192 | tf_op jit(solution)/shard_map/ppermute | solution.py:17
  25.7 236.1 %collective-permute-start = (bf16[1536,1024]{1,0:T(8,128)(2,1)}, bf16[1536,1024]{1,0:T(8,128)(2,1)}, u32[]{:S(2)}, u32[]{:S(2)}) collective-permute-start(bf16[1536,1024]{1,0:T(8,128)(2,1)} %gate_up_chunk.6), channel_id=1, source_target_pairs={{0,1},{1,0},{2,3},{3,2},{4,5},{5,4},{6,7},{7,6},{8,9},{9,8},{10,11... | collective-permute-start | bytes 9437192 | tf_op jit(solution)/shard_map/ppermute | solution.py:17
  183.4 30.7 %copy-start.2 = (bf16[1536,1024]{1,0:T(8,128)(2,1)}, bf16[1536,1024]{1,0:T(8,128)(2,1)S(1)}, u32[]{:S(2)}) copy-start(bf16[1536,1024]{1,0:T(8,128)(2,1)S(1)} %collective-permute-done.1.refs_2_) | copy-start | bytes 9437188
  183.4 85.9 %collective-permute-start.2 = (bf16[1536,1024]{1,0:T(8,128)(2,1)}, bf16[1536,1024]{1,0:T(8,128)(2,1)}, u32[]{:S(2)}, u32[]{:S(2)}) collective-permute-start(bf16[1536,1024]{1,0:T(8,128)(2,1)} %gate_up_chunk.4), channel_id=1, source_target_pairs={{0,3},{1,2},{2,1},{3,0},{4,7},{5,6},{6,5},{7,4},{8,11},{9,10},{10,... | collective-permute-start | bytes 9437192 | tf_op jit(solution)/shard_map/ppermute | solution.py:17
  189.2 22.1 %collective-permute-start.7 = (bf16[296,1536]{1,0:T(8,128)(2,1)}, bf16[296,1536]{1,0:T(8,128)(2,1)}, u32[]{:S(2)}, u32[]{:S(2)}) collective-permute-start(bf16[296,1536]{1,0:T(8,128)(2,1)} %constant_dynamic-slice_fusion.6), channel_id=1, source_target_pairs={{0,8},{8,0},{16,24},{24,16},{1,9},{9,1},{17,25},{25,17},{2,10},{10... | collective-permute-start | bytes 2727944 | tf_op jit(solution)/shard_map/ppermute | solution.py:17
  214.1 40.3 %collective-permute-start.8 = (bf16[296,1536]{1,0:T(8,128)(2,1)S(1)}, bf16[296,1536]{1,0:T(8,128)(2,1)S(1)}, u32[]{:S(2)}, u32[]{:S(2)}) collective-permute-start(bf16[296,1536]{1,0:T(8,128)(2,1)S(1)} %get-tuple-element.100), channel_id=1, source_target_pairs={{0,16},{8,24},{16,0},{24,8},{1,17},{9,25},{17,1},{25,9},{2,18},{10... | collective-permute-start | bytes 2727944 | tf_op jit(solution)/shard_map/ppermute | solution.py:17
  215.6 39.9 %collective-permute-start.9 = (bf16[296,1536]{1,0:T(8,128)(2,1)S(1)}, bf16[296,1536]{1,0:T(8,128)(2,1)S(1)}, u32[]{:S(2)}, u32[]{:S(2)}) collective-permute-start(bf16[296,1536]{1,0:T(8,128)(2,1)S(1)} %get-tuple-element.99), channel_id=1, source_target_pairs={{0,24},{8,16},{16,8},{24,0},{1,25},{9,17},{17,9},{25,1},{2,26},{10... | collective-permute-start | bytes 2727944 | tf_op jit(solution)/shard_map/ppermute | solution.py:17
  256.4 172.0 %collective-permute-start.10 = (bf16[1184,1536]{1,0:T(8,128)(2,1)}, bf16[1184,1536]{1,0:T(8,128)(2,1)}, u32[]{:S(2)}, u32[]{:S(2)}) collective-permute-start(bf16[1184,1536]{1,0:T(8,128)(2,1)} %constant_dynamic-update-slice_fusion.xa_ref), channel_id=1, source_target_pairs={{0,4},{4,0},{1,5},{5,1},{2,6},{6,2},{3,7},{7,3},{8,12},{12,8},{9,1... | collective-permute-start | bytes 10911752 | tf_op jit(solution)/shard_map/ppermute | solution.py:17
  269.4 145.7 %collective-permute-start.5 = (bf16[1024,768]{1,0:T(8,128)(2,1)}, bf16[1024,768]{1,0:T(8,128)(2,1)S(1)}, u32[]{:S(2)}, u32[]{:S(2)}) collective-permute-start(bf16[1024,768]{1,0:T(8,128)(2,1)} %get-tuple-element.64), channel_id=1, source_target_pairs={{0,2},{1,3},{2,0},{3,1},{4,6},{5,7},{6,4},{7,5},{8,10},{9,11},{10,... | collective-permute-start | bytes 4718600 | tf_op jit(solution)/shard_map/ppermute | solution.py:17
  355.5 122.5 %all-to-all-start = ((bf16[4,296,1536]{2,1,0:T(8,128)(2,1)}), bf16[4,296,1536]{2,1,0:T(8,128)(2,1)}, u32[]{:S(2)}, u32[]{:S(2)}) async-start(bf16[4,296,1536]{2,1,0:T(8,128)(2,1)} %bitcast.66), calls=%async_computation | async-start | bytes 7274496 | tf_op jit(solution)/shard_map/all_to_all | solution.py:305
  360.3 101.0 %collective-permute-start.4 = (bf16[1024,768]{1,0:T(8,128)(2,1)}, bf16[1024,768]{1,0:T(8,128)(2,1)S(1)}, u32[]{:S(2)}, u32[]{:S(2)}) collective-permute-start(bf16[1024,768]{1,0:T(8,128)(2,1)} %get-tuple-element.62), channel_id=1, source_target_pairs={{0,1},{1,0},{2,3},{3,2},{4,5},{5,4},{6,7},{7,6},{8,9},{9,8},{10,11... | collective-permute-start | bytes 4718600 | tf_op jit(solution)/shard_map/ppermute | solution.py:17
  415.0 46.3 %collective-permute-start.6 = (bf16[1024,768]{1,0:T(8,128)(2,1)}, bf16[1024,768]{1,0:T(8,128)(2,1)}, u32[]{:S(2)}, u32[]{:S(2)}) collective-permute-start(bf16[1024,768]{1,0:T(8,128)(2,1)} %get-tuple-element.66), channel_id=1, source_target_pairs={{0,3},{1,2},{2,1},{3,0},{4,7},{5,6},{6,5},{7,4},{8,11},{9,10},{10,... | collective-permute-start | bytes 4718600 | tf_op jit(solution)/shard_map/ppermute | solution.py:17
  478.0 6.7 collective-permute-start.11
  478.0 16.0 %collective-permute-start.3 = (bf16[1184,1536]{1,0:T(8,128)(2,1)}, bf16[1184,1536]{1,0:T(8,128)(2,1)}, u32[]{:S(2)}, u32[]{:S(2)}) collective-permute-start(bf16[1184,1536]{1,0:T(8,128)(2,1)} %bitcast.14.ga_ref), channel_id=1, source_target_pairs={{0,4},{4,0},{1,5},{5,1},{2,6},{6,2},{3,7},{7,3},{8,12},{12,8},{9,1... | collective-permute-start | bytes 10911752 | tf_op jit(solution)/shard_map/ppermute | solution.py:17
  494.0 62.7 %all-to-all-start.1 = ((bf16[4,296,1536]{2,1,0:T(8,128)(2,1)}), bf16[4,296,1536]{2,1,0:T(8,128)(2,1)}, u32[]{:S(2)}, u32[]{:S(2)}) async-start(bf16[4,296,1536]{2,1,0:T(8,128)(2,1)} %bitcast.67), calls=%async_computation.1 | async-start | bytes 7274496 | tf_op jit(solution)/shard_map/all_to_all | solution.py:305
  524.6 12.1 %collective-permute-start.13 = (bf16[1184,768]{1,0:T(8,128)(2,1)}, bf16[1184,768]{1,0:T(8,128)(2,1)}, u32[]{:S(2)}, u32[]{:S(2)}) collective-permute-start(bf16[1184,768]{1,0:T(8,128)(2,1)} %pair_product.6), channel_id=1, source_target_pairs={{0,4},{4,0},{1,5},{5,1},{2,6},{6,2},{3,7},{7,3},{8,12},{12,8},{9,1... | collective-permute-start | bytes 5455880 | tf_op jit(solution)/shard_map/ppermute | solution.py:17
  532.8 14.2 %collective-permute-start.12 = (bf16[1184,768]{1,0:T(8,128)(2,1)}, bf16[1184,768]{1,0:T(8,128)(2,1)S(1)}, u32[]{:S(2)}, u32[]{:S(2)}) collective-permute-start(bf16[1184,768]{1,0:T(8,128)(2,1)} %pair_product.4), channel_id=1, source_target_pairs={{0,4},{4,0},{1,5},{5,1},{2,6},{6,2},{3,7},{7,3},{8,12},{12,8},{9,1... | collective-permute-start | bytes 5455880 | tf_op jit(solution)/shard_map/ppermute | solution.py:17
  533.4 3.2 collective-permute-start.14
  556.8 26.4 %all-to-all-start.2 = ((bf16[4,296,768]{2,1,0:T(8,128)(2,1)}), bf16[4,296,768]{2,1,0:T(8,128)(2,1)S(1)}, u32[]{:S(2)}, u32[]{:S(2)}) async-start(bf16[4,296,768]{2,1,0:T(8,128)(2,1)} %bitcast.68), calls=%async_computation.2 | async-start | bytes 3637248 | tf_op jit(solution)/shard_map/all_to_all | solution.py:305
  584.4 57.2 %all-to-all-start.3 = ((bf16[4,296,768]{2,1,0:T(8,128)(2,1)}), bf16[4,296,768]{2,1,0:T(8,128)(2,1)S(1)}, u32[]{:S(2)}, u32[]{:S(2)}) async-start(bf16[4,296,768]{2,1,0:T(8,128)(2,1)} %bitcast.22), calls=%async_computation.4 | async-start | bytes 3637248 | tf_op jit(solution)/shard_map/all_to_all | solution.py:305
  588.0 86.4 %reduce-scatter.2.cloned.1.call-start = ((), (), s32[]{:S(2)}) async-start(), calls=%async_computation.7 | async-start | bytes 1966080 | tf_op jit(solution)/shard_map/reduce_scatter | solution.py:394
  592.8 32.1 %collective-permute-start.15 = (bf16[128,768]{1,0:T(8,128)(2,1)S(1)}, bf16[128,768]{1,0:T(8,128)(2,1)S(1)}, u32[]{:S(2)}, u32[]{:S(2)}) collective-permute-start(bf16[128,768]{1,0:T(8,128)(2,1)S(1)} %get-tuple-element.102), channel_id=1, source_target_pairs={{0,1},{1,0},{2,3},{3,2},{4,5},{5,4},{6,7},{7,6},{8,9},{9,8},{10,11... | collective-permute-start | bytes 589832 | tf_op jit(solution)/shard_map/ppermute | solution.py:17
  614.0 26.5 %collective-permute-start.16 = (bf16[128,768]{1,0:T(8,128)(2,1)S(1)}, bf16[128,768]{1,0:T(8,128)(2,1)S(1)}, u32[]{:S(2)}, u32[]{:S(2)}) collective-permute-start(bf16[128,768]{1,0:T(8,128)(2,1)S(1)} %get-tuple-element.104), channel_id=1, source_target_pairs={{0,2},{1,3},{2,0},{3,1},{4,6},{5,7},{6,4},{7,5},{8,10},{9,11},{10,... | collective-permute-start | bytes 589832 | tf_op jit(solution)/shard_map/ppermute | solution.py:17
  614.2 26.3 %collective-permute-start.17 = (bf16[128,768]{1,0:T(8,128)(2,1)S(1)}, bf16[128,768]{1,0:T(8,128)(2,1)S(1)}, u32[]{:S(2)}, u32[]{:S(2)}) collective-permute-start(bf16[128,768]{1,0:T(8,128)(2,1)S(1)} %get-tuple-element.103), channel_id=1, source_target_pairs={{0,3},{1,2},{2,1},{3,0},{4,7},{5,6},{6,5},{7,4},{8,11},{9,10},{10,... | collective-permute-start | bytes 589832 | tf_op jit(solution)/shard_map/ppermute | solution.py:17
  642.0 19.6 %collective-permute-start.21 = (f32[128,2]{0,1:T(2,128)S(1)}, f32[128,2]{0,1:T(2,128)S(1)}, u32[]{:S(2)}, u32[]{:S(2)}) collective-permute-start(f32[128,2]{0,1:T(2,128)S(1)} %get-tuple-element.115), channel_id=1, source_target_pairs={{0,1},{1,0},{2,3},{3,2},{4,5},{5,4},{6,7},{7,6},{8,9},{9,8},{10,11... | collective-permute-start | bytes 3080 | tf_op jit(solution)/shard_map/ppermute | solution.py:17
  655.7 8.3 %collective-permute-start.22 = (f32[128,2]{0,1:T(2,128)S(1)}, f32[128,2]{0,1:T(2,128)S(1)}, u32[]{:S(2)}, u32[]{:S(2)}) collective-permute-start(f32[128,2]{0,1:T(2,128)S(1)} %get-tuple-element.117), channel_id=1, source_target_pairs={{0,2},{1,3},{2,0},{3,1},{4,6},{5,7},{6,4},{7,5},{8,10},{9,11},{10,... | collective-permute-start | bytes 3080 | tf_op jit(solution)/shard_map/ppermute | solution.py:17
  655.7 8.3 %collective-permute-start.23 = (f32[128,2]{0,1:T(2,128)S(1)}, f32[128,2]{0,1:T(2,128)S(1)}, u32[]{:S(2)}, u32[]{:S(2)}) collective-permute-start(f32[128,2]{0,1:T(2,128)S(1)} %get-tuple-element.116), channel_id=1, source_target_pairs={{0,3},{1,2},{2,1},{3,0},{4,7},{5,6},{6,5},{7,4},{8,11},{9,10},{10,... | collective-permute-start | bytes 3080 | tf_op jit(solution)/shard_map/ppermute | solution.py:17
  659.6 6.4 collective-permute-start.18
  660.7 12.7 %collective-permute-start.19 = (bf16[128,768]{1,0:T(8,128)(2,1)S(1)}, bf16[128,768]{1,0:T(8,128)(2,1)S(1)}, u32[]{:S(2)}, u32[]{:S(2)}) collective-permute-start(bf16[128,768]{1,0:T(8,128)(2,1)S(1)} %get-tuple-element.107), channel_id=1, source_target_pairs={{0,2},{1,3},{2,0},{3,1},{4,6},{5,7},{6,4},{7,5},{8,10},{9,11},{10,... | collective-permute-start | bytes 589832 | tf_op jit(solution)/shard_map/ppermute | solution.py:17
  661.6 11.8 %collective-permute-start.20 = (bf16[128,768]{1,0:T(8,128)(2,1)S(1)}, bf16[128,768]{1,0:T(8,128)(2,1)S(1)}, u32[]{:S(2)}, u32[]{:S(2)}) collective-permute-start(bf16[128,768]{1,0:T(8,128)(2,1)S(1)} %get-tuple-element.106), channel_id=1, source_target_pairs={{0,3},{1,2},{2,1},{3,0},{4,7},{5,6},{6,5},{7,4},{8,11},{9,10},{10,... | collective-permute-start | bytes 589832 | tf_op jit(solution)/shard_map/ppermute | solution.py:17
  (9 other events, 44.3 us)
Sparse Core Ops, SparseCore 0:
  10.7 120.4 all-gather.2
  190.8 103.0 all-gather.4
  591.7 70.2 reduce-scatter.1

commit v4 on v3

--- a/solution.py
+++ b/solution.py
@@ -379,7 +379,7 @@
         last = in_mine[1].reshape(E, capr, -1)
         last = lax.dynamic_update_slice(last, rows3, (0, Z * cap, 0))
         in_mine[1] = last.reshape(R, -1)
-    in_mine, out_back = tie(in_mine, out_back)
+    in_mine[0], out_back = tie(in_mine[0], out_back)
     out_tok = (combine(heavy_hi, out_back) + combine(heavy_lo, out_back)).astype(BF16)
     in_back = []
     for n, part in enumerate(in_mine):

time: 683 us -> 672 us (0.984)
  waiting for transfers between devices: 314 us -> 302 us
    all_to_all x4, waiting for transfers between devices: 11.9 us -> 1.15 us  [over_expert(): return lax.all_to_all(rows, 'expert', 0, 0, tiled=True).reshape(R, -1)]
  transfers between devices with their start and end apart: 31 -> 31, of which waited for: 14 -> 14; matrix products, arithmetic and copies ran while one was open for 6% -> 6% of each run, Pallas kernels for 21% -> 22%
where the time goes in v4:
time: 672 us; the launch traced here: 670 us
  waiting for transfers between devices  302 us (45%)
  starting transfers between devices  158 us (24%)
  Pallas kernels  144 us (21%)
  local copies, waits for them, and re-layouts  24.4 us (4%)
  matrix products  14.6 us (2%)
  between operations  14.1 us (2%)
  other arithmetic  12.7 us (2%)
    ppermute x24, waiting for transfers between devices, swap(): return lax.ppermute(value, axis, [(i, i ^ shift) for i in range(size)])  208 us
    ppermute x24, starting transfers between devices, swap(): return lax.ppermute(value, axis, [(i, i ^ shift) for i in range(size)])  140 us
    all_gather x1, waiting for transfers between devices, local(): lax.all_gather(jnp.concatenate([tokens, wide], axis=1), 'dp', axis=0, til...  92.7 us
    pallas_call x4, Pallas kernels, pair_product(): pl.pallas_call(pair_body, grid=(steps,), in_specs=[row_spec, row_spec, co...  33.5 us
    pallas_call x4, Pallas kernels, product(): pl.pallas_call(product_body, grid=(steps,), in_specs=[pl.BlockSpec((heigh...  31.7 us
    pallas_call x4, Pallas kernels, gate_up_chunk(): pl.pallas_call(chunk_body, grid_spec=pltpu.PrefetchScalarGridSpec(num_sca...  22 us
    pallas_call x1, Pallas kernels, hidden_layer(): pl.pallas_call(hidden_body, grid=(R // height, Fc // tile), in_specs=[row...  22 us
    all_to_all x4, starting transfers between devices, over_expert(): return lax.all_to_all(rows, 'expert', 0, 0, tiled=True).reshape(R, -1)  17.8 us
  transfers between devices with their start and end apart: 31, of which 14 were waited for; matrix products, arithmetic and copies ran while one was open for 6% of the time, Pallas kernels for 22%

profile of v4, /device:TPU:0, one launch (start us, length us, event | category | flops | bytes accessed | tf_op | source)
XLA Modules:
  0.0 669.8 jit_solution(4685099433199335850)
XLA Ops:
  10.7 5.5 gate_up_chunk.7
  20.3 5.5 gate_up_chunk.6
  27.4 5.5 gate_up_chunk.4
  33.0 5.5 dynamic-slice_bitcast_fusion
  38.5 92.7 %all-gather.3.cloned.1.call-done = bf16[512,1664]{1,0:T(8,128)(2,1)} async-done(((bf16[128,1664]{1,0:T(8,128)(2,1)}), bf16[512,1664]{1,0:T(8,128)(2,1)}) %all-gather.3.cloned.1.call-update) | async-done | bytes 1703952 | tf_op jit(solution)/shard_map/all_gather | solution.py:265
  138.9 6.7 %product.5 = bf16[1184,1536]{1,0:T(8,128)(2,1)} custom-call(bf16[1184,512]{1,0:T(8,128)(2,1)} %get-tuple-element.109.a_ref, bf16[512,1536]{1,0:T(8,128)(2,1)} %slice.26.w_ref), custom_call_target="tpu_custom_call" | custom-call | tf_op jit(solution)/shard_map/product/pallas_call | solution.py:109
  145.6 37.9 %collective-permute-done.1.refs_2_ = bf16[1536,1024]{1,0:T(8,128)(2,1)S(1)} collective-permute-done((bf16[1536,1024]{1,0:T(8,128)(2,1)}, bf16[1536,1024]{1,0:T(8,128)(2,1)S(1)}, u32[]{:S(2)}, u32[]{:S(2)}) %collective-permute-start.1) | collective-permute-done | bytes 3145760 | tf_op jit(solution)/shard_map/ppermute | solution.py:17
  190.7 20.5 %collective-permute-done.7 = bf16[296,1536]{1,0:T(8,128)(2,1)} collective-permute-done((bf16[296,1536]{1,0:T(8,128)(2,1)}, bf16[296,1536]{1,0:T(8,128)(2,1)}, u32[]{:S(2)}, u32[]{:S(2)}) %collective-permute-start.7) | collective-permute-done | bytes 909344 | tf_op jit(solution)/shard_map/ppermute | solution.py:17
  217.1 37.4 %collective-permute-done.8 = bf16[296,1536]{1,0:T(8,128)(2,1)S(1)} collective-permute-done((bf16[296,1536]{1,0:T(8,128)(2,1)S(1)}, bf16[296,1536]{1,0:T(8,128)(2,1)S(1)}, u32[]{:S(2)}, u32[]{:S(2)}) %collective-permute-start.8) | collective-permute-done | bytes 909344 | tf_op jit(solution)/shard_map/ppermute | solution.py:17
  256.5 5.4 gate_up_chunk.5.refs_0_
  261.9 7.5 %collective-permute-done.2.refs_3_ = bf16[1536,1024]{1,0:T(8,128)(2,1)} collective-permute-done((bf16[1536,1024]{1,0:T(8,128)(2,1)}, bf16[1536,1024]{1,0:T(8,128)(2,1)}, u32[]{:S(2)}, u32[]{:S(2)}) %collective-permute-start.2) | collective-permute-done | bytes 3145760 | tf_op jit(solution)/shard_map/ppermute | solution.py:17
  269.4 77.6 %collective-permute-start.5 = (bf16[1024,768]{1,0:T(8,128)(2,1)}, bf16[1024,768]{1,0:T(8,128)(2,1)S(1)}, u32[]{:S(2)}, u32[]{:S(2)}) collective-permute-start(bf16[1024,768]{1,0:T(8,128)(2,1)} %get-tuple-element.63), channel_id=1, source_target_pairs={{0,2},{1,3},{2,0},{3,1},{4,6},{5,7},{6,4},{7,5},{8,10},{9,11},{10,... | collective-permute-start | bytes 4718600 | tf_op jit(solution)/shard_map/ppermute | solution.py:17
  348.6 6.9 %product.4 = bf16[1184,1536]{1,0:T(8,128)(2,1)} custom-call(bf16[1184,512]{1,0:T(8,128)(2,1)} %get-tuple-element.109.a_ref, bf16[512,1536]{1,0:T(8,128)(2,1)} %all-gather.5.cloned.1.call-done.w_ref, f32[1184,1]{1,0:T(8,128)} %broadcast_in_dim.79.rest_0_), custom_call_target="tpu_custom_call" | custom-call | tf_op jit(solution)/shard_map/product/pallas_call | solution.py:109
  360.7 54.4 %collective-permute-done.5.refs_2_ = bf16[1024,768]{1,0:T(8,128)(2,1)S(1)} collective-permute-done((bf16[1024,768]{1,0:T(8,128)(2,1)}, bf16[1024,768]{1,0:T(8,128)(2,1)S(1)}, u32[]{:S(2)}, u32[]{:S(2)}) %collective-permute-start.5) | collective-permute-done | bytes 1572896 | tf_op jit(solution)/shard_map/ppermute | solution.py:17
  418.0 10.5 %join.2 = (bf16[3072,1024]{1,0:T(8,128)(2,1)}, bf16[3072,1024]{1,0:T(8,128)(2,1)}) custom-call(s32[4]{0:T(128)} %fusion.20.at_ref, bf16[1536,1024]{1,0:T(8,128)(2,1)} %gate_up_chunk.5.refs_0_, bf16[1536,1024]{1,0:T(8,128)(2,1)} %collective-permute-done.refs_1_, bf16[1536,1024]{1,0:T(8,128)(2,1)} %copy-done.2, bf16[1536,1024]{1,0:T(8,128)(2,1)} %collective-permute-done.2.refs_3_), custom_call_target="tpu_custom_call" | custom-call | tf_op jit(solution)/shard_map/join/pallas_call | solution.py:49
  428.5 22.0 %hidden_layer.1 = (bf16[1184,1024]{1,0:T(8,128)(2,1)S(1)}, f32[1184,1024]{1,0:T(8,128)}, f32[1184,1024]{1,0:T(8,128)}) custom-call(bf16[1184,1536]{1,0:T(8,128)(2,1)S(1)} %copy-done, bf16[1184,1536]{1,0:T(8,128)(2,1)} %collective-permute-done.10.xb_ref, bf16[3072,1024]{1,0:T(8,128)(2,1)} %get-tuple-element.70.gate_ref.wa_ref, ...), custom_call_target="tpu_custom_call" | custom-call | tf_op jit(solution)/shard_map/hidden_layer/pallas_call | solution.py:174
  451.9 9.4 %collective-permute-done.4.refs_1_ = bf16[1024,768]{1,0:T(8,128)(2,1)S(1)} collective-permute-done((bf16[1024,768]{1,0:T(8,128)(2,1)}, bf16[1024,768]{1,0:T(8,128)(2,1)S(1)}, u32[]{:S(2)}, u32[]{:S(2)}) %collective-permute-start.4) | collective-permute-done | bytes 1572896 | tf_op jit(solution)/shard_map/ppermute | solution.py:17
  462.5 6.7 %join.3.w_ref.down_ref = bf16[1024,3072]{1,0:T(8,128)(2,1)} custom-call(s32[4]{0:T(128)} %fusion.20.at_ref, bf16[1024,768]{1,0:T(8,128)(2,1)} %get-tuple-element.76.refs_0_, bf16[1024,768]{1,0:T(8,128)(2,1)} %copy-done.5, bf16[1024,768]{1,0:T(8,128)(2,1)} %copy-done.4, bf16[1024,768]{1,0:T(8,128)(2,1)} %collective-permute-done.6.refs_3_), custom_call_target="tpu_custom_call" | custom-call | tf_op jit(solution)/shard_map/join/pallas_call | solution.py:49
  469.2 8.7 %product.6 = bf16[1184,1536]{1,0:T(8,128)(2,1)} custom-call(bf16[1184,1024]{1,0:T(8,128)(2,1)} %copy-done.1, bf16[1024,3072]{1,0:T(8,128)(2,1)} %join.3.w_ref.down_ref), custom_call_target="tpu_custom_call" | custom-call | tf_op jit(solution)/shard_map/product/pallas_call | solution.py:109
  478.4 6.2 collective-permute-done.11.rest_0_
  484.6 9.3 %product.7 = bf16[1184,1536]{1,0:T(8,128)(2,1)} custom-call(bf16[1184,1024]{1,0:T(8,128)(2,1)} %copy-done.1, bf16[1024,3072]{1,0:T(8,128)(2,1)} %join.3.w_ref.down_ref, bf16[1184,1536]{1,0:T(8,128)(2,1)} %collective-permute-done.11.rest_0_), custom_call_target="tpu_custom_call" | custom-call | tf_op jit(solution)/shard_map/product/pallas_call | solution.py:109
  498.9 17.6 %grads.1 = (bf16[1184,1024]{1,0:T(8,128)(2,1)}, bf16[1184,1024]{1,0:T(8,128)(2,1)}, f32[1184,128]{1,0:T(8,128)}) custom-call(bf16[1184,1536]{1,0:T(8,128)(2,1)} %bitcast.14.ga_ref, bf16[1184,1536]{1,0:T(8,128)(2,1)} %collective-permute-done.3.gb_ref, bf16[1024,3072]{1,0:T(8,128)(2,1)} %join.3.w_ref.down_ref, f32[1184,1024]{1,0:T(8,128)} %get-tuple-element.82.silu_ref, ...), custom_call_target="tpu_custom_call" | custom-call | tf_op jit(solution)/shard_map/grads/pallas_call | solution.py:215
  516.5 8.1 %pair_product.6 = bf16[1184,768]{1,0:T(8,128)(2,1)} custom-call(bf16[1184,1024]{1,0:T(8,128)(2,1)} %get-tuple-element.84.a_ref, bf16[1184,1024]{1,0:T(8,128)(2,1)} %get-tuple-element.85.b_ref, bf16[3072,1024]{1,0:T(8,128)(2,1)} %get-tuple-element.70.gate_ref.wa_ref, bf16[3072,1024]{1,0:T(8,128)(2,1)} %get-tuple-element.71.up_ref.wb_ref), custom_call_target="tpu_custom_call" | custom-call | tf_op jit(solution)/shard_map/pair_product/pallas_call | solution.py:141
  524.7 8.1 %pair_product.4 = bf16[1184,768]{1,0:T(8,128)(2,1)} custom-call(bf16[1184,1024]{1,0:T(8,128)(2,1)} %get-tuple-element.84.a_ref, bf16[1184,1024]{1,0:T(8,128)(2,1)} %get-tuple-element.85.b_ref, bf16[3072,1024]{1,0:T(8,128)(2,1)} %get-tuple-element.70.gate_ref.wa_ref, bf16[3072,1024]{1,0:T(8,128)(2,1)} %get-tuple-element.71.up_ref.wb_ref), custom_call_target="tpu_custom_call" | custom-call | tf_op jit(solution)/shard_map/pair_product/pallas_call | solution.py:141
  536.7 8.6 %pair_product.7 = bf16[1184,768]{1,0:T(8,128)(2,1)} custom-call(bf16[1184,1024]{1,0:T(8,128)(2,1)} %get-tuple-element.84.a_ref, bf16[1184,1024]{1,0:T(8,128)(2,1)} %get-tuple-element.85.b_ref, bf16[3072,1024]{1,0:T(8,128)(2,1)} %get-tuple-element.70.gate_ref.wa_ref, bf16[3072,1024]{1,0:T(8,128)(2,1)} %get-tuple-element.71.up_ref.wb_ref, ...), custom_call_target="tpu_custom_call" | custom-call | tf_op jit(solution)/shard_map/pair_product/pallas_call | solution.py:141
  551.0 8.7 %pair_product.5 = bf16[1184,768]{1,0:T(8,128)(2,1)} custom-call(bf16[1184,1024]{1,0:T(8,128)(2,1)} %get-tuple-element.84.a_ref, bf16[1184,1024]{1,0:T(8,128)(2,1)} %get-tuple-element.85.b_ref, bf16[3072,1024]{1,0:T(8,128)(2,1)} %get-tuple-element.70.gate_ref.wa_ref, bf16[3072,1024]{1,0:T(8,128)(2,1)} %get-tuple-element.71.up_ref.wb_ref, ...), custom_call_target="tpu_custom_call" | custom-call | tf_op jit(solution)/shard_map/pair_product/pallas_call | solution.py:141
  565.9 5.5 fusion
  581.1 21.3 %collective-permute-start.15 = (bf16[128,768]{1,0:T(8,128)(2,1)S(1)}, bf16[128,768]{1,0:T(8,128)(2,1)S(1)}, u32[]{:S(2)}, u32[]{:S(2)}) collective-permute-start(bf16[128,768]{1,0:T(8,128)(2,1)S(1)} %get-tuple-element.100), channel_id=1, source_target_pairs={{0,1},{1,0},{2,3},{3,2},{4,5},{5,4},{6,7},{7,6},{8,9},{9,8},{10,11... | collective-permute-start | bytes 589832 | tf_op jit(solution)/shard_map/ppermute | solution.py:17
  604.9 9.4 %collective-permute-done.15 = bf16[128,768]{1,0:T(8,128)(2,1)S(1)} collective-permute-done((bf16[128,768]{1,0:T(8,128)(2,1)S(1)}, bf16[128,768]{1,0:T(8,128)(2,1)S(1)}, u32[]{:S(2)}, u32[]{:S(2)}) %collective-permute-start.15) | collective-permute-done | bytes 196640 | tf_op jit(solution)/shard_map/ppermute | solution.py:17
  614.3 14.8 %collective-permute-done.16 = bf16[128,768]{1,0:T(8,128)(2,1)S(1)} collective-permute-done((bf16[128,768]{1,0:T(8,128)(2,1)S(1)}, bf16[128,768]{1,0:T(8,128)(2,1)S(1)}, u32[]{:S(2)}, u32[]{:S(2)}) %collective-permute-start.16) | collective-permute-done | bytes 196640 | tf_op jit(solution)/shard_map/ppermute | solution.py:17
  630.7 13.8 %collective-permute-start.21 = (f32[128,2]{0,1:T(2,128)S(1)}, f32[128,2]{0,1:T(2,128)S(1)}, u32[]{:S(2)}, u32[]{:S(2)}) collective-permute-start(f32[128,2]{0,1:T(2,128)S(1)} %get-tuple-element.113), channel_id=1, source_target_pairs={{0,1},{1,0},{2,3},{3,2},{4,5},{5,4},{6,7},{7,6},{8,9},{9,8},{10,11... | collective-permute-start | bytes 3080 | tf_op jit(solution)/shard_map/ppermute | solution.py:17
  654.8 7.5 %collective-permute-done.19 = bf16[128,768]{1,0:T(8,128)(2,1)S(1)} collective-permute-done((bf16[128,768]{1,0:T(8,128)(2,1)S(1)}, bf16[128,768]{1,0:T(8,128)(2,1)S(1)}, u32[]{:S(2)}, u32[]{:S(2)}) %collective-permute-start.19) | collective-permute-done | bytes 196640 | tf_op jit(solution)/shard_map/ppermute | solution.py:17
  (114 shorter events, 90.1 us)
Async XLA Ops:
  7.2 124.1 %all-gather.3.cloned.1.call-start = ((), (), s32[]{:S(2)}) async-start(), calls=%async_computation.5 | async-start | bytes 2129920 | tf_op jit(solution)/shard_map/all_gather | solution.py:265
  10.6 338.0 %all-gather.5.cloned.1.call-start = ((), (), s32[]{:S(2)}) async-start(), calls=%async_computation.6 | async-start | bytes 1966080 | tf_op jit(solution)/shard_map/all_gather | solution.py:266
  16.2 167.2 %collective-permute-start.1 = (bf16[1536,1024]{1,0:T(8,128)(2,1)}, bf16[1536,1024]{1,0:T(8,128)(2,1)S(1)}, u32[]{:S(2)}, u32[]{:S(2)}) collective-permute-start(bf16[1536,1024]{1,0:T(8,128)(2,1)} %gate_up_chunk.7), channel_id=1, source_target_pairs={{0,2},{1,3},{2,0},{3,1},{4,6},{5,7},{6,4},{7,5},{8,10},{9,11},{10,... | collective-permute-start | bytes 9437192 | tf_op jit(solution)/shard_map/ppermute | solution.py:17
  25.8 236.1 %collective-permute-start = (bf16[1536,1024]{1,0:T(8,128)(2,1)}, bf16[1536,1024]{1,0:T(8,128)(2,1)}, u32[]{:S(2)}, u32[]{:S(2)}) collective-permute-start(bf16[1536,1024]{1,0:T(8,128)(2,1)} %gate_up_chunk.6), channel_id=1, source_target_pairs={{0,1},{1,0},{2,3},{3,2},{4,5},{5,4},{6,7},{7,6},{8,9},{9,8},{10,11... | collective-permute-start | bytes 9437192 | tf_op jit(solution)/shard_map/ppermute | solution.py:17
  183.5 30.7 %copy-start.2 = (bf16[1536,1024]{1,0:T(8,128)(2,1)}, bf16[1536,1024]{1,0:T(8,128)(2,1)S(1)}, u32[]{:S(2)}) copy-start(bf16[1536,1024]{1,0:T(8,128)(2,1)S(1)} %collective-permute-done.1.refs_2_) | copy-start | bytes 9437188
  183.5 85.9 %collective-permute-start.2 = (bf16[1536,1024]{1,0:T(8,128)(2,1)}, bf16[1536,1024]{1,0:T(8,128)(2,1)}, u32[]{:S(2)}, u32[]{:S(2)}) collective-permute-start(bf16[1536,1024]{1,0:T(8,128)(2,1)} %gate_up_chunk.4), channel_id=1, source_target_pairs={{0,3},{1,2},{2,1},{3,0},{4,7},{5,6},{6,5},{7,4},{8,11},{9,10},{10,... | collective-permute-start | bytes 9437192 | tf_op jit(solution)/shard_map/ppermute | solution.py:17
  189.2 22.1 %collective-permute-start.7 = (bf16[296,1536]{1,0:T(8,128)(2,1)}, bf16[296,1536]{1,0:T(8,128)(2,1)}, u32[]{:S(2)}, u32[]{:S(2)}) collective-permute-start(bf16[296,1536]{1,0:T(8,128)(2,1)} %constant_dynamic-slice_fusion.6), channel_id=1, source_target_pairs={{0,8},{8,0},{16,24},{24,16},{1,9},{9,1},{17,25},{25,17},{2,10},{10... | collective-permute-start | bytes 2727944 | tf_op jit(solution)/shard_map/ppermute | solution.py:17
  214.1 40.3 %collective-permute-start.8 = (bf16[296,1536]{1,0:T(8,128)(2,1)S(1)}, bf16[296,1536]{1,0:T(8,128)(2,1)S(1)}, u32[]{:S(2)}, u32[]{:S(2)}) collective-permute-start(bf16[296,1536]{1,0:T(8,128)(2,1)S(1)} %get-tuple-element.98), channel_id=1, source_target_pairs={{0,16},{8,24},{16,0},{24,8},{1,17},{9,25},{17,1},{25,9},{2,18},{10... | collective-permute-start | bytes 2727944 | tf_op jit(solution)/shard_map/ppermute | solution.py:17
  215.7 39.8 %collective-permute-start.9 = (bf16[296,1536]{1,0:T(8,128)(2,1)S(1)}, bf16[296,1536]{1,0:T(8,128)(2,1)S(1)}, u32[]{:S(2)}, u32[]{:S(2)}) collective-permute-start(bf16[296,1536]{1,0:T(8,128)(2,1)S(1)} %get-tuple-element.97), channel_id=1, source_target_pairs={{0,24},{8,16},{16,8},{24,0},{1,25},{9,17},{17,9},{25,1},{2,26},{10... | collective-permute-start | bytes 2727944 | tf_op jit(solution)/shard_map/ppermute | solution.py:17
  256.5 172.1 %collective-permute-start.10 = (bf16[1184,1536]{1,0:T(8,128)(2,1)}, bf16[1184,1536]{1,0:T(8,128)(2,1)}, u32[]{:S(2)}, u32[]{:S(2)}) collective-permute-start(bf16[1184,1536]{1,0:T(8,128)(2,1)} %constant_dynamic-update-slice_fusion.xa_ref), channel_id=1, source_target_pairs={{0,4},{4,0},{1,5},{5,1},{2,6},{6,2},{3,7},{7,3},{8,12},{12,8},{9,1... | collective-permute-start | bytes 10911752 | tf_op jit(solution)/shard_map/ppermute | solution.py:17
  269.4 145.7 %collective-permute-start.5 = (bf16[1024,768]{1,0:T(8,128)(2,1)}, bf16[1024,768]{1,0:T(8,128)(2,1)S(1)}, u32[]{:S(2)}, u32[]{:S(2)}) collective-permute-start(bf16[1024,768]{1,0:T(8,128)(2,1)} %get-tuple-element.63), channel_id=1, source_target_pairs={{0,2},{1,3},{2,0},{3,1},{4,6},{5,7},{6,4},{7,5},{8,10},{9,11},{10,... | collective-permute-start | bytes 4718600 | tf_op jit(solution)/shard_map/ppermute | solution.py:17
  355.5 122.4 %all-to-all-start = ((bf16[4,296,1536]{2,1,0:T(8,128)(2,1)}), bf16[4,296,1536]{2,1,0:T(8,128)(2,1)}, u32[]{:S(2)}, u32[]{:S(2)}) async-start(bf16[4,296,1536]{2,1,0:T(8,128)(2,1)} %bitcast.66), calls=%async_computation | async-start | bytes 7274496 | tf_op jit(solution)/shard_map/all_to_all | solution.py:305
  360.3 101.0 %collective-permute-start.4 = (bf16[1024,768]{1,0:T(8,128)(2,1)}, bf16[1024,768]{1,0:T(8,128)(2,1)S(1)}, u32[]{:S(2)}, u32[]{:S(2)}) collective-permute-start(bf16[1024,768]{1,0:T(8,128)(2,1)} %get-tuple-element.61), channel_id=1, source_target_pairs={{0,1},{1,0},{2,3},{3,2},{4,5},{5,4},{6,7},{7,6},{8,9},{9,8},{10,11... | collective-permute-start | bytes 4718600 | tf_op jit(solution)/shard_map/ppermute | solution.py:17
  415.1 46.3 %collective-permute-start.6 = (bf16[1024,768]{1,0:T(8,128)(2,1)}, bf16[1024,768]{1,0:T(8,128)(2,1)}, u32[]{:S(2)}, u32[]{:S(2)}) collective-permute-start(bf16[1024,768]{1,0:T(8,128)(2,1)} %get-tuple-element.65), channel_id=1, source_target_pairs={{0,3},{1,2},{2,1},{3,0},{4,7},{5,6},{6,5},{7,4},{8,11},{9,10},{10,... | collective-permute-start | bytes 4718600 | tf_op jit(solution)/shard_map/ppermute | solution.py:17
  477.9 6.7 %collective-permute-start.11 = (bf16[1184,1536]{1,0:T(8,128)(2,1)}, bf16[1184,1536]{1,0:T(8,128)(2,1)}, u32[]{:S(2)}, u32[]{:S(2)}) collective-permute-start(bf16[1184,1536]{1,0:T(8,128)(2,1)} %product.6), channel_id=1, source_target_pairs={{0,4},{4,0},{1,5},{5,1},{2,6},{6,2},{3,7},{7,3},{8,12},{12,8},{9,1... | collective-permute-start | bytes 10911752 | tf_op jit(solution)/shard_map/ppermute | solution.py:17
  477.9 16.0 %collective-permute-start.3 = (bf16[1184,1536]{1,0:T(8,128)(2,1)}, bf16[1184,1536]{1,0:T(8,128)(2,1)}, u32[]{:S(2)}, u32[]{:S(2)}) collective-permute-start(bf16[1184,1536]{1,0:T(8,128)(2,1)} %bitcast.14.ga_ref), channel_id=1, source_target_pairs={{0,4},{4,0},{1,5},{5,1},{2,6},{6,2},{3,7},{7,3},{8,12},{12,8},{9,1... | collective-permute-start | bytes 10911752 | tf_op jit(solution)/shard_map/ppermute | solution.py:17
  493.9 51.4 %all-to-all-start.1 = ((bf16[4,296,1536]{2,1,0:T(8,128)(2,1)}), bf16[4,296,1536]{2,1,0:T(8,128)(2,1)}, u32[]{:S(2)}, u32[]{:S(2)}) async-start(bf16[4,296,1536]{2,1,0:T(8,128)(2,1)} %bitcast.67), calls=%async_computation.1 | async-start | bytes 7274496 | tf_op jit(solution)/shard_map/all_to_all | solution.py:305
  524.6 12.2 %collective-permute-start.14 = (bf16[1184,768]{1,0:T(8,128)(2,1)}, bf16[1184,768]{1,0:T(8,128)(2,1)}, u32[]{:S(2)}, u32[]{:S(2)}) collective-permute-start(bf16[1184,768]{1,0:T(8,128)(2,1)} %pair_product.6), channel_id=1, source_target_pairs={{0,4},{4,0},{1,5},{5,1},{2,6},{6,2},{3,7},{7,3},{8,12},{12,8},{9,1... | collective-permute-start | bytes 5455880 | tf_op jit(solution)/shard_map/ppermute | solution.py:17
  532.9 16.9 %collective-permute-start.12 = (bf16[1184,768]{1,0:T(8,128)(2,1)}, bf16[1184,768]{1,0:T(8,128)(2,1)S(1)}, u32[]{:S(2)}, u32[]{:S(2)}) collective-permute-start(bf16[1184,768]{1,0:T(8,128)(2,1)} %pair_product.4), channel_id=1, source_target_pairs={{0,4},{4,0},{1,5},{5,1},{2,6},{6,2},{3,7},{7,3},{8,12},{12,8},{9,1... | collective-permute-start | bytes 5455880 | tf_op jit(solution)/shard_map/ppermute | solution.py:17
  533.5 3.2 collective-permute-start.13
  545.3 27.2 %all-to-all-start.2 = ((bf16[4,296,768]{2,1,0:T(8,128)(2,1)}), bf16[4,296,768]{2,1,0:T(8,128)(2,1)}, u32[]{:S(2)}, u32[]{:S(2)}) async-start(bf16[4,296,768]{2,1,0:T(8,128)(2,1)} %bitcast.68), calls=%async_computation.2 | async-start | bytes 3637248 | tf_op jit(solution)/shard_map/all_to_all | solution.py:305
  572.5 57.7 %all-to-all-start.3 = ((bf16[4,296,768]{2,1,0:T(8,128)(2,1)}), bf16[4,296,768]{2,1,0:T(8,128)(2,1)S(1)}, u32[]{:S(2)}, u32[]{:S(2)}) async-start(bf16[4,296,768]{2,1,0:T(8,128)(2,1)} %bitcast.22), calls=%async_computation.4 | async-start | bytes 3637248 | tf_op jit(solution)/shard_map/all_to_all | solution.py:305
  576.2 87.0 %reduce-scatter.2.cloned.1.call-start = ((), (), s32[]{:S(2)}) async-start(), calls=%async_computation.7 | async-start | bytes 1966080 | tf_op jit(solution)/shard_map/reduce_scatter | solution.py:394
  581.1 33.2 %collective-permute-start.15 = (bf16[128,768]{1,0:T(8,128)(2,1)S(1)}, bf16[128,768]{1,0:T(8,128)(2,1)S(1)}, u32[]{:S(2)}, u32[]{:S(2)}) collective-permute-start(bf16[128,768]{1,0:T(8,128)(2,1)S(1)} %get-tuple-element.100), channel_id=1, source_target_pairs={{0,1},{1,0},{2,3},{3,2},{4,5},{5,4},{6,7},{7,6},{8,9},{9,8},{10,11... | collective-permute-start | bytes 589832 | tf_op jit(solution)/shard_map/ppermute | solution.py:17
  602.4 26.7 %collective-permute-start.16 = (bf16[128,768]{1,0:T(8,128)(2,1)S(1)}, bf16[128,768]{1,0:T(8,128)(2,1)S(1)}, u32[]{:S(2)}, u32[]{:S(2)}) collective-permute-start(bf16[128,768]{1,0:T(8,128)(2,1)S(1)} %get-tuple-element.102), channel_id=1, source_target_pairs={{0,2},{1,3},{2,0},{3,1},{4,6},{5,7},{6,4},{7,5},{8,10},{9,11},{10,... | collective-permute-start | bytes 589832 | tf_op jit(solution)/shard_map/ppermute | solution.py:17
  602.8 26.4 %collective-permute-start.17 = (bf16[128,768]{1,0:T(8,128)(2,1)S(1)}, bf16[128,768]{1,0:T(8,128)(2,1)S(1)}, u32[]{:S(2)}, u32[]{:S(2)}) collective-permute-start(bf16[128,768]{1,0:T(8,128)(2,1)S(1)} %get-tuple-element.101), channel_id=1, source_target_pairs={{0,3},{1,2},{2,1},{3,0},{4,7},{5,6},{6,5},{7,4},{8,11},{9,10},{10,... | collective-permute-start | bytes 589832 | tf_op jit(solution)/shard_map/ppermute | solution.py:17
  630.7 19.7 %collective-permute-start.21 = (f32[128,2]{0,1:T(2,128)S(1)}, f32[128,2]{0,1:T(2,128)S(1)}, u32[]{:S(2)}, u32[]{:S(2)}) collective-permute-start(f32[128,2]{0,1:T(2,128)S(1)} %get-tuple-element.113), channel_id=1, source_target_pairs={{0,1},{1,0},{2,3},{3,2},{4,5},{5,4},{6,7},{7,6},{8,9},{9,8},{10,11... | collective-permute-start | bytes 3080 | tf_op jit(solution)/shard_map/ppermute | solution.py:17
  644.5 8.3 %collective-permute-start.22 = (f32[128,2]{0,1:T(2,128)S(1)}, f32[128,2]{0,1:T(2,128)S(1)}, u32[]{:S(2)}, u32[]{:S(2)}) collective-permute-start(f32[128,2]{0,1:T(2,128)S(1)} %get-tuple-element.115), channel_id=1, source_target_pairs={{0,2},{1,3},{2,0},{3,1},{4,6},{5,7},{6,4},{7,5},{8,10},{9,11},{10,... | collective-permute-start | bytes 3080 | tf_op jit(solution)/shard_map/ppermute | solution.py:17
  644.5 8.3 %collective-permute-start.23 = (f32[128,2]{0,1:T(2,128)S(1)}, f32[128,2]{0,1:T(2,128)S(1)}, u32[]{:S(2)}, u32[]{:S(2)}) collective-permute-start(f32[128,2]{0,1:T(2,128)S(1)} %get-tuple-element.114), channel_id=1, source_target_pairs={{0,3},{1,2},{2,1},{3,0},{4,7},{5,6},{6,5},{7,4},{8,11},{9,10},{10,... | collective-permute-start | bytes 3080 | tf_op jit(solution)/shard_map/ppermute | solution.py:17
  648.3 6.5 collective-permute-start.18
  649.4 12.9 %collective-permute-start.19 = (bf16[128,768]{1,0:T(8,128)(2,1)S(1)}, bf16[128,768]{1,0:T(8,128)(2,1)S(1)}, u32[]{:S(2)}, u32[]{:S(2)}) collective-permute-start(bf16[128,768]{1,0:T(8,128)(2,1)S(1)} %get-tuple-element.105), channel_id=1, source_target_pairs={{0,2},{1,3},{2,0},{3,1},{4,6},{5,7},{6,4},{7,5},{8,10},{9,11},{10,... | collective-permute-start | bytes 589832 | tf_op jit(solution)/shard_map/ppermute | solution.py:17
  650.4 12.0 %collective-permute-start.20 = (bf16[128,768]{1,0:T(8,128)(2,1)S(1)}, bf16[128,768]{1,0:T(8,128)(2,1)S(1)}, u32[]{:S(2)}, u32[]{:S(2)}) collective-permute-start(bf16[128,768]{1,0:T(8,128)(2,1)S(1)} %get-tuple-element.104), channel_id=1, source_target_pairs={{0,3},{1,2},{2,1},{3,0},{4,7},{5,6},{6,5},{7,4},{8,11},{9,10},{10,... | collective-permute-start | bytes 589832 | tf_op jit(solution)/shard_map/ppermute | solution.py:17
  (8 other events, 42.1 us)
Sparse Core Ops, SparseCore 0:
  10.8 120.4 all-gather.2
  190.8 102.9 all-gather.4
  580.0 70.8 reduce-scatter.1

commit v5 on v4

--- a/solution.py
+++ b/solution.py
@@ -103,7 +103,7 @@
 
 def product(a, w, first, width, extra=None, scale=None):
     height, depth = a.shape
-    tile = 256
+    tile = 512 if width % 512 == 0 else 256
     steps = width // tile
     out_spec = pl.BlockSpec((height, tile), lambda n: (0, n))
     return pl.pallas_call(

time: 672 us -> 669 us (level)
  transfers between devices with their start and end apart: 31 -> 31, of which waited for: 14 -> 14; matrix products, arithmetic and copies ran while one was open for 6% -> 6% of each run, Pallas kernels for 22% -> 21%
where the time goes in v5:
time: 669 us; the launch traced here: 668 us
  waiting for transfers between devices  303 us (45%)
  starting transfers between devices  159 us (24%)
  Pallas kernels  140 us (21%)
  local copies, waits for them, and re-layouts  24.4 us (4%)
  matrix products  14.5 us (2%)
  between operations  14.1 us (2%)
  other arithmetic  12.7 us (2%)
    ppermute x24, waiting for transfers between devices, swap(): return lax.ppermute(value, axis, [(i, i ^ shift) for i in range(size)])  209 us
    ppermute x24, starting transfers between devices, swap(): return lax.ppermute(value, axis, [(i, i ^ shift) for i in range(size)])  141 us
    all_gather x1, waiting for transfers between devices, local(): lax.all_gather(jnp.concatenate([tokens, wide], axis=1), 'dp', axis=0, til...  92.7 us
    pallas_call x4, Pallas kernels, pair_product(): pl.pallas_call(pair_body, grid=(steps,), in_specs=[row_spec, row_spec, co...  33.5 us
    pallas_call x4, Pallas kernels, product(): pl.pallas_call(product_body, grid=(steps,), in_specs=[pl.BlockSpec((heigh...  27.2 us
    pallas_call x4, Pallas kernels, gate_up_chunk(): pl.pallas_call(chunk_body, grid_spec=pltpu.PrefetchScalarGridSpec(num_sca...  22 us
    pallas_call x1, Pallas kernels, hidden_layer(): pl.pallas_call(hidden_body, grid=(R // height, Fc // tile), in_specs=[row...  22 us
    all_to_all x4, starting transfers between devices, over_expert(): return lax.all_to_all(rows, 'expert', 0, 0, tiled=True).reshape(R, -1)  17.8 us
  transfers between devices with their start and end apart: 31, of which 14 were waited for; matrix products, arithmetic and copies ran while one was open for 6% of the time, Pallas kernels for 21%

profile of v5, /device:TPU:0, one launch (start us, length us, event | category | flops | bytes accessed | tf_op | source)
XLA Modules:
  0.0 667.8 jit_solution(4257135167846226301)
XLA Ops:
  10.7 5.5 gate_up_chunk.7
  20.3 5.5 gate_up_chunk.6
  27.4 5.5 gate_up_chunk.4
  33.0 5.5 dynamic-slice_bitcast_fusion
  38.5 92.7 %all-gather.3.cloned.1.call-done = bf16[512,1664]{1,0:T(8,128)(2,1)} async-done(((bf16[128,1664]{1,0:T(8,128)(2,1)}), bf16[512,1664]{1,0:T(8,128)(2,1)}) %all-gather.3.cloned.1.call-update) | async-done | bytes 1703952 | tf_op jit(solution)/shard_map/all_gather | solution.py:265
  138.9 5.6 product.5
  144.4 39.0 %collective-permute-done.1.refs_2_ = bf16[1536,1024]{1,0:T(8,128)(2,1)S(1)} collective-permute-done((bf16[1536,1024]{1,0:T(8,128)(2,1)}, bf16[1536,1024]{1,0:T(8,128)(2,1)S(1)}, u32[]{:S(2)}, u32[]{:S(2)}) %collective-permute-start.1) | collective-permute-done | bytes 3145760 | tf_op jit(solution)/shard_map/ppermute | solution.py:17
  190.7 20.5 %collective-permute-done.7 = bf16[296,1536]{1,0:T(8,128)(2,1)} collective-permute-done((bf16[296,1536]{1,0:T(8,128)(2,1)}, bf16[296,1536]{1,0:T(8,128)(2,1)}, u32[]{:S(2)}, u32[]{:S(2)}) %collective-permute-start.7) | collective-permute-done | bytes 909344 | tf_op jit(solution)/shard_map/ppermute | solution.py:17
  217.1 37.4 %collective-permute-done.8 = bf16[296,1536]{1,0:T(8,128)(2,1)S(1)} collective-permute-done((bf16[296,1536]{1,0:T(8,128)(2,1)S(1)}, bf16[296,1536]{1,0:T(8,128)(2,1)S(1)}, u32[]{:S(2)}, u32[]{:S(2)}) %collective-permute-start.8) | collective-permute-done | bytes 909344 | tf_op jit(solution)/shard_map/ppermute | solution.py:17
  256.5 5.4 gate_up_chunk.5.refs_0_
  261.9 7.5 %collective-permute-done.2.refs_3_ = bf16[1536,1024]{1,0:T(8,128)(2,1)} collective-permute-done((bf16[1536,1024]{1,0:T(8,128)(2,1)}, bf16[1536,1024]{1,0:T(8,128)(2,1)}, u32[]{:S(2)}, u32[]{:S(2)}) %collective-permute-start.2) | collective-permute-done | bytes 3145760 | tf_op jit(solution)/shard_map/ppermute | solution.py:17
  269.4 77.6 %collective-permute-start.5 = (bf16[1024,768]{1,0:T(8,128)(2,1)}, bf16[1024,768]{1,0:T(8,128)(2,1)S(1)}, u32[]{:S(2)}, u32[]{:S(2)}) collective-permute-start(bf16[1024,768]{1,0:T(8,128)(2,1)} %get-tuple-element.63), channel_id=1, source_target_pairs={{0,2},{1,3},{2,0},{3,1},{4,6},{5,7},{6,4},{7,5},{8,10},{9,11},{10,... | collective-permute-start | bytes 4718600 | tf_op jit(solution)/shard_map/ppermute | solution.py:17
  348.6 5.7 product.4
  359.5 55.6 %collective-permute-done.5.refs_2_ = bf16[1024,768]{1,0:T(8,128)(2,1)S(1)} collective-permute-done((bf16[1024,768]{1,0:T(8,128)(2,1)}, bf16[1024,768]{1,0:T(8,128)(2,1)S(1)}, u32[]{:S(2)}, u32[]{:S(2)}) %collective-permute-start.5) | collective-permute-done | bytes 1572896 | tf_op jit(solution)/shard_map/ppermute | solution.py:17
  418.0 10.5 %join.2 = (bf16[3072,1024]{1,0:T(8,128)(2,1)}, bf16[3072,1024]{1,0:T(8,128)(2,1)}) custom-call(s32[4]{0:T(128)} %fusion.20.at_ref, bf16[1536,1024]{1,0:T(8,128)(2,1)} %gate_up_chunk.5.refs_0_, bf16[1536,1024]{1,0:T(8,128)(2,1)} %collective-permute-done.refs_1_, bf16[1536,1024]{1,0:T(8,128)(2,1)} %copy-done.2, bf16[1536,1024]{1,0:T(8,128)(2,1)} %collective-permute-done.2.refs_3_), custom_call_target="tpu_custom_call" | custom-call | tf_op jit(solution)/shard_map/join/pallas_call | solution.py:49
  428.5 22.0 %hidden_layer.1 = (bf16[1184,1024]{1,0:T(8,128)(2,1)S(1)}, f32[1184,1024]{1,0:T(8,128)}, f32[1184,1024]{1,0:T(8,128)}) custom-call(bf16[1184,1536]{1,0:T(8,128)(2,1)S(1)} %copy-done, bf16[1184,1536]{1,0:T(8,128)(2,1)} %collective-permute-done.10.xb_ref, bf16[3072,1024]{1,0:T(8,128)(2,1)} %get-tuple-element.70.gate_ref.wa_ref, ...), custom_call_target="tpu_custom_call" | custom-call | tf_op jit(solution)/shard_map/hidden_layer/pallas_call | solution.py:174
  451.9 8.2 %collective-permute-done.4.refs_1_ = bf16[1024,768]{1,0:T(8,128)(2,1)S(1)} collective-permute-done((bf16[1024,768]{1,0:T(8,128)(2,1)}, bf16[1024,768]{1,0:T(8,128)(2,1)S(1)}, u32[]{:S(2)}, u32[]{:S(2)}) %collective-permute-start.4) | collective-permute-done | bytes 1572896 | tf_op jit(solution)/shard_map/ppermute | solution.py:17
  461.2 6.7 %join.3.w_ref.down_ref = bf16[1024,3072]{1,0:T(8,128)(2,1)} custom-call(s32[4]{0:T(128)} %fusion.20.at_ref, bf16[1024,768]{1,0:T(8,128)(2,1)} %get-tuple-element.76.refs_0_, bf16[1024,768]{1,0:T(8,128)(2,1)} %copy-done.5, bf16[1024,768]{1,0:T(8,128)(2,1)} %copy-done.4, bf16[1024,768]{1,0:T(8,128)(2,1)} %collective-permute-done.6.refs_3_), custom_call_target="tpu_custom_call" | custom-call | tf_op jit(solution)/shard_map/join/pallas_call | solution.py:49
  468.0 7.6 %product.6 = bf16[1184,1536]{1,0:T(8,128)(2,1)} custom-call(bf16[1184,1024]{1,0:T(8,128)(2,1)} %copy-done.1, bf16[1024,3072]{1,0:T(8,128)(2,1)} %join.3.w_ref.down_ref), custom_call_target="tpu_custom_call" | custom-call | tf_op jit(solution)/shard_map/product/pallas_call | solution.py:109
  476.1 6.2 collective-permute-done.11.rest_0_
  482.3 8.4 %product.7 = bf16[1184,1536]{1,0:T(8,128)(2,1)} custom-call(bf16[1184,1024]{1,0:T(8,128)(2,1)} %copy-done.1, bf16[1024,3072]{1,0:T(8,128)(2,1)} %join.3.w_ref.down_ref, bf16[1184,1536]{1,0:T(8,128)(2,1)} %collective-permute-done.11.rest_0_), custom_call_target="tpu_custom_call" | custom-call | tf_op jit(solution)/shard_map/product/pallas_call | solution.py:109
  495.6 17.6 %grads.1 = (bf16[1184,1024]{1,0:T(8,128)(2,1)}, bf16[1184,1024]{1,0:T(8,128)(2,1)}, f32[1184,128]{1,0:T(8,128)}) custom-call(bf16[1184,1536]{1,0:T(8,128)(2,1)} %bitcast.14.ga_ref, bf16[1184,1536]{1,0:T(8,128)(2,1)} %collective-permute-done.3.gb_ref, bf16[1024,3072]{1,0:T(8,128)(2,1)} %join.3.w_ref.down_ref, f32[1184,1024]{1,0:T(8,128)} %get-tuple-element.82.silu_ref, ...), custom_call_target="tpu_custom_call" | custom-call | tf_op jit(solution)/shard_map/grads/pallas_call | solution.py:215
  513.2 8.1 %pair_product.6 = bf16[1184,768]{1,0:T(8,128)(2,1)} custom-call(bf16[1184,1024]{1,0:T(8,128)(2,1)} %get-tuple-element.84.a_ref, bf16[1184,1024]{1,0:T(8,128)(2,1)} %get-tuple-element.85.b_ref, bf16[3072,1024]{1,0:T(8,128)(2,1)} %get-tuple-element.70.gate_ref.wa_ref, bf16[3072,1024]{1,0:T(8,128)(2,1)} %get-tuple-element.71.up_ref.wb_ref), custom_call_target="tpu_custom_call" | custom-call | tf_op jit(solution)/shard_map/pair_product/pallas_call | solution.py:141
  521.4 8.1 %pair_product.4 = bf16[1184,768]{1,0:T(8,128)(2,1)} custom-call(bf16[1184,1024]{1,0:T(8,128)(2,1)} %get-tuple-element.84.a_ref, bf16[1184,1024]{1,0:T(8,128)(2,1)} %get-tuple-element.85.b_ref, bf16[3072,1024]{1,0:T(8,128)(2,1)} %get-tuple-element.70.gate_ref.wa_ref, bf16[3072,1024]{1,0:T(8,128)(2,1)} %get-tuple-element.71.up_ref.wb_ref), custom_call_target="tpu_custom_call" | custom-call | tf_op jit(solution)/shard_map/pair_product/pallas_call | solution.py:141
  533.5 8.6 %pair_product.7 = bf16[1184,768]{1,0:T(8,128)(2,1)} custom-call(bf16[1184,1024]{1,0:T(8,128)(2,1)} %get-tuple-element.84.a_ref, bf16[1184,1024]{1,0:T(8,128)(2,1)} %get-tuple-element.85.b_ref, bf16[3072,1024]{1,0:T(8,128)(2,1)} %get-tuple-element.70.gate_ref.wa_ref, bf16[3072,1024]{1,0:T(8,128)(2,1)} %get-tuple-element.71.up_ref.wb_ref, ...), custom_call_target="tpu_custom_call" | custom-call | tf_op jit(solution)/shard_map/pair_product/pallas_call | solution.py:141
  547.7 8.7 %pair_product.5 = bf16[1184,768]{1,0:T(8,128)(2,1)} custom-call(bf16[1184,1024]{1,0:T(8,128)(2,1)} %get-tuple-element.84.a_ref, bf16[1184,1024]{1,0:T(8,128)(2,1)} %get-tuple-element.85.b_ref, bf16[3072,1024]{1,0:T(8,128)(2,1)} %get-tuple-element.70.gate_ref.wa_ref, bf16[3072,1024]{1,0:T(8,128)(2,1)} %get-tuple-element.71.up_ref.wb_ref, ...), custom_call_target="tpu_custom_call" | custom-call | tf_op jit(solution)/shard_map/pair_product/pallas_call | solution.py:141
  562.6 5.5 fusion
  577.8 22.6 %collective-permute-start.15 = (bf16[128,768]{1,0:T(8,128)(2,1)S(1)}, bf16[128,768]{1,0:T(8,128)(2,1)S(1)}, u32[]{:S(2)}, u32[]{:S(2)}) collective-permute-start(bf16[128,768]{1,0:T(8,128)(2,1)S(1)} %get-tuple-element.100), channel_id=1, source_target_pairs={{0,1},{1,0},{2,3},{3,2},{4,5},{5,4},{6,7},{7,6},{8,9},{9,8},{10,11... | collective-permute-start | bytes 589832 | tf_op jit(solution)/shard_map/ppermute | solution.py:17
  602.9 9.4 %collective-permute-done.15 = bf16[128,768]{1,0:T(8,128)(2,1)S(1)} collective-permute-done((bf16[128,768]{1,0:T(8,128)(2,1)S(1)}, bf16[128,768]{1,0:T(8,128)(2,1)S(1)}, u32[]{:S(2)}, u32[]{:S(2)}) %collective-permute-start.15) | collective-permute-done | bytes 196640 | tf_op jit(solution)/shard_map/ppermute | solution.py:17
  612.2 14.9 %collective-permute-done.16 = bf16[128,768]{1,0:T(8,128)(2,1)S(1)} collective-permute-done((bf16[128,768]{1,0:T(8,128)(2,1)S(1)}, bf16[128,768]{1,0:T(8,128)(2,1)S(1)}, u32[]{:S(2)}, u32[]{:S(2)}) %collective-permute-start.16) | collective-permute-done | bytes 196640 | tf_op jit(solution)/shard_map/ppermute | solution.py:17
  628.7 13.8 %collective-permute-start.21 = (f32[128,2]{0,1:T(2,128)S(1)}, f32[128,2]{0,1:T(2,128)S(1)}, u32[]{:S(2)}, u32[]{:S(2)}) collective-permute-start(f32[128,2]{0,1:T(2,128)S(1)} %get-tuple-element.113), channel_id=1, source_target_pairs={{0,1},{1,0},{2,3},{3,2},{4,5},{5,4},{6,7},{7,6},{8,9},{9,8},{10,11... | collective-permute-start | bytes 3080 | tf_op jit(solution)/shard_map/ppermute | solution.py:17
  652.9 7.5 %collective-permute-done.19 = bf16[128,768]{1,0:T(8,128)(2,1)S(1)} collective-permute-done((bf16[128,768]{1,0:T(8,128)(2,1)S(1)}, bf16[128,768]{1,0:T(8,128)(2,1)S(1)}, u32[]{:S(2)}, u32[]{:S(2)}) %collective-permute-start.19) | collective-permute-done | bytes 196640 | tf_op jit(solution)/shard_map/ppermute | solution.py:17
  (114 shorter events, 90.2 us)
Async XLA Ops:
  7.2 124.1 %all-gather.3.cloned.1.call-start = ((), (), s32[]{:S(2)}) async-start(), calls=%async_computation.5 | async-start | bytes 2129920 | tf_op jit(solution)/shard_map/all_gather | solution.py:265
  10.6 338.0 %all-gather.5.cloned.1.call-start = ((), (), s32[]{:S(2)}) async-start(), calls=%async_computation.6 | async-start | bytes 1966080 | tf_op jit(solution)/shard_map/all_gather | solution.py:266
  16.2 167.2 %collective-permute-start.1 = (bf16[1536,1024]{1,0:T(8,128)(2,1)}, bf16[1536,1024]{1,0:T(8,128)(2,1)S(1)}, u32[]{:S(2)}, u32[]{:S(2)}) collective-permute-start(bf16[1536,1024]{1,0:T(8,128)(2,1)} %gate_up_chunk.7), channel_id=1, source_target_pairs={{0,2},{1,3},{2,0},{3,1},{4,6},{5,7},{6,4},{7,5},{8,10},{9,11},{10,... | collective-permute-start | bytes 9437192 | tf_op jit(solution)/shard_map/ppermute | solution.py:17
  25.8 236.1 %collective-permute-start = (bf16[1536,1024]{1,0:T(8,128)(2,1)}, bf16[1536,1024]{1,0:T(8,128)(2,1)}, u32[]{:S(2)}, u32[]{:S(2)}) collective-permute-start(bf16[1536,1024]{1,0:T(8,128)(2,1)} %gate_up_chunk.6), channel_id=1, source_target_pairs={{0,1},{1,0},{2,3},{3,2},{4,5},{5,4},{6,7},{7,6},{8,9},{9,8},{10,11... | collective-permute-start | bytes 9437192 | tf_op jit(solution)/shard_map/ppermute | solution.py:17
  183.5 30.7 %copy-start.2 = (bf16[1536,1024]{1,0:T(8,128)(2,1)}, bf16[1536,1024]{1,0:T(8,128)(2,1)S(1)}, u32[]{:S(2)}) copy-start(bf16[1536,1024]{1,0:T(8,128)(2,1)S(1)} %collective-permute-done.1.refs_2_) | copy-start | bytes 9437188
  183.5 85.9 %collective-permute-start.2 = (bf16[1536,1024]{1,0:T(8,128)(2,1)}, bf16[1536,1024]{1,0:T(8,128)(2,1)}, u32[]{:S(2)}, u32[]{:S(2)}) collective-permute-start(bf16[1536,1024]{1,0:T(8,128)(2,1)} %gate_up_chunk.4), channel_id=1, source_target_pairs={{0,3},{1,2},{2,1},{3,0},{4,7},{5,6},{6,5},{7,4},{8,11},{9,10},{10,... | collective-permute-start | bytes 9437192 | tf_op jit(solution)/shard_map/ppermute | solution.py:17
  189.2 22.1 %collective-permute-start.7 = (bf16[296,1536]{1,0:T(8,128)(2,1)}, bf16[296,1536]{1,0:T(8,128)(2,1)}, u32[]{:S(2)}, u32[]{:S(2)}) collective-permute-start(bf16[296,1536]{1,0:T(8,128)(2,1)} %constant_dynamic-slice_fusion.6), channel_id=1, source_target_pairs={{0,8},{8,0},{16,24},{24,16},{1,9},{9,1},{17,25},{25,17},{2,10},{10... | collective-permute-start | bytes 2727944 | tf_op jit(solution)/shard_map/ppermute | solution.py:17
  214.1 40.3 %collective-permute-start.8 = (bf16[296,1536]{1,0:T(8,128)(2,1)S(1)}, bf16[296,1536]{1,0:T(8,128)(2,1)S(1)}, u32[]{:S(2)}, u32[]{:S(2)}) collective-permute-start(bf16[296,1536]{1,0:T(8,128)(2,1)S(1)} %get-tuple-element.98), channel_id=1, source_target_pairs={{0,16},{8,24},{16,0},{24,8},{1,17},{9,25},{17,1},{25,9},{2,18},{10... | collective-permute-start | bytes 2727944 | tf_op jit(solution)/shard_map/ppermute | solution.py:17
  215.7 39.8 %collective-permute-start.9 = (bf16[296,1536]{1,0:T(8,128)(2,1)S(1)}, bf16[296,1536]{1,0:T(8,128)(2,1)S(1)}, u32[]{:S(2)}, u32[]{:S(2)}) collective-permute-start(bf16[296,1536]{1,0:T(8,128)(2,1)S(1)} %get-tuple-element.97), channel_id=1, source_target_pairs={{0,24},{8,16},{16,8},{24,0},{1,25},{9,17},{17,9},{25,1},{2,26},{10... | collective-permute-start | bytes 2727944 | tf_op jit(solution)/shard_map/ppermute | solution.py:17
  256.5 172.1 %collective-permute-start.10 = (bf16[1184,1536]{1,0:T(8,128)(2,1)}, bf16[1184,1536]{1,0:T(8,128)(2,1)}, u32[]{:S(2)}, u32[]{:S(2)}) collective-permute-start(bf16[1184,1536]{1,0:T(8,128)(2,1)} %constant_dynamic-update-slice_fusion.xa_ref), channel_id=1, source_target_pairs={{0,4},{4,0},{1,5},{5,1},{2,6},{6,2},{3,7},{7,3},{8,12},{12,8},{9,1... | collective-permute-start | bytes 10911752 | tf_op jit(solution)/shard_map/ppermute | solution.py:17
  269.4 145.7 %collective-permute-start.5 = (bf16[1024,768]{1,0:T(8,128)(2,1)}, bf16[1024,768]{1,0:T(8,128)(2,1)S(1)}, u32[]{:S(2)}, u32[]{:S(2)}) collective-permute-start(bf16[1024,768]{1,0:T(8,128)(2,1)} %get-tuple-element.63), channel_id=1, source_target_pairs={{0,2},{1,3},{2,0},{3,1},{4,6},{5,7},{6,4},{7,5},{8,10},{9,11},{10,... | collective-permute-start | bytes 4718600 | tf_op jit(solution)/shard_map/ppermute | solution.py:17
  354.3 121.3 %all-to-all-start = ((bf16[4,296,1536]{2,1,0:T(8,128)(2,1)}), bf16[4,296,1536]{2,1,0:T(8,128)(2,1)}, u32[]{:S(2)}, u32[]{:S(2)}) async-start(bf16[4,296,1536]{2,1,0:T(8,128)(2,1)} %bitcast.66), calls=%async_computation | async-start | bytes 7274496 | tf_op jit(solution)/shard_map/all_to_all | solution.py:305
  359.1 101.0 %collective-permute-start.4 = (bf16[1024,768]{1,0:T(8,128)(2,1)}, bf16[1024,768]{1,0:T(8,128)(2,1)S(1)}, u32[]{:S(2)}, u32[]{:S(2)}) collective-permute-start(bf16[1024,768]{1,0:T(8,128)(2,1)} %get-tuple-element.61), channel_id=1, source_target_pairs={{0,1},{1,0},{2,3},{3,2},{4,5},{5,4},{6,7},{7,6},{8,9},{9,8},{10,11... | collective-permute-start | bytes 4718600 | tf_op jit(solution)/shard_map/ppermute | solution.py:17
  415.1 45.0 %collective-permute-start.6 = (bf16[1024,768]{1,0:T(8,128)(2,1)}, bf16[1024,768]{1,0:T(8,128)(2,1)}, u32[]{:S(2)}, u32[]{:S(2)}) collective-permute-start(bf16[1024,768]{1,0:T(8,128)(2,1)} %get-tuple-element.65), channel_id=1, source_target_pairs={{0,3},{1,2},{2,1},{3,0},{4,7},{5,6},{6,5},{7,4},{8,11},{9,10},{10,... | collective-permute-start | bytes 4718600 | tf_op jit(solution)/shard_map/ppermute | solution.py:17
  475.6 6.7 %collective-permute-start.11 = (bf16[1184,1536]{1,0:T(8,128)(2,1)}, bf16[1184,1536]{1,0:T(8,128)(2,1)}, u32[]{:S(2)}, u32[]{:S(2)}) collective-permute-start(bf16[1184,1536]{1,0:T(8,128)(2,1)} %product.6), channel_id=1, source_target_pairs={{0,4},{4,0},{1,5},{5,1},{2,6},{6,2},{3,7},{7,3},{8,12},{12,8},{9,1... | collective-permute-start | bytes 10911752 | tf_op jit(solution)/shard_map/ppermute | solution.py:17
  475.6 15.1 %collective-permute-start.3 = (bf16[1184,1536]{1,0:T(8,128)(2,1)}, bf16[1184,1536]{1,0:T(8,128)(2,1)}, u32[]{:S(2)}, u32[]{:S(2)}) collective-permute-start(bf16[1184,1536]{1,0:T(8,128)(2,1)} %bitcast.14.ga_ref), channel_id=1, source_target_pairs={{0,4},{4,0},{1,5},{5,1},{2,6},{6,2},{3,7},{7,3},{8,12},{12,8},{9,1... | collective-permute-start | bytes 10911752 | tf_op jit(solution)/shard_map/ppermute | solution.py:17
  490.6 51.4 %all-to-all-start.1 = ((bf16[4,296,1536]{2,1,0:T(8,128)(2,1)}), bf16[4,296,1536]{2,1,0:T(8,128)(2,1)}, u32[]{:S(2)}, u32[]{:S(2)}) async-start(bf16[4,296,1536]{2,1,0:T(8,128)(2,1)} %bitcast.67), calls=%async_computation.1 | async-start | bytes 7274496 | tf_op jit(solution)/shard_map/all_to_all | solution.py:305
  521.3 12.2 %collective-permute-start.14 = (bf16[1184,768]{1,0:T(8,128)(2,1)}, bf16[1184,768]{1,0:T(8,128)(2,1)}, u32[]{:S(2)}, u32[]{:S(2)}) collective-permute-start(bf16[1184,768]{1,0:T(8,128)(2,1)} %pair_product.6), channel_id=1, source_target_pairs={{0,4},{4,0},{1,5},{5,1},{2,6},{6,2},{3,7},{7,3},{8,12},{12,8},{9,1... | collective-permute-start | bytes 5455880 | tf_op jit(solution)/shard_map/ppermute | solution.py:17
  529.6 16.9 %collective-permute-start.12 = (bf16[1184,768]{1,0:T(8,128)(2,1)}, bf16[1184,768]{1,0:T(8,128)(2,1)S(1)}, u32[]{:S(2)}, u32[]{:S(2)}) collective-permute-start(bf16[1184,768]{1,0:T(8,128)(2,1)} %pair_product.4), channel_id=1, source_target_pairs={{0,4},{4,0},{1,5},{5,1},{2,6},{6,2},{3,7},{7,3},{8,12},{12,8},{9,1... | collective-permute-start | bytes 5455880 | tf_op jit(solution)/shard_map/ppermute | solution.py:17
  530.2 3.2 collective-permute-start.13
  542.0 27.2 %all-to-all-start.2 = ((bf16[4,296,768]{2,1,0:T(8,128)(2,1)}), bf16[4,296,768]{2,1,0:T(8,128)(2,1)}, u32[]{:S(2)}, u32[]{:S(2)}) async-start(bf16[4,296,768]{2,1,0:T(8,128)(2,1)} %bitcast.68), calls=%async_computation.2 | async-start | bytes 3637248 | tf_op jit(solution)/shard_map/all_to_all | solution.py:305
  569.2 59.0 %all-to-all-start.3 = ((bf16[4,296,768]{2,1,0:T(8,128)(2,1)}), bf16[4,296,768]{2,1,0:T(8,128)(2,1)S(1)}, u32[]{:S(2)}, u32[]{:S(2)}) async-start(bf16[4,296,768]{2,1,0:T(8,128)(2,1)} %bitcast.22), calls=%async_computation.4 | async-start | bytes 3637248 | tf_op jit(solution)/shard_map/all_to_all | solution.py:305
  573.0 88.3 %reduce-scatter.2.cloned.1.call-start = ((), (), s32[]{:S(2)}) async-start(), calls=%async_computation.7 | async-start | bytes 1966080 | tf_op jit(solution)/shard_map/reduce_scatter | solution.py:394
  577.8 34.4 %collective-permute-start.15 = (bf16[128,768]{1,0:T(8,128)(2,1)S(1)}, bf16[128,768]{1,0:T(8,128)(2,1)S(1)}, u32[]{:S(2)}, u32[]{:S(2)}) collective-permute-start(bf16[128,768]{1,0:T(8,128)(2,1)S(1)} %get-tuple-element.100), channel_id=1, source_target_pairs={{0,1},{1,0},{2,3},{3,2},{4,5},{5,4},{6,7},{7,6},{8,9},{9,8},{10,11... | collective-permute-start | bytes 589832 | tf_op jit(solution)/shard_map/ppermute | solution.py:17
  600.4 26.7 %collective-permute-start.16 = (bf16[128,768]{1,0:T(8,128)(2,1)S(1)}, bf16[128,768]{1,0:T(8,128)(2,1)S(1)}, u32[]{:S(2)}, u32[]{:S(2)}) collective-permute-start(bf16[128,768]{1,0:T(8,128)(2,1)S(1)} %get-tuple-element.102), channel_id=1, source_target_pairs={{0,2},{1,3},{2,0},{3,1},{4,6},{5,7},{6,4},{7,5},{8,10},{9,11},{10,... | collective-permute-start | bytes 589832 | tf_op jit(solution)/shard_map/ppermute | solution.py:17
  600.7 26.4 %collective-permute-start.17 = (bf16[128,768]{1,0:T(8,128)(2,1)S(1)}, bf16[128,768]{1,0:T(8,128)(2,1)S(1)}, u32[]{:S(2)}, u32[]{:S(2)}) collective-permute-start(bf16[128,768]{1,0:T(8,128)(2,1)S(1)} %get-tuple-element.101), channel_id=1, source_target_pairs={{0,3},{1,2},{2,1},{3,0},{4,7},{5,6},{6,5},{7,4},{8,11},{9,10},{10,... | collective-permute-start | bytes 589832 | tf_op jit(solution)/shard_map/ppermute | solution.py:17
  628.7 19.7 %collective-permute-start.21 = (f32[128,2]{0,1:T(2,128)S(1)}, f32[128,2]{0,1:T(2,128)S(1)}, u32[]{:S(2)}, u32[]{:S(2)}) collective-permute-start(f32[128,2]{0,1:T(2,128)S(1)} %get-tuple-element.113), channel_id=1, source_target_pairs={{0,1},{1,0},{2,3},{3,2},{4,5},{5,4},{6,7},{7,6},{8,9},{9,8},{10,11... | collective-permute-start | bytes 3080 | tf_op jit(solution)/shard_map/ppermute | solution.py:17
  642.5 8.3 %collective-permute-start.22 = (f32[128,2]{0,1:T(2,128)S(1)}, f32[128,2]{0,1:T(2,128)S(1)}, u32[]{:S(2)}, u32[]{:S(2)}) collective-permute-start(f32[128,2]{0,1:T(2,128)S(1)} %get-tuple-element.115), channel_id=1, source_target_pairs={{0,2},{1,3},{2,0},{3,1},{4,6},{5,7},{6,4},{7,5},{8,10},{9,11},{10,... | collective-permute-start | bytes 3080 | tf_op jit(solution)/shard_map/ppermute | solution.py:17
  642.5 8.3 %collective-permute-start.23 = (f32[128,2]{0,1:T(2,128)S(1)}, f32[128,2]{0,1:T(2,128)S(1)}, u32[]{:S(2)}, u32[]{:S(2)}) collective-permute-start(f32[128,2]{0,1:T(2,128)S(1)} %get-tuple-element.114), channel_id=1, source_target_pairs={{0,3},{1,2},{2,1},{3,0},{4,7},{5,6},{6,5},{7,4},{8,11},{9,10},{10,... | collective-permute-start | bytes 3080 | tf_op jit(solution)/shard_map/ppermute | solution.py:17
  646.3 6.5 collective-permute-start.18
  647.4 12.9 %collective-permute-start.19 = (bf16[128,768]{1,0:T(8,128)(2,1)S(1)}, bf16[128,768]{1,0:T(8,128)(2,1)S(1)}, u32[]{:S(2)}, u32[]{:S(2)}) collective-permute-start(bf16[128,768]{1,0:T(8,128)(2,1)S(1)} %get-tuple-element.105), channel_id=1, source_target_pairs={{0,2},{1,3},{2,0},{3,1},{4,6},{5,7},{6,4},{7,5},{8,10},{9,11},{10,... | collective-permute-start | bytes 589832 | tf_op jit(solution)/shard_map/ppermute | solution.py:17
  648.4 12.0 %collective-permute-start.20 = (bf16[128,768]{1,0:T(8,128)(2,1)S(1)}, bf16[128,768]{1,0:T(8,128)(2,1)S(1)}, u32[]{:S(2)}, u32[]{:S(2)}) collective-permute-start(bf16[128,768]{1,0:T(8,128)(2,1)S(1)} %get-tuple-element.104), channel_id=1, source_target_pairs={{0,3},{1,2},{2,1},{3,0},{4,7},{5,6},{6,5},{7,4},{8,11},{9,10},{10,... | collective-permute-start | bytes 589832 | tf_op jit(solution)/shard_map/ppermute | solution.py:17
  (8 other events, 42.1 us)
Sparse Core Ops, SparseCore 0:
  10.8 120.4 all-gather.2
  190.8 102.9 all-gather.4
  576.7 72.0 reduce-scatter.1
